TPU v7x, 32 devices: a whole 2x2x4 slice. The times are simulated.
32 devices in a mesh: dp: 4 (over y, x), row: 4 (over z), col: 2 (over core).
Axes of the slice: x: 2, y: 2, z: 4, core: 2. Of those that a mesh axis runs over, the one named last changes fastest.
Arguments:
- inputs: bfloat16 [16384, 768], P(('dp', 'row'), 'col'), may hold values from -6 to 6
- out_grad: bfloat16 [16384, 768], P(('dp', 'row'), 'col'), may hold values from -6 to 6
- deal: int32 [16, 1024], P(('dp', 'row')), may hold values from 0 to 1023, each once within a row
- seq_lengths: int32 [8, 4], P(('dp', 'col')), may hold values from 1 to 1024, 2048 in all within a row
- key_trim: int32 [8, 4], P(('dp', 'col')), may hold values from 0 to 255
- query_weight: bfloat16 [768, 768], P('col', 'row'), may hold values from -0.21875 to 0.21875
- query_bias: bfloat16 [768], P('row'), may hold values from -3 to 3
- key_weight: bfloat16 [768, 768], P('col', 'row'), may hold values from -0.21875 to 0.21875
- value_weight: bfloat16 [768, 768], P('col', 'row'), may hold values from -0.21875 to 0.21875
- value_bias: bfloat16 [768], P('row'), may hold values from -3 to 3
- out_weight: bfloat16 [768, 768], P('row', 'col'), may hold values from -3.5 to 3.5
- out_bias: bfloat16 [768], P('col'), may hold values from -3 to 3
- first_gain: bfloat16 [768], P('col'), may hold values from 0.5 to 1.5
- first_shift: bfloat16 [768], P('col'), may hold values from -3 to 3
- up_weight: bfloat16 [768, 3072], P('col', 'row'), may hold values from -0.21875 to 0.21875
- up_bias: bfloat16 [3072], P('row'), may hold values from -3 to 3
- down_weight: bfloat16 [3072, 768], P('row', 'col'), may hold values from -0.109375 to 0.109375
- down_bias: bfloat16 [768], P('col'), may hold values from -3 to 3
- second_gain: bfloat16 [768], P('col'), may hold values from 0.5 to 1.5
- second_shift: bfloat16 [768], P('col'), may hold values from -3 to 3
Outputs:
- output: bfloat16 [16384, 768], P(('dp', 'row'), 'col')
- input_grad: bfloat16 [16384, 768], P(('dp', 'row'), 'col')
- query_weight_grad: float32 [768, 768], P('col', 'row')
- query_bias_grad: float32 [768], P('row')
- key_weight_grad: float32 [768, 768], P('col', 'row')
- value_weight_grad: float32 [768, 768], P('col', 'row')
- value_bias_grad: float32 [768], P('row')
- out_weight_grad: float32 [768, 768], P('row', 'col')
- out_bias_grad: float32 [768], P('col')
- first_gain_grad: float32 [768], P('col')
- first_shift_grad: float32 [768], P('col')
- up_weight_grad: float32 [768, 3072], P('col', 'row')
- up_bias_grad: float32 [3072], P('row')
- down_weight_grad: float32 [3072, 768], P('row', 'col')
- down_bias_grad: float32 [768], P('col')
- second_gain_grad: float32 [768], P('col')
- second_shift_grad: float32 [768], P('col')
Inputs may be any that keep to these rules, and one draw needn't show every extreme that they name: Each row of deal lists every number below 1024 once. `seq_lengths`: each row sums to 2048, and its largest entry is exactly 1024.
All inputs are finite; a program needn't handle non-finite values.
Results may differ from a plain program's by a relative error of at most 0.022.
Values may be sent and summed in bfloat16 or wider, within the bound.
A program may use at most 192 MiB of HBM per device.

v0:
```python
import jax
import jax.numpy as jnp
from jax import lax
from jax.sharding import PartitionSpec as P

HEAD_DIM = 64
SLOT = 2048


norm_eps = 1e-05
far_below = -1e30
inv_root_two = 0.7071067811865476
inv_root_tau = 0.3989422804014327


def contract_rows(left, right):
    return lax.dot_general(
        left, right, (((0,), (0,)), ((), ())), preferred_element_type=jnp.float32
    )


def contract_cols(left, right):
    return lax.dot_general(
        left, right, (((1,), (1,)), ((), ())), preferred_element_type=jnp.float32
    )


def deal_rows(pair):
    return (
        lax.all_to_all(pair[0], "dp", split_axis=0, concat_axis=0, tiled=True),
        lax.all_to_all(pair[1], "dp", split_axis=0, concat_axis=0, tiled=True),
    )


def rows_forward(block_in):
    return lax.all_gather(block_in, "row", axis=0, tiled=True)


def tokens_forward(block_in):
    return lax.all_gather(block_in, "col", axis=0, tiled=True)


def features_total(term):
    return lax.psum_scatter(
        term.astype(jnp.bfloat16), "row", scatter_dimension=0, tiled=True
    ).astype(jnp.float32)


def feature_sums(sum_one, sum_two):
    return lax.psum((sum_one, sum_two), "col")


def rows_backward(block_in):
    return lax.all_gather(block_in, "row", axis=0, tiled=True)


def heads_back_total(term):
    return lax.psum_scatter(term, "col", scatter_dimension=0, tiled=True)


def tokens_backward(block_in):
    return lax.all_gather(block_in, "col", axis=0, tiled=True)


def features_back_total(term):
    return lax.psum_scatter(
        term.astype(jnp.bfloat16), "row", scatter_dimension=0, tiled=True
    ).astype(jnp.float32)


def norm_forward(hidden, gain_vec, shift_vec, model_width):
    sum_one, sum_two = feature_sums(jnp.sum(hidden, axis=1), jnp.sum(hidden * hidden, axis=1))
    row_mean = sum_one / model_width
    row_var = sum_two / model_width - row_mean * row_mean
    inv_std = lax.rsqrt(row_var + norm_eps)
    normed_x = (hidden - row_mean[:, None]) * inv_std[:, None]
    return (normed_x * gain_vec + shift_vec, normed_x, inv_std)


def norm_backward(incoming, normed_x, inv_std, gain_vec, model_width):
    scaled = incoming * gain_vec
    sum_one, sum_two = feature_sums(jnp.sum(scaled, axis=1), jnp.sum(scaled * normed_x, axis=1))
    outgoing = inv_std[:, None] * (
        scaled - sum_one[:, None] / model_width - normed_x * (sum_two[:, None] / model_width)
    )
    return (outgoing, jnp.sum(incoming * normed_x, axis=0), jnp.sum(incoming, axis=0))


def gelu_slope(pre_act):
    return (
        0.5 * (1.0 + lax.erf(pre_act * inv_root_two))
        + pre_act * jnp.exp(-0.5 * pre_act * pre_act) * inv_root_tau
    )


def pack_info(seq_len, trim_len):
    seq_ends = jnp.cumsum(seq_len)
    seq_starts = seq_ends - seq_len
    position = jnp.arange(SLOT, dtype=jnp.int32)
    segment = jnp.sum((position[:, None] >= seq_ends[None, :]).astype(jnp.int32), axis=1)
    onehot = segment[:, None] == jnp.arange(seq_len.shape[0], dtype=jnp.int32)[None, :]
    begin = jnp.sum(jnp.where(onehot, seq_starts[None, :], 0), axis=1)
    valid_len = jnp.maximum(seq_len - trim_len, 1)
    limit = jnp.sum(jnp.where(onehot, valid_len[None, :], 0), axis=1)
    return (segment, position - begin < limit)


def split_heads(block_in, num_packs, head_dim):
    row_count, col_count = block_in.shape
    per_pack = col_count // head_dim
    shaped = block_in.reshape(num_packs, row_count // num_packs, per_pack, head_dim).transpose(
        0, 2, 1, 3
    )
    return shaped.reshape(num_packs * per_pack, row_count // num_packs, head_dim)


def join_heads(block_in, num_packs):
    heads_all, slot_len, head_dim = block_in.shape
    per_pack = heads_all // num_packs
    shaped = block_in.reshape(num_packs, per_pack, slot_len, head_dim).transpose(0, 2, 1, 3)
    return shaped.reshape(num_packs * slot_len, per_pack * head_dim)


def block_scores(q_block, k_head, seg_block, segment, live_keys, score_scale):
    scores = contract_cols(q_block, k_head) * score_scale
    allowed = (seg_block[:, None] == segment[None, :]) & live_keys[None, :]
    return jnp.where(allowed, scores, far_below)


def attention_forward(query, key, value, segments, live_all, head_dim):
    num_packs, slot_len = segments.shape
    per_pack = query.shape[1] // head_dim
    block_rows = min(512, slot_len)
    score_scale = head_dim ** (-0.5)
    offsets = jnp.arange(slot_len // block_rows, dtype=jnp.int32) * block_rows
    seg_heads = jnp.repeat(segments, per_pack, axis=0)
    live_heads = jnp.repeat(live_all, per_pack, axis=0)

    def one_head(operands):
        q_head, k_head, v_head, segment, live_keys = operands

        def one_block(offset):
            q_block = lax.dynamic_slice_in_dim(q_head, offset, block_rows, 0)
            seg_block = lax.dynamic_slice_in_dim(segment, offset, block_rows, 0)
            scores = block_scores(q_block, k_head, seg_block, segment, live_keys, score_scale)
            row_max = jnp.max(scores, axis=1, keepdims=True)
            exp_scores = jnp.exp(scores - row_max)
            row_sum = jnp.sum(exp_scores, axis=1, keepdims=True)
            probs = (exp_scores / row_sum).astype(jnp.bfloat16)
            result = jnp.dot(probs, v_head, preferred_element_type=jnp.float32)
            return (result, (row_max + jnp.log(row_sum))[:, 0])

        results, log_total = lax.map(one_block, offsets)
        return (results.reshape(slot_len, head_dim), log_total.reshape(slot_len))

    operands = (
        split_heads(query, num_packs, head_dim),
        split_heads(key, num_packs, head_dim),
        split_heads(value, num_packs, head_dim),
        seg_heads,
        live_heads,
    )
    head_outs, log_total = lax.map(one_head, operands)
    return (join_heads(head_outs, num_packs), log_total)


def attention_backward(query, key, value, grad_att, log_total, segments, live_all, head_dim):
    num_packs, slot_len = segments.shape
    per_pack = query.shape[1] // head_dim
    block_rows = min(512, slot_len)
    score_scale = head_dim ** (-0.5)
    offsets = jnp.arange(slot_len // block_rows, dtype=jnp.int32) * block_rows
    seg_heads = jnp.repeat(segments, per_pack, axis=0)
    live_heads = jnp.repeat(live_all, per_pack, axis=0)

    def one_head(operands):
        q_head, k_head, v_head, g_head, lse_head, segment, live_keys = operands

        def one_block(accum, offset):
            key_acc, value_acc = accum
            q_block = lax.dynamic_slice_in_dim(q_head, offset, block_rows, 0)
            g_block = lax.dynamic_slice_in_dim(g_head, offset, block_rows, 0)
            lse_block = lax.dynamic_slice_in_dim(lse_head, offset, block_rows, 0)
            seg_block = lax.dynamic_slice_in_dim(segment, offset, block_rows, 0)
            scores = block_scores(q_block, k_head, seg_block, segment, live_keys, score_scale)
            probs = jnp.exp(scores - lse_block[:, None])
            dprob = contract_cols(g_block, v_head)
            delta = jnp.sum(probs * dprob, axis=1, keepdims=True)
            dscore = (probs * (dprob - delta)).astype(jnp.bfloat16)
            q_grad = jnp.dot(dscore, k_head, preferred_element_type=jnp.float32) * score_scale
            key_acc = key_acc + contract_rows(dscore, q_block) * score_scale
            value_acc = value_acc + contract_rows(probs.astype(jnp.bfloat16), g_block)
            return ((key_acc, value_acc), q_grad)

        zero_acc = jnp.zeros((slot_len, head_dim), jnp.float32)
        (k_grad, v_grad), q_grad = lax.scan(one_block, (zero_acc, zero_acc), offsets)
        return (q_grad.reshape(slot_len, head_dim), k_grad, v_grad)

    operands = (
        split_heads(query, num_packs, head_dim),
        split_heads(key, num_packs, head_dim),
        split_heads(value, num_packs, head_dim),
        split_heads(grad_att, num_packs, head_dim),
        log_total,
        seg_heads,
        live_heads,
    )
    q_grads, k_grads, v_grads = lax.map(one_head, operands)
    return (
        join_heads(q_grads, num_packs),
        join_heads(k_grads, num_packs),
        join_heads(v_grads, num_packs),
    )


def on_device(
    inputs,
    out_grad,
    deal,
    seq_lengths,
    key_trim,
    query_weight,
    query_bias,
    key_weight,
    value_weight,
    value_bias,
    out_weight,
    out_bias,
    first_gain,
    first_shift,
    up_weight,
    up_bias,
    down_weight,
    down_bias,
    second_gain,
    second_shift,
):
    model_width = inputs.shape[1] * lax.axis_size("col")
    head_dim = HEAD_DIM
    dealing = deal[0]
    arranged, cotangent = deal_rows((inputs[dealing], out_grad[dealing]))
    segments, live_all = jax.vmap(pack_info)(seq_lengths, key_trim)
    head_cols = query_weight.shape[1]
    merged = jnp.concatenate([query_weight, key_weight, value_weight], axis=1)
    tokens_full = rows_forward(arranged)
    projected = lax.psum_scatter(
        jnp.dot(tokens_full, merged, preferred_element_type=jnp.float32),
        "col",
        scatter_dimension=0,
        tiled=True,
    )
    query = (projected[:, :head_cols] + query_bias).astype(jnp.bfloat16)
    key = projected[:, head_cols : 2 * head_cols].astype(jnp.bfloat16)
    value = (projected[:, 2 * head_cols :] + value_bias).astype(jnp.bfloat16)
    attended, log_total = attention_forward(query, key, value, segments, live_all, head_dim)
    attended = attended.astype(jnp.bfloat16)
    attended_full = tokens_forward(attended)
    branch = (
        features_total(jnp.dot(attended_full, out_weight, preferred_element_type=jnp.float32))
        + out_bias
    )
    first_out, first_normed, first_inv = norm_forward(
        arranged.astype(jnp.float32) + branch, first_gain, first_shift, model_width
    )
    normed = first_out.astype(jnp.bfloat16)
    normed_full = rows_forward(normed)
    pre_act = (
        lax.psum_scatter(
            jnp.dot(normed_full, up_weight, preferred_element_type=jnp.float32).astype(
                jnp.bfloat16
            ),
            "col",
            scatter_dimension=0,
            tiled=True,
        ).astype(jnp.float32)
        + up_bias
    )
    hidden = jax.nn.gelu(pre_act, approximate=False).astype(jnp.bfloat16)
    hidden_full = tokens_forward(hidden)
    ffn_out = (
        features_total(jnp.dot(hidden_full, down_weight, preferred_element_type=jnp.float32))
        + down_bias
    )
    second_out, second_normed, second_inv = norm_forward(
        normed.astype(jnp.float32) + ffn_out, second_gain, second_shift, model_width
    )
    result = second_out.astype(jnp.bfloat16)
    grad_second, second_gain_part, second_shift_part = norm_backward(
        cotangent.astype(jnp.float32), second_normed, second_inv, second_gain, model_width
    )
    grad_ffn = grad_second.astype(jnp.bfloat16)
    down_bias_part = jnp.sum(grad_ffn.astype(jnp.float32), axis=0)
    grad_ffn_full = rows_backward(grad_ffn)
    down_grad = contract_rows(hidden_full, grad_ffn_full)
    grad_hidden = heads_back_total(contract_cols(grad_ffn_full, down_weight))
    grad_pre = (grad_hidden * gelu_slope(pre_act)).astype(jnp.bfloat16)
    grad_pre_full = tokens_backward(grad_pre)
    up_grad = contract_rows(normed_full, grad_pre_full)
    up_bias_grad = jnp.sum(grad_pre_full.astype(jnp.float32), axis=0)
    grad_normed = features_back_total(contract_cols(grad_pre_full, up_weight)) + grad_second
    grad_first, first_gain_part, first_shift_part = norm_backward(
        grad_normed, first_normed, first_inv, first_gain, model_width
    )
    grad_branch = grad_first.astype(jnp.bfloat16)
    out_bias_part = jnp.sum(grad_branch.astype(jnp.float32), axis=0)
    grad_branch_full = rows_backward(grad_branch)
    out_weight_grad = contract_rows(attended_full, grad_branch_full)
    grad_att = heads_back_total(contract_cols(grad_branch_full, out_weight)).astype(jnp.bfloat16)
    grad_query, grad_key, grad_value = attention_backward(
        query, key, value, grad_att, log_total, segments, live_all, head_dim
    )
    grad_proj = jnp.concatenate(
        [
            grad_query.astype(jnp.bfloat16),
            grad_key.astype(jnp.bfloat16),
            grad_value.astype(jnp.bfloat16),
        ],
        axis=1,
    )
    grad_proj_full = tokens_backward(grad_proj)
    merged_grad = contract_rows(tokens_full, grad_proj_full)
    proj_bias_grad = jnp.sum(grad_proj_full.astype(jnp.float32), axis=0)
    grad_tokens = (features_back_total(contract_cols(grad_proj_full, merged)) + grad_first).astype(
        jnp.bfloat16
    )
    query_grad = merged_grad[:, :head_cols]
    key_grad = merged_grad[:, head_cols : 2 * head_cols]
    value_grad = merged_grad[:, 2 * head_cols :]
    query_bias_grad = proj_bias_grad[:head_cols]
    value_bias_grad = proj_bias_grad[2 * head_cols :]
    (
        query_grad,
        key_grad,
        value_grad,
        out_weight_grad,
        query_bias_grad,
        value_bias_grad,
        down_grad,
        up_grad,
        up_bias_grad,
    ) = (
        lax.psum(query_grad.astype(jnp.bfloat16), "dp").astype(jnp.float32),
        lax.psum(key_grad.astype(jnp.bfloat16), "dp").astype(jnp.float32),
        lax.psum(value_grad.astype(jnp.bfloat16), "dp").astype(jnp.float32),
        lax.psum(out_weight_grad.astype(jnp.bfloat16), "dp").astype(jnp.float32),
        lax.psum(query_bias_grad.astype(jnp.bfloat16), "dp").astype(jnp.float32),
        lax.psum(value_bias_grad.astype(jnp.bfloat16), "dp").astype(jnp.float32),
        lax.psum(down_grad.astype(jnp.bfloat16), "dp").astype(jnp.float32),
        lax.psum(up_grad.astype(jnp.bfloat16), "dp").astype(jnp.float32),
        lax.psum(up_bias_grad.astype(jnp.bfloat16), "dp").astype(jnp.float32),
    )
    (
        out_bias_grad,
        first_gain_grad,
        first_shift_grad,
        down_bias_grad,
        second_gain_grad,
        second_shift_grad,
    ) = lax.psum(
        (
            out_bias_part,
            first_gain_part,
            first_shift_part,
            down_bias_part,
            second_gain_part,
            second_shift_part,
        ),
        ("dp", "row"),
    )
    result_back, grad_back = deal_rows((result, grad_tokens))
    output = jnp.zeros_like(result_back).at[dealing].set(result_back)
    input_grad = jnp.zeros_like(grad_back).at[dealing].set(grad_back)
    return (
        output,
        input_grad,
        query_grad,
        query_bias_grad,
        key_grad,
        value_grad,
        value_bias_grad,
        out_weight_grad,
        out_bias_grad,
        first_gain_grad,
        first_shift_grad,
        up_grad,
        up_bias_grad,
        down_grad,
        down_bias_grad,
        second_gain_grad,
        second_shift_grad,
    )


def solution(mesh):
    in_specs = (
        P(("dp", "row"), "col"),
        P(("dp", "row"), "col"),
        P(("dp", "row"), None),
        P(("dp", "col"), None),
        P(("dp", "col"), None),
        P("col", "row"),
        P("row"),
        P("col", "row"),
        P("col", "row"),
        P("row"),
        P("row", "col"),
        P("col"),
        P("col"),
        P("col"),
        P("col", "row"),
        P("row"),
        P("row", "col"),
        P("col"),
        P("col"),
        P("col"),
    )
    out_specs = (
        P(("dp", "row"), "col"),
        P(("dp", "row"), "col"),
        P("col", "row"),
        P("row"),
        P("col", "row"),
        P("col", "row"),
        P("row"),
        P("row", "col"),
        P("col"),
        P("col"),
        P("col"),
        P("col", "row"),
        P("row"),
        P("row", "col"),
        P("col"),
        P("col"),
        P("col"),
    )
    return jax.shard_map(
        on_device, mesh=mesh, in_specs=in_specs, out_specs=out_specs, check_vma=False
    )
```

profile of v0, /device:TPU:30, one launch (start us, length us, event | category | flops | bytes accessed | tf_op | source)
XLA Modules:
  0.0 1093.2 jit_solution(6277087048368522447)
XLA Ops:
  8.6 3.9 gather_fusion
  12.6 13.4 %all_to_all.45 = bf16[4,256,384]{2,1,0:T(8,128)(2,1)} all-to-all(bf16[4,256,384]{2,1,0:T(8,128)(2,1)S(1)} %bitcast.212), channel_id=1, replica_groups=mesh['dp'=4,'row'=4,'col'=2] {'dp'}, dimensions={0} | all-to-all | bytes 1572864 | tf_op jit(solution)/shard_map/all_to_all | solution.py:30
  26.2 61.9 %all-gather.9.cloned.1.call-done = bf16[4096,384]{1,0:T(8,128)(2,1)} async-done(((bf16[1024,384]{1,0:T(8,128)(2,1)}), bf16[4096,384]{1,0:T(8,128)(2,1)}) %all-gather.9.cloned.1.call-update) | async-done | bytes 3145744 | tf_op jit(solution)/shard_map/all_gather | solution.py:36
  88.2 6.9 fusion.62
  96.2 17.6 %reduce-scatter.9.cloned.1.call-done = f32[2048,576]{0,1:T(8,128)} async-done(((f32[4096,576]{0,1:T(8,128)}), f32[2048,576]{0,1:T(8,128)}) %reduce-scatter.9.cloned.1.call-update) | async-done | bytes 4718608 | tf_op jit(solution)/shard_map/reduce_scatter | solution.py:246
  122.4 79.6 %while.58 = (s32[]{:T(128)}, bf16[3,2048,64]{1,2,0:T(8,128)(2,1)}, f32[3,2048]{1,0:T(4,128)S(1)}, bf16[3,2048,64]{2,1,0:T(8,128)(2,1)}, s32[3,2048]{1,0:T(4,128)...) while((s32[]{:T(128)}, bf16[3,2048,64]{1,2,0:T(8,128)(2,1)}, ...), condition=%wide.region_10.11_spmd.clone, body=%wide.region_5.10_spmd.clone.sunk | while | flops 278920704 | bytes 17129936 | solution.py:163
  124.7 22.9 %while.61 = (s32[]{:T(128)}, bf16[4,512,64]{1,2,0:T(8,128)(2,1)S(1)}, f32[4,512]{1,0:T(4,128)S(1)}, s32[4]{0:T(128)S(1)}, s32[2048]{0:T(1024)S(1)}, /*index=5*/p...) while((s32[]{:T(128)}, ...), condition=%wide.region_9.9_spmd, body=%wide.region_6.8_spmd.sunk | while | flops 278920704 | bytes 13930683 | solution.py:153
  151.2 22.9 %while.61 = (s32[]{:T(128)}, bf16[4,512,64]{1,2,0:T(8,128)(2,1)S(1)}, f32[4,512]{1,0:T(4,128)S(1)}, s32[4]{0:T(128)S(1)}, s32[2048]{0:T(1024)S(1)}, /*index=5*/p...) while((s32[]{:T(128)}, ...), condition=%wide.region_9.9_spmd, body=%wide.region_6.8_spmd.sunk | while | flops 278920704 | bytes 13930683 | solution.py:153
  177.7 22.9 %while.61 = (s32[]{:T(128)}, bf16[4,512,64]{1,2,0:T(8,128)(2,1)S(1)}, f32[4,512]{1,0:T(4,128)S(1)}, s32[4]{0:T(128)S(1)}, s32[2048]{0:T(1024)S(1)}, /*index=5*/p...) while((s32[]{:T(128)}, ...), condition=%wide.region_9.9_spmd, body=%wide.region_6.8_spmd.sunk | while | flops 278920704 | bytes 13930683 | solution.py:153
  202.1 11.1 %all-gather.11.cloned.1.call-done = bf16[4096,192]{0,1:T(8,128)(2,1)} async-done(((bf16[2048,192]{0,1:T(8,128)(2,1)}), bf16[4096,192]{0,1:T(8,128)(2,1)}) %all-gather.11.cloned.1.call-update) | async-done | bytes 1572880 | tf_op jit(solution)/shard_map/all_gather | solution.py:40
  213.1 4.4 convolution_convert_fusion.2
  218.2 59.7 %reduce-scatter.11.cloned.1.call-done = bf16[1024,384]{1,0:T(8,128)(2,1)} async-done(((bf16[4096,384]{1,0:T(8,128)(2,1)}), bf16[1024,384]{1,0:T(8,128)(2,1)}) %reduce-scatter.11.cloned.1.call-update) | async-done | bytes 786448 | tf_op jit(solution)/shard_map/reduce_scatter | solution.py:44
  284.7 62.0 %all-gather.13.cloned.1.call-done = bf16[4096,384]{1,0:T(8,128)(2,1)} async-done(((bf16[1024,384]{1,0:T(8,128)(2,1)}), bf16[4096,384]{1,0:T(8,128)(2,1)}) %all-gather.13.cloned.1.call-update) | async-done | bytes 3145744 | tf_op jit(solution)/shard_map/all_gather | solution.py:36
  346.8 8.0 convolution_convert_fusion
  355.4 15.7 %reduce-scatter.13.cloned.1.call-done = bf16[2048,768]{1,0:T(8,128)(2,1)} async-done(((bf16[4096,768]{1,0:T(8,128)(2,1)}), bf16[2048,768]{1,0:T(8,128)(2,1)}) %reduce-scatter.13.cloned.1.call-update) | async-done | bytes 3145744 | tf_op jit(solution)/shard_map/reduce_scatter | solution.py:268
  371.1 16.0 %fusion.25 = bf16[2048,768]{1,0:T(8,128)(2,1)} fusion(bf16[2048,768]{1,0:T(8,128)(2,1)} %reduce-scatter.13.cloned.1.call-done, f32[768]{0:T(1024)S(1)} %convert_element_type.245), kind=kLoop, calls=%fused_computation.58 | loop fusion | flops 105381888 | bytes 6294528 | tf_op jit(solution)/shard_map/convert_element_type | solution.py:278
  387.1 18.0 %all-gather.15.cloned.1.call-done = bf16[4096,768]{1,0:T(8,128)(2,1)} async-done(((bf16[2048,768]{1,0:T(8,128)(2,1)}), bf16[4096,768]{1,0:T(8,128)(2,1)}) %all-gather.15.cloned.1.call-update) | async-done | bytes 6291472 | tf_op jit(solution)/shard_map/all_gather | solution.py:40
  405.2 7.8 convolution_convert_fusion.4
  414.2 5.0 gather_fusion.1
  419.2 4.8 all-to-all-start.2
  424.1 10.1 all-to-all-done.2
  436.3 37.1 %reduce-scatter.15.cloned.1.call-done = bf16[1024,384]{1,0:T(8,128)(2,1)} async-done(((bf16[4096,384]{1,0:T(8,128)(2,1)}), bf16[1024,384]{1,0:T(8,128)(2,1)}) %reduce-scatter.15.cloned.1.call-update) | async-done | bytes 786448 | tf_op jit(solution)/shard_map/reduce_scatter | solution.py:44
  483.1 3.8 convert_reduce_fusion.1
  487.2 62.0 %all-gather.17.cloned.1.call-done = bf16[4096,384]{1,0:T(8,128)(2,1)} async-done(((bf16[1024,384]{1,0:T(8,128)(2,1)}), bf16[4096,384]{1,0:T(8,128)(2,1)}) %all-gather.17.cloned.1.call-update) | async-done | bytes 3145744 | tf_op jit(solution)/shard_map/all_gather | solution.py:54
  549.2 10.0 fusion.63
  559.3 23.3 %reduce-scatter.17.cloned.1.call-done = f32[2048,768]{1,0:T(8,128)} async-done(((f32[4096,768]{1,0:T(8,128)}), f32[2048,768]{1,0:T(8,128)}) %reduce-scatter.17.cloned.1.call-update) | async-done | bytes 6291472 | tf_op jit(solution)/shard_map/reduce_scatter | solution.py:58
  582.6 7.5 fusion.31
  590.2 18.0 %all-gather.19.cloned.1.call-done = bf16[4096,768]{1,0:T(8,128)(2,1)} async-done(((bf16[2048,768]{1,0:T(8,128)(2,1)}), bf16[4096,768]{1,0:T(8,128)(2,1)}) %all-gather.19.cloned.1.call-update) | async-done | bytes 6291472 | tf_op jit(solution)/shard_map/all_gather | solution.py:62
  608.3 8.0 convolution_convert_fusion.3
  616.3 60.3 %reduce-scatter.19.cloned.1.call-done = bf16[1024,384]{1,0:T(8,128)(2,1)} async-done(((bf16[4096,384]{1,0:T(8,128)(2,1)}), bf16[1024,384]{1,0:T(8,128)(2,1)}) %reduce-scatter.19.cloned.1.call-update) | async-done | bytes 786448 | tf_op jit(solution)/shard_map/reduce_scatter | solution.py:66
  686.2 62.2 %all-gather.21.cloned.1.call-done = bf16[4096,384]{1,0:T(8,128)(2,1)} async-done(((bf16[1024,384]{1,0:T(8,128)(2,1)}), bf16[4096,384]{1,0:T(8,128)(2,1)}) %all-gather.21.cloned.1.call-update) | async-done | bytes 3145744 | tf_op jit(solution)/shard_map/all_gather | solution.py:54
  748.4 4.8 fusion.64
  753.7 12.1 %reduce-scatter.21.cloned.1.call-done = f32[2048,192]{0,1:T(8,128)} async-done(((f32[4096,192]{0,1:T(8,128)}), f32[2048,192]{0,1:T(8,128)}) %reduce-scatter.21.cloned.1.call-update) | async-done | bytes 1572880 | tf_op jit(solution)/shard_map/reduce_scatter | solution.py:58
  771.8 111.3 %while.60 = (s32[]{:T(128)}, bf16[3,2048,64]{1,2,0:T(8,128)(2,1)}, bf16[3,2048,64]{1,2,0:T(8,128)(2,1)}, bf16[3,2048,64]{1,2,0:T(8,128)(2,1)}, bf16[3,2048,64]{2...) while((s32[]{:T(128)}, bf16[3,2048,64]{1,2,0:T(8,128)(2,1)}, ...), condition=%wide.region_38.39_spmd.clone, body=%wide.region_34.38_spmd.clone.sunk | while | flops 683310592 | bytes 47905392 | solution.py:208
  776.3 30.5 %while.62 = (s32[]{:T(128)}, f32[2048,64]{0,1:T(8,128)S(1)}, f32[2048,64]{0,1:T(8,128)S(1)}, bf16[4,512,64]{1,2,0:T(8,128)(2,1)S(1)}, s32[4]{0:T(128)S(1)}, /*in...) while((s32[]{:T(128)}, f32[2048,64]{0,1:T(8,128)S(1)}, ...), condition=%wide.region_37.37_spmd.clone, body=%wide.region_35.36_spmd.clone.sunk | while | flops 683310592 | bytes 35809512 | solution.py:196
  813.4 30.5 %while.62 = (s32[]{:T(128)}, f32[2048,64]{0,1:T(8,128)S(1)}, f32[2048,64]{0,1:T(8,128)S(1)}, bf16[4,512,64]{1,2,0:T(8,128)(2,1)S(1)}, s32[4]{0:T(128)S(1)}, /*in...) while((s32[]{:T(128)}, f32[2048,64]{0,1:T(8,128)S(1)}, ...), condition=%wide.region_37.37_spmd.clone, body=%wide.region_35.36_spmd.clone.sunk | while | flops 683310592 | bytes 35809512 | solution.py:196
  850.5 30.5 %while.62 = (s32[]{:T(128)}, f32[2048,64]{0,1:T(8,128)S(1)}, f32[2048,64]{0,1:T(8,128)S(1)}, bf16[4,512,64]{1,2,0:T(8,128)(2,1)S(1)}, s32[4]{0:T(128)S(1)}, /*in...) while((s32[]{:T(128)}, f32[2048,64]{0,1:T(8,128)S(1)}, ...), condition=%wide.region_37.37_spmd.clone, body=%wide.region_35.36_spmd.clone.sunk | while | flops 683310592 | bytes 35809512 | solution.py:196
  886.5 15.7 %all-gather.23.cloned.1.call-done = bf16[4096,576]{0,1:T(8,128)(2,1)} async-done(((bf16[2048,576]{0,1:T(8,128)(2,1)}), bf16[4096,576]{0,1:T(8,128)(2,1)}) %all-gather.23.cloned.1.call-update) | async-done | bytes 4718608 | tf_op jit(solution)/shard_map/all_gather | solution.py:62
  902.2 7.2 convolution_convert_fusion.1
  909.7 8.1 convolution_convert_fusion.5
  917.8 6.4 convolution_convert_fusion.6
  929.5 4.2 all-to-all-start.1
  933.8 36.1 %reduce-scatter.23.cloned.1.call-done = bf16[1024,384]{1,0:T(8,128)(2,1)} async-done(((bf16[4096,384]{1,0:T(8,128)(2,1)}), bf16[1024,384]{1,0:T(8,128)(2,1)}) %reduce-scatter.23.cloned.1.call-update) | async-done | bytes 786448 | tf_op jit(solution)/shard_map/reduce_scatter | solution.py:66
  972.0 4.2 all-to-all-start.3
  976.2 6.0 scatter_custom_fusion
  986.1 72.2 %all-reduce = (f32[384]{0:T(512)}, f32[384]{0:T(512)}, f32[384]{0:T(512)}, f32[384]{0:T(512)}, f32[384]{0:T(512)}, /*index=5*/f32[384]{0:T(512)}) all-reduce(f32[384]{0:T(512)S(1)} %copy-done.24, f32[384]{0:T(512)S(1)} %copy-done.27, f32[384]{0:T(512)S(1)} %copy-done.28, ...), channel_id=1, replica_groups=mesh['dp'=4,'row'=4,'col'=2] {'dp','row'}, use_global_device_ids=true, to_apply=%region_49.50 | all-reduce | flops 2304 | bytes 18432 | tf_op jit(solution)/shard_map/psum | solution.py:359
  1061.4 7.4 all-reduce.5
  1080.5 6.0 scatter_custom_fusion.1
  (476 shorter events, 221.4 us)
Async XLA Ops:
  7.2 80.9 %all-gather.9.cloned.1.call-start = ((), (), s32[]{:S(2)}) async-start(), calls=%async_computation.12 | async-start | bytes 3932160 | tf_op jit(solution)/shard_map/all_gather | solution.py:36
  8.6 4.0 copy-start.21
  8.6 17.5 %copy-start.18 = (bf16[384,192]{0,1:T(8,128)(2,1)S(1)}, bf16[384,192]{0,1:T(8,128)(2,1)}, u32[]{:S(2)}) copy-start(bf16[384,192]{0,1:T(8,128)(2,1)} %param.33) | copy-start | bytes 442372
  8.6 17.5 %copy-start.19 = (bf16[384,192]{0,1:T(8,128)(2,1)S(1)}, bf16[384,192]{0,1:T(8,128)(2,1)}, u32[]{:S(2)}) copy-start(bf16[384,192]{0,1:T(8,128)(2,1)} %param.35) | copy-start | bytes 442372
  8.6 17.5 %copy-start.20 = (bf16[384,192]{0,1:T(8,128)(2,1)S(1)}, bf16[384,192]{0,1:T(8,128)(2,1)}, u32[]{:S(2)}) copy-start(bf16[384,192]{0,1:T(8,128)(2,1)} %param.36) | copy-start | bytes 442372
  26.0 87.8 %reduce-scatter.9.cloned.1.call-start = ((), (), s32[]{:S(2)}) async-start(), calls=%async_computation.13 | async-start | bytes 14155776 | tf_op jit(solution)/shard_map/reduce_scatter | solution.py:246
  26.2 68.9 %copy-start.13 = (bf16[384,576]{0,1:T(8,128)(2,1)}, bf16[384,576]{0,1:T(8,128)(2,1)S(1)}, u32[]{:S(2)}) copy-start(bf16[384,576]{0,1:T(8,128)(2,1)S(1)} %constant_dynamic-update-slice_fusion.2) | copy-start | bytes 1327108
  95.1 118.0 %all-gather.11.cloned.1.call-start = ((), (), s32[]{:S(2)}) async-start(), calls=%async_computation.14 | async-start | bytes 2359296 | tf_op jit(solution)/shard_map/all_gather | solution.py:40
  202.0 75.9 %reduce-scatter.11.cloned.1.call-start = ((), (), s32[]{:S(2)}) async-start(), calls=%async_computation.15 | async-start | bytes 3932160 | tf_op jit(solution)/shard_map/reduce_scatter | solution.py:44
  217.5 60.4 %copy-start.5 = (bf16[4,256,384]{2,1,0:T(8,128)(2,1)S(1)}, bf16[4,256,384]{2,1,0:T(8,128)(2,1)}, u32[]{:S(2)}) copy-start(bf16[4,256,384]{2,1,0:T(8,128)(2,1)} %all_to_all.45) | copy-start | bytes 2359300
  217.5 129.2 %copy-start.39 = (bf16[384,768]{1,0:T(8,128)(2,1)S(1)}, bf16[384,768]{1,0:T(8,128)(2,1)}, u32[]{:S(2)}) copy-start(bf16[384,768]{1,0:T(8,128)(2,1)} %param.42) | copy-start | bytes 1769476
  217.5 129.2 %all-gather.13.cloned.1.call-start = ((), (), s32[]{:S(2)}) async-start(), calls=%async_computation.16 | async-start | bytes 3932160 | tf_op jit(solution)/shard_map/all_gather | solution.py:36
  284.5 86.6 %reduce-scatter.13.cloned.1.call-start = ((), (), s32[]{:S(2)}) async-start(), calls=%async_computation.17 | async-start | bytes 9437184 | tf_op jit(solution)/shard_map/reduce_scatter | solution.py:268
  354.8 50.4 %all-gather.15.cloned.1.call-start = ((), (), s32[]{:S(2)}) async-start(), calls=%async_computation.18 | async-start | bytes 9437184 | tf_op jit(solution)/shard_map/all_gather | solution.py:40
  387.1 18.1 %copy-start.15 = (bf16[768,384]{1,0:T(8,128)(2,1)S(1)}, bf16[768,384]{1,0:T(8,128)(2,1)}, u32[]{:S(2)}) copy-start(bf16[768,384]{1,0:T(8,128)(2,1)} %param.44) | copy-start | bytes 1769476
  387.1 86.3 %reduce-scatter.15.cloned.1.call-start = ((), (), s32[]{:S(2)}) async-start(), calls=%async_computation.19 | async-start | bytes 3932160 | tf_op jit(solution)/shard_map/reduce_scatter | solution.py:44
  414.2 9.8 copy-start.34
  414.2 9.8 copy-start.35
  414.2 9.9 copy-start.36
  419.2 58.6 %copy-start.6 = (bf16[1024,384]{1,0:T(8,128)(2,1)S(1)}, bf16[1024,384]{1,0:T(8,128)(2,1)}, u32[]{:S(2)}) copy-start(bf16[1024,384]{1,0:T(8,128)(2,1)} %add_convert_fusion.2) | copy-start | bytes 2359300
  419.2 15.0 %all-to-all-start.2 = ((bf16[4,256,384]{2,1,0:T(8,128)(2,1)}), bf16[4,256,384]{2,1,0:T(8,128)(2,1)}, u32[]{:S(2)}, u32[]{:S(2)}) async-start(bf16[4,256,384]{2,1,0:T(8,128)(2,1)} %bitcast.211), calls=%async_computation.6 | async-start | bytes 1572864 | tf_op jit(solution)/shard_map/all_to_all | solution.py:31
  424.0 125.2 %all-gather.17.cloned.1.call-start = ((), (), s32[]{:S(2)}) async-start(), calls=%async_computation.20 | async-start | bytes 3932160 | tf_op jit(solution)/shard_map/all_gather | solution.py:54
  487.0 95.6 %reduce-scatter.17.cloned.1.call-start = ((), (), s32[]{:S(2)}) async-start(), calls=%async_computation.21 | async-start | bytes 18874368 | tf_op jit(solution)/shard_map/reduce_scatter | solution.py:58
  559.2 49.0 %all-gather.19.cloned.1.call-start = ((), (), s32[]{:S(2)}) async-start(), calls=%async_computation.22 | async-start | bytes 9437184 | tf_op jit(solution)/shard_map/all_gather | solution.py:62
  590.2 18.1 %copy-start.40 = (bf16[384,768]{1,0:T(8,128)(2,1)S(1)}, bf16[384,768]{1,0:T(8,128)(2,1)}, u32[]{:S(2)}) copy-start(bf16[384,768]{1,0:T(8,128)(2,1)} %param.42) | copy-start | bytes 1769476
  590.2 86.4 %reduce-scatter.19.cloned.1.call-start = ((), (), s32[]{:S(2)}) async-start(), calls=%async_computation.23 | async-start | bytes 3932160 | tf_op jit(solution)/shard_map/reduce_scatter | solution.py:66
  616.2 60.4 %copy-start.8 = (bf16[1024,384]{1,0:T(8,128)(2,1)S(1)}, bf16[1024,384]{1,0:T(8,128)(2,1)}, u32[]{:S(2)}) copy-start(bf16[1024,384]{1,0:T(8,128)(2,1)} %reduce-scatter.11.cloned.1.call-done) | copy-start | bytes 2359300
  616.3 132.1 %all-gather.21.cloned.1.call-start = ((), (), s32[]{:S(2)}) async-start(), calls=%async_computation.24 | async-start | bytes 3932160 | tf_op jit(solution)/shard_map/all_gather | solution.py:54
  682.3 66.1 %copy-start.17 = (bf16[192,384]{1,0:T(8,128)(2,1)S(1)}, bf16[192,384]{1,0:T(8,128)(2,1)}, u32[]{:S(2)}) copy-start(bf16[192,384]{1,0:T(8,128)(2,1)} %param.38) | copy-start | bytes 442372
  686.2 79.6 %reduce-scatter.21.cloned.1.call-start = ((), (), s32[]{:S(2)}) async-start(), calls=%async_computation.25 | async-start | bytes 4718592 | tf_op jit(solution)/shard_map/reduce_scatter | solution.py:58
  753.2 149.0 %all-gather.23.cloned.1.call-start = ((), (), s32[]{:S(2)}) async-start(), calls=%async_computation.26 | async-start | bytes 7077888 | tf_op jit(solution)/shard_map/all_gather | solution.py:62
  883.1 19.2 %copy-start.14 = (bf16[384,576]{0,1:T(8,128)(2,1)S(1)}, bf16[384,576]{0,1:T(8,128)(2,1)}, u32[]{:S(2)}) copy-start(bf16[384,576]{0,1:T(8,128)(2,1)} %copy-done.13) | copy-start | bytes 1327108
  886.5 83.4 %reduce-scatter.23.cloned.1.call-start = ((), (), s32[]{:S(2)}) async-start(), calls=%async_computation.27 | async-start | bytes 3932160 | tf_op jit(solution)/shard_map/reduce_scatter | solution.py:66
  909.5 161.1 %all-reduce.9.cloned.1.call-start = ((), (), s32[]{:S(2)}) async-start(), calls=%async_computation.28 | async-start | bytes 3538944 | tf_op jit(solution)/shard_map/psum | solution.py:342
  909.7 8.1 copy-start.10
  909.7 16.3 %slice-start = ((s8[4718592]{0:T(1024)(128)(4,1)}), s8[4194304]{0:T(1024)(128)(4,1)S(1)}, s32[]{:S(2)}) async-start(s8[4718592]{0:T(1024)(128)(4,1)} %bitcast.209), calls=%async_computation.29 | async-start | bytes 8388608
  917.8 6.4 copy-start.7
  917.8 6.4 copy-start.9
  917.8 8.1 slice-start.1
  928.7 41.1 %copy-start.11 = (f32[1024,384]{1,0:T(8,128)S(1)}, f32[1024,384]{1,0:T(8,128)}, u32[]{:S(2)}) copy-start(f32[1024,384]{1,0:T(8,128)} %get-tuple-element.499) | copy-start | bytes 4718596
  929.5 42.4 %all-to-all-start.1 = ((bf16[4,256,384]{2,1,0:T(8,128)(2,1)}), bf16[4,256,384]{2,1,0:T(8,128)(2,1)S(1)}, u32[]{:S(2)}, u32[]{:S(2)}) async-start(bf16[4,256,384]{2,1,0:T(8,128)(2,1)} %bitcast.22), calls=%async_computation.5 | async-start | bytes 1572864 | tf_op jit(solution)/shard_map/all_to_all | solution.py:30
  972.0 108.5 %all-to-all-start.3 = ((bf16[4,256,384]{2,1,0:T(8,128)(2,1)}), bf16[4,256,384]{2,1,0:T(8,128)(2,1)S(1)}, u32[]{:S(2)}, u32[]{:S(2)}) async-start(bf16[4,256,384]{2,1,0:T(8,128)(2,1)} %bitcast.41), calls=%async_computation.11 | async-start | bytes 1572864 | tf_op jit(solution)/shard_map/all_to_all | solution.py:31
  982.2 3.8 copy-start.26
  982.2 3.8 copy-start.27
  982.2 3.8 copy-start.28
  982.2 3.8 copy-start.29
  1058.3 28.2 %copy-start.1 = (bf16[1024,384]{1,0:T(8,128)(2,1)S(1)}, bf16[1024,384]{1,0:T(8,128)(2,1)}, u32[]{:S(2)}) copy-start(bf16[1024,384]{1,0:T(8,128)(2,1)} %param.28) | copy-start | bytes 2359300
  1070.6 8.8 copy-start.16
  (21 other events, 29.5 us)
Sparse Core Ops, SparseCore 0:
  26.1 61.9 all-gather.8
  95.3 18.4 reduce-scatter.8
  202.1 10.9 all-gather.10
  217.7 60.1 reduce-scatter.10
  284.6 62.0 all-gather.12
  354.9 16.1 reduce-scatter.12
  387.2 17.9 all-gather.14
  413.2 60.1 reduce-scatter.14
  487.1 62.0 all-gather.16
  559.4 23.2 reduce-scatter.16
  590.3 17.9 all-gather.18
  616.4 60.1 reduce-scatter.18
  686.3 62.0 all-gather.20
  753.4 12.3 reduce-scatter.20
  886.6 15.6 all-gather.22
  909.6 60.1 reduce-scatter.22
  974.6 68.3 all-reduce.8
where the time goes:
time: 1110 us; the launch traced here: 1090 us
  waiting for transfers between devices  583 us (53%)
  matrix products  157 us (14%)
  blocking collectives  103 us (9%)
  other arithmetic  88.1 us (8%)
  local copies, waits for them, and re-layouts  84.2 us (8%)
  loops' own time  48.1 us (4%)
  starting transfers between devices  14.8 us (1%)
  between operations  14.7 us (1%)
    all_gather x2, waiting for transfers between devices, rows_backward(): return lax.all_gather(block_in, 'row', axis=0, tiled=True)  124 us
    all_gather x2, waiting for transfers between devices, rows_forward(): return lax.all_gather(block_in, 'row', axis=0, tiled=True)  124 us
    reduce_scatter x2, waiting for transfers between devices, features_total(): lax.psum_scatter(term.astype(jnp.bfloat16), 'row', scatter_dimension=0, t...  96.7 us
    reduce_scatter x2, waiting for transfers between devices, features_back_total(): lax.psum_scatter(term.astype(jnp.bfloat16), 'row', scatter_dimension=0, t...  96.4 us
    dot_general x40, matrix products, contract_cols(): lax.dot_general(left, right, (((1,), (1,)), ((), ())), preferred_element_...  75.3 us
    psum x1, blocking collectives, on_device(): lax.psum((out_bias_part, first_gain_part, first_shift_part, down_bias_par...  72.2 us
    reduce_scatter x2, waiting for transfers between devices, heads_back_total(): return lax.psum_scatter(term, 'col', scatter_dimension=0, tiled=True)  35.4 us
    all_gather x2, waiting for transfers between devices, tokens_backward(): return lax.all_gather(block_in, 'col', axis=0, tiled=True)  33.8 us
  transfers between devices with their start and end apart: 20, of which 17 were waited for; matrix products, arithmetic and copies ran while one was open for 5% of the time, Pallas kernels for 0%

commit v1 on v0

v1 whole, which is shorter than its diff:
```python
import functools
import math

import jax
import jax.numpy as jnp
from jax import lax
from jax.experimental import pallas as pl
from jax.experimental.pallas import tpu as pltpu
from jax.sharding import PartitionSpec as P

MESH = pl.DeviceIdType.MESH
f32 = jnp.float32
bf16 = jnp.bfloat16

HEAD = 64
EPS = 1e-05
FAR = -1e30
INV_ROOT_TWO = 0.7071067811865476
INV_ROOT_TAU = 0.3989422804014327
VMEM_LIMIT = 62 * 1024 * 1024

VM = pl.BlockSpec(memory_space=pltpu.VMEM)
SM = pl.BlockSpec(memory_space=pltpu.SMEM)
ANY = pl.BlockSpec(memory_space=pl.ANY)
DMA = pltpu.SemaphoreType.DMA


def nn(a, b):
    return lax.dot_general(a, b, (((1,), (0,)), ((), ())), preferred_element_type=f32)


def nt(a, b):
    return lax.dot_general(a, b, (((1,), (1,)), ((), ())), preferred_element_type=f32)


def tn(a, b):
    return lax.dot_general(a, b, (((0,), (0,)), ((), ())), preferred_element_type=f32)


def sds(shape, dtype):
    return jax.ShapeDtypeStruct(shape, dtype)


def me():
    return lax.axis_index("dp"), lax.axis_index("row"), lax.axis_index("col")


def flip(v):
    return v + 1 - 2 * lax.rem(v, 2)


def remote(src, dst, ssem, rsem, dev):
    return pltpu.make_async_remote_copy(
        src_ref=src, dst_ref=dst, send_sem=ssem, recv_sem=rsem, device_id=dev, device_id_type=MESH
    )


def greet(devs):
    barrier = pltpu.get_barrier_semaphore()
    for dev in devs:
        pl.semaphore_signal(barrier, inc=1, device_id=dev, device_id_type=MESH)
    pl.semaphore_wait(barrier, len(devs))


def deal_kernel(
    n_dp, x_ref, dy_ref, deal_ref, w_ref, seq_ref,
    xf_ref, dya_ref, dyb_ref, qkv_ref, qkvt_ref, wq_ref, seqo_ref,
    xs, dys, dyin, seqrx, sx, rx, sc, rc, sz, rz, sc2, rc2, sd, rd, sw, rw, sm, rm,
):
    d, r, c = me()
    half = lax.rem(r, 2)
    tokens = x_ref.shape[0]
    piece = tokens // n_dp
    core = (d, r, 1 - c)
    zdev = (d, flip(r), c)
    far_row = lax.rem(r + 2, 4)
    ring = [(lax.rem(d + k, n_dp), r, c) for k in range(1, n_dp)]
    greet(ring + [core, zdev, (d, far_row, 0), (d, far_row, 1)])

    w_far = remote(w_ref, wq_ref.at[c], sw.at[0], rw.at[c], (d, far_row, 1))
    w_far.start()
    w_near = remote(w_ref, wq_ref.at[1], sw.at[1], rw.at[1], (d, r, 0))

    @pl.when(c == 0)
    def _():
        wq_ref[0] = w_ref[...]

    @pl.when(c == 1)
    def _():
        w_near.start()

    seq_cp = remote(seq_ref, seqrx, sm.at[0], rm.at[0], core)
    seq_cp.start()

    def rows(s):
        return pl.ds(pl.multiple_of(s * piece, piece), piece)

    lane = lax.broadcasted_iota(jnp.int32, (piece, tokens), 1)
    sends = []
    dsends = []
    for k in list(range(1, n_dp)) + [0]:
        dest = lax.rem(d + k, n_dp)
        pick = (deal_ref[rows(dest), :] == lane).astype(bf16)
        px = nn(pick, x_ref[...]).astype(bf16)
        pd = nn(pick, dy_ref[...]).astype(bf16)
        if k:
            xs[k] = px
            cp = remote(xs.at[k], xf_ref.at[half, c, rows(d), :], sx.at[k], rx.at[k], (dest, r, c))
            cp.start()
            sends.append(cp)
            dys[k] = pd
            dsends.append(remote(dys.at[k], dyin.at[rows(d), :], sd.at[k], rd.at[k], (dest, r, c)))
        else:
            xf_ref[half, c, rows(d), :] = px
            dyin[rows(d), :] = pd

    core_cp, z_cp, core2_cp = [], [], []
    for k in range(n_dp):
        s = lax.rem(d - k + n_dp, n_dp)
        ref = xf_ref.at[half, c, rows(s), :]
        if k:
            sends[k - 1].wait_recv()
        a = remote(ref, ref, sz.at[k], rz.at[k], zdev)
        a.start()
        b = remote(ref, ref, sc.at[k], rc.at[k], core)
        b.start()
        z_cp.append(a)
        core_cp.append(b)
        if k == 0:
            for cp in dsends:
                cp.start()
    for k in range(n_dp):
        s = lax.rem(d - k + n_dp, n_dp)
        z_cp[k].wait_recv()
        ref = xf_ref.at[1 - half, c, rows(s), :]
        b = remote(ref, ref, sc2.at[k], rc2.at[k], core)
        b.start()
        core2_cp.append(b)
    for cp in dsends:
        cp.wait_recv()
    own = tokens // 2
    theirs = pl.ds(pl.multiple_of((1 - c) * own, own), own)
    mine = pl.ds(pl.multiple_of(c * own, own), own)
    dy_cp = remote(dyin.at[theirs, :], dyb_ref, sm.at[1], rm.at[1], core)
    dy_cp.start()
    dya_ref[...] = dyin[mine, :]
    seq_cp.wait()
    is_mine = lax.div(r, 2) == c
    seqo_ref[...] = jnp.where(is_mine, seq_ref[...], seqrx[...])

    @pl.when(c == 0)
    def _():
        w_near.wait_recv()

    @pl.when(c == 1)
    def _():
        w_near.wait_send()
        remote(w_ref, wq_ref.at[0], sw.at[0], rw.at[0], (d, far_row, 1)).wait_recv()
        remote(w_ref, wq_ref.at[1], sw.at[0], rw.at[1], (d, far_row, 1)).wait_recv()

    w_far.wait_send()
    for k in range(n_dp):
        core_cp[k].wait_recv()
        core2_cp[k].wait_recv()
    width = w_ref.shape[0] - 16
    bias = wq_ref[0, width : width + 1, :].astype(f32)

    def project(i, carry):
        h = lax.div(i, 2)
        base = pl.ds(pl.multiple_of(lax.rem(i, 2) * 512, 512), 512)
        y = nn(xf_ref[h, 0, base, :], wq_ref[0, :width, :])
        y = y + nn(xf_ref[h, 1, base, :], wq_ref[1, :width, :]) + bias
        y = y.astype(bf16)
        out = pl.ds(pl.multiple_of(i * 512, 512), 512)
        qkv_ref[out, :] = y
        qkvt_ref[:, out] = y.T
        return carry

    lax.fori_loop(0, 4, project, 0)
    for cp in sends + dsends + core_cp + z_cp + core2_cp:
        cp.wait_send()
    dy_cp.wait()


def deal_call(n_dp, x, dy, deal_col, w, seq):
    tokens, wide = x.shape
    piece = tokens // n_dp
    cols = w.shape[1]
    return pl.pallas_call(
        functools.partial(deal_kernel, n_dp),
        out_shape=(
            sds((2, 2, tokens, wide), bf16),
            sds((tokens // 2, wide), bf16),
            sds((tokens // 2, wide), bf16),
            sds((2 * tokens, cols), bf16),
            sds((cols, 2 * tokens), bf16),
            sds((2,) + w.shape, bf16),
            sds(seq.shape, jnp.int32),
        ),
        in_specs=[VM] * 5,
        out_specs=(VM,) * 7,
        scratch_shapes=[
            pltpu.VMEM((n_dp, piece, wide), bf16),
            pltpu.VMEM((n_dp, piece, wide), bf16),
            pltpu.VMEM((tokens, wide), bf16),
            pltpu.VMEM(seq.shape, jnp.int32),
        ]
        + [DMA((n_dp,))] * 10
        + [DMA((2,))] * 4,
        compiler_params=pltpu.CompilerParams(
            collective_id=1, has_side_effects=True, vmem_limit_bytes=VMEM_LIMIT
        ),
        name="deal",
    )(x, dy, deal_col, w, seq)


def seq_bounds(seq_ref, n_seq):
    ends, total = [], 0
    for j in range(n_seq):
        total = total + seq_ref[0, j]
        ends.append(total)
    starts = [ends[j] - seq_ref[0, j] for j in range(n_seq)]
    lives = [starts[j] + jnp.maximum(seq_ref[0, j] - seq_ref[1, j], 1) for j in range(n_seq)]
    return starts, ends, lives


def block_range(first, last, starts, ends, block):
    lo, hi = 0, ends[-1]
    for j in range(len(ends)):
        lo = jnp.where((first >= starts[j]) & (first < ends[j]), starts[j], lo)
        hi = jnp.where((last >= starts[j]) & (last < ends[j]), ends[j], hi)
    return lax.div(lo, block), lax.div(hi + block - 1, block)


def key_columns(starts, ends, lives, length, extra):
    pos = lax.broadcasted_iota(jnp.int32, (length, HEAD), 0)
    lane = lax.broadcasted_iota(jnp.int32, (length, HEAD), 1)
    n_seq = len(ends)
    cols = jnp.where(lane < n_seq, FAR, 0.0)
    cols = jnp.where((lane >= n_seq) & (lane < n_seq + extra), -1.0, cols)
    for j in range(n_seq):
        live = (pos >= starts[j]) & (pos < lives[j]) & (lane == j)
        cols = jnp.where(live, 0.0, cols)
    return cols.astype(bf16)


def query_rows(starts, ends, length):
    pos = lax.broadcasted_iota(jnp.int32, (16, length), 1)
    row = lax.broadcasted_iota(jnp.int32, (16, length), 0)
    out = jnp.zeros((16, length), f32)
    for j in range(len(ends)):
        out = jnp.where((row == j) & (pos >= starts[j]) & (pos < ends[j]), 1.0, out)
    return out


def split_three(v):
    hi = v.astype(bf16).astype(f32)
    mid = (v - hi).astype(bf16).astype(f32)
    low = (v - hi - mid).astype(bf16).astype(f32)
    return hi, mid, low


def put_rows(base, values, first):
    row = lax.broadcasted_iota(jnp.int32, base.shape, 0)
    for i, v in enumerate(values):
        base = jnp.where(row == first + i, v, base)
    return base


def attend_kernel(n_seq, block, seq_ref, qkv_ref, qkvt_ref, ot_ref, lse_ref, kaug, qaug, vaug, acc, mx):
    length = qkv_ref.shape[0]
    heads = qkv_ref.shape[1] // (3 * HEAD)
    width = heads * HEAD
    starts, ends, lives = seq_bounds(seq_ref, n_seq)
    kcols = key_columns(starts, ends, lives, length, 0)
    qrows = query_rows(starts, ends, length).astype(bf16)
    ones = (lax.broadcasted_iota(jnp.int32, (16, length), 0) == 0).astype(f32).astype(bf16)
    for h in range(heads):
        kaug[h, :, :HEAD] = qkv_ref[:, width + h * HEAD : width + (h + 1) * HEAD]
        kaug[h, :, HEAD:] = kcols
        qaug[h, :HEAD, :] = qkvt_ref[h * HEAD : (h + 1) * HEAD, :] * 0.125
        qaug[h, HEAD : HEAD + 16, :] = qrows
        qaug[h, HEAD + 16 :, :] = jnp.zeros((HEAD - 16, length), bf16)
        vaug[h, :HEAD, :] = qkvt_ref[2 * width + h * HEAD : 2 * width + (h + 1) * HEAD, :]
        vaug[h, HEAD:, :] = ones
    lse_ref[...] = jnp.zeros_like(lse_ref)

    def q_step(qb, carry):
        qs = pl.ds(pl.multiple_of(qb * block, block), block)
        lo, hi = block_range(qb * block, qb * block + block - 1, starts, ends, block)
        for h in range(heads):
            acc[h] = jnp.zeros((HEAD + 16, block), f32)
            mx[h] = jnp.full((8, block), 2 * FAR, f32)

        def k_step(kb, inner):
            ks = pl.ds(pl.multiple_of(kb * block, block), block)
            for h in range(heads):
                s = nn(kaug[h, ks, :], qaug[h, :, qs])
                old = mx[h, 0:1, :]
                new = jnp.maximum(old, jnp.max(s, axis=0, keepdims=True))
                p = jnp.exp(s - new).astype(bf16)
                acc[h] = acc[h] * jnp.exp(old - new) + nn(vaug[h, :, ks], p)
                mx[h] = jnp.broadcast_to(new, (8, block))
            return inner

        lax.fori_loop(lo, hi, k_step, 0)
        for h in range(heads):
            total = acc[h, HEAD : HEAD + 1, :]
            ot_ref[h * HEAD : (h + 1) * HEAD, qs] = (acc[h, :HEAD, :] / total).astype(bf16)
            lse_ref[h : h + 1, qs] = mx[h, 0:1, :] + jnp.log(total)
        return carry

    lax.fori_loop(0, length // block, q_step, 0)


def attend_call(n_seq, seq, qkv, qkvt):
    length, cols = qkv.shape
    heads = cols // (3 * HEAD)
    block = 256
    return pl.pallas_call(
        functools.partial(attend_kernel, n_seq, block),
        out_shape=(sds((heads * HEAD, length), bf16), sds((8, length), f32)),
        in_specs=[SM, VM, VM],
        out_specs=(VM, VM),
        scratch_shapes=[
            pltpu.VMEM((heads, length, 2 * HEAD), bf16),
            pltpu.VMEM((heads, 2 * HEAD, length), bf16),
            pltpu.VMEM((heads, HEAD + 16, length), bf16),
            pltpu.VMEM((heads, HEAD + 16, block), f32),
            pltpu.VMEM((heads, 8, block), f32),
        ],
        compiler_params=pltpu.CompilerParams(vmem_limit_bytes=VMEM_LIMIT),
        cost_estimate=pl.CostEstimate(flops=4 * 10**9, bytes_accessed=6 * 10**6, transcendentals=10**7),
        name="attend",
    )(seq, qkv, qkvt)


def attend_back_kernel(
    n_seq, block, seq_ref, qkv_ref, qkvt_ref, dot_ref, ot_ref, lse_ref, dqkv_ref, dqkvt_ref,
    kaug, qaug, vaug, doaug, qn, don, dqt, dk, dv,
):
    length = qkv_ref.shape[0]
    heads = qkv_ref.shape[1] // (3 * HEAD)
    width = heads * HEAD
    starts, ends, lives = seq_bounds(seq_ref, n_seq)
    kcols = key_columns(starts, ends, lives, length, 3)
    lane = lax.broadcasted_iota(jnp.int32, (length, HEAD), 1)
    vcols = jnp.where(lane < 3, -1.0, 0.0).astype(bf16)
    qrows = query_rows(starts, ends, length)
    zero = jnp.zeros((HEAD - 16, length), bf16)
    for h in range(heads):
        hs = slice(h * HEAD, (h + 1) * HEAD)
        kaug[h, :, :HEAD] = qkv_ref[:, width + h * HEAD : width + (h + 1) * HEAD]
        kaug[h, :, HEAD:] = kcols
        vaug[h, :, :HEAD] = qkv_ref[:, 2 * width + h * HEAD : 2 * width + (h + 1) * HEAD]
        vaug[h, :, HEAD:] = vcols
        qaug[h, :HEAD, :] = qkvt_ref[hs, :] * 0.125
        qaug[h, HEAD : HEAD + 16, :] = put_rows(qrows, split_three(lse_ref[h : h + 1, :]), n_seq).astype(bf16)
        qaug[h, HEAD + 16 :, :] = zero
        do = dot_ref[hs, :]
        delta = jnp.sum(do.astype(f32) * ot_ref[hs, :].astype(f32), axis=0, keepdims=True)
        doaug[h, :HEAD, :] = do
        doaug[h, HEAD : HEAD + 16, :] = put_rows(
            jnp.zeros((16, length), f32), split_three(delta), 0
        ).astype(bf16)
        doaug[h, HEAD + 16 :, :] = zero
        qn[h] = qkv_ref[:, hs] * 0.125
        don[h] = do.T
        dqt[h] = jnp.zeros((HEAD, length), f32)

    def k_step(kb, carry):
        ks = pl.ds(pl.multiple_of(kb * block, block), block)
        lo, hi = block_range(kb * block, kb * block + block - 1, starts, ends, block)
        dk[...] = jnp.zeros_like(dk)
        dv[...] = jnp.zeros_like(dv)

        def q_step(qb, inner):
            qs = pl.ds(pl.multiple_of(qb * block, block), block)
            for h in range(heads):
                p = jnp.exp(nn(kaug[h, ks, :], qaug[h, :, qs]))
                ds = (p * nn(vaug[h, ks, :], doaug[h, :, qs])).astype(bf16)
                dv[h] = dv[h] + nn(p.astype(bf16), don[h, qs, :])
                dk[h] = dk[h] + nn(ds, qn[h, qs, :])
                kt = qkvt_ref[width + h * HEAD : width + (h + 1) * HEAD, ks]
                dqt[h, :, qs] = dqt[h, :, qs] + nn(kt, ds)
            return inner

        lax.fori_loop(lo, hi, q_step, 0)
        for h in range(heads):
            vk = dk[h].astype(bf16)
            vv = dv[h].astype(bf16)
            a, b = width + h * HEAD, 2 * width + h * HEAD
            dqkv_ref[ks, a : a + HEAD] = vk
            dqkv_ref[ks, b : b + HEAD] = vv
            dqkvt_ref[a : a + HEAD, ks] = vk.T
            dqkvt_ref[b : b + HEAD, ks] = vv.T
        return carry

    lax.fori_loop(0, length // block, k_step, 0)
    for h in range(heads):
        v = (dqt[h] * 0.125).astype(bf16)
        dqkvt_ref[h * HEAD : (h + 1) * HEAD, :] = v
        dqkv_ref[:, h * HEAD : (h + 1) * HEAD] = v.T


def attend_back_call(n_seq, seq, qkv, qkvt, dot, ot, lse):
    length, cols = qkv.shape
    heads = cols // (3 * HEAD)
    block = 256
    nat = pltpu.VMEM((heads, length, 2 * HEAD), bf16)
    tra = pltpu.VMEM((heads, 2 * HEAD, length), bf16)
    return pl.pallas_call(
        functools.partial(attend_back_kernel, n_seq, block),
        out_shape=(sds((length, cols), bf16), sds((cols, length), bf16)),
        in_specs=[SM] + [VM] * 5,
        out_specs=(VM, VM),
        scratch_shapes=[
            nat, tra, nat, tra,
            pltpu.VMEM((heads, length, HEAD), bf16),
            pltpu.VMEM((heads, length, HEAD), bf16),
            pltpu.VMEM((heads, HEAD, length), f32),
            pltpu.VMEM((heads, block, HEAD), f32),
            pltpu.VMEM((heads, block, HEAD), f32),
        ],
        compiler_params=pltpu.CompilerParams(vmem_limit_bytes=VMEM_LIMIT),
        cost_estimate=pl.CostEstimate(flops=10**10, bytes_accessed=12 * 10**6, transcendentals=10**7),
        name="attend_back",
    )(seq, qkv, qkvt, dot, ot, lse)


def shard_of(r, c):
    return lax.rem(r + 2 * c, 4)


def spread_kernel(src_ref, dst_ref, ss, rs):
    d, r, c = me()
    half = lax.rem(r, 2)
    base = r - half
    n = dst_ref.shape[2]
    peers = [(d, flip(r), c), (d, flip(r), 1 - c), (d, r, 1 - c)]
    greet(peers)
    shard = shard_of(r, c)
    cps = []
    for i, dev in enumerate(peers):
        q = (dev[1] - base) * 2 + dev[2]
        src = src_ref.at[:, pl.ds(pl.multiple_of(q * n, n), n)]
        cp = remote(src, dst_ref.at[shard], ss.at[i], rs.at[i], dev)
        cp.start()
        cps.append(cp)
    q = half * 2 + c
    dst_ref[shard] = src_ref[:, pl.ds(pl.multiple_of(q * n, n), n)]
    for cp in cps:
        cp.wait()


def spread_call(src):
    rows, length = src.shape
    n = length // 4
    return pl.pallas_call(
        spread_kernel,
        out_shape=sds((4, rows, n), bf16),
        in_specs=[VM],
        out_specs=VM,
        scratch_shapes=[DMA((3,)), DMA((3,))],
        compiler_params=pltpu.CompilerParams(
            collective_id=2, has_side_effects=True, vmem_limit_bytes=VMEM_LIMIT
        ),
        name="spread",
    )(src)


def gather_kernel(src_ref, dst_ref, ss, rs):
    d, r, c = me()
    half = lax.rem(r, 2)
    n = src_ref.shape[2]
    peers = [(d, flip(r), c), (d, flip(r), 1 - c), (d, r, 1 - c)]
    greet(peers)
    q = half * 2 + c
    mine = pl.ds(pl.multiple_of(q * n, n), n)
    cps = []
    for i, dev in enumerate(peers):
        cp = remote(src_ref.at[shard_of(dev[1], dev[2])], dst_ref.at[:, mine], ss.at[i], rs.at[i], dev)
        cp.start()
        cps.append(cp)
    dst_ref[:, mine] = src_ref[shard_of(r, c)]
    for cp in cps:
        cp.wait()


def gather_call(src):
    _, rows, n = src.shape
    return pl.pallas_call(
        gather_kernel,
        out_shape=sds((rows, 4 * n), bf16),
        in_specs=[VM],
        out_specs=VM,
        scratch_shapes=[DMA((3,)), DMA((3,))],
        compiler_params=pltpu.CompilerParams(
            collective_id=3, has_side_effects=True, vmem_limit_bytes=VMEM_LIMIT
        ),
        name="gather",
    )(src)


UP, DOWN, OUT, VEC = 0, 768, 1536, 1728
BLOCK_ROWS = 1744


def middle_kernel(
    ot_ref, xf_ref, dya_ref, dyb_ref, w_ref, res_ref, dh1_ref, dot_ref, g_ref,
    wup, wdn, wo, vec, ub, hid, slope, gbuf, facc, yacc, wsem, gsem,
):
    r, c = lax.axis_index("row"), lax.axis_index("col")
    half = lax.rem(r, 2)
    wide = xf_ref.shape[3]
    width = 2 * wide
    tok = dya_ref.shape[0]
    loads_a, loads_b, loads_c = [], [], []
    for j in range(4):
        for cc in range(2):
            cs = slice(cc * wide, (cc + 1) * wide)
            loads_a.append((w_ref.at[j, cc, OUT:VEC], wo.at[j * 192 : (j + 1) * 192, cs], wsem.at[0]))
            for h in range(2):
                hs = slice(h * wide, (h + 1) * wide)
                loads_b.append((w_ref.at[j, cc, hs], wup.at[j, cs, hs], wsem.at[1]))
            loads_c.append((w_ref.at[j, cc, DOWN:OUT], wdn.at[j, :, cs], wsem.at[2]))
        loads_a.append((w_ref.at[j, 0, VEC:BLOCK_ROWS], ub.at[j], wsem.at[0]))
    for cc in range(2):
        loads_a.append((w_ref.at[0, cc, VEC:BLOCK_ROWS], vec.at[:, cc * wide : (cc + 1) * wide], wsem.at[0]))
    for group in (loads_a, loads_b, loads_c):
        for src, dst, sem in group:
            pltpu.make_async_copy(src, dst, sem).start()

    def settle(group):
        for src, dst, sem in group:
            pltpu.make_async_copy(src, dst, sem).wait()

    mine = pl.ds(pl.multiple_of(c * tok, tok), tok)
    x = jnp.concatenate([xf_ref[half, 0, mine, :], xf_ref[half, 1, mine, :]], axis=1).astype(f32)
    settle(loads_a)
    ob, g1, s1, db, g2, s2 = [vec[i : i + 1, :].astype(f32) for i in range(6)]
    o = ot_ref[...].reshape(width, tok).T
    h1 = x + (nn(o, wo[...]) + ob)
    mu = jnp.mean(h1, axis=1, keepdims=True)
    r1 = lax.rsqrt(jnp.mean(h1 * h1, axis=1, keepdims=True) - mu * mu + EPS)
    n1 = (h1 - mu) * r1
    y1 = (n1 * g1 + s1).astype(bf16)
    settle(loads_b)
    settle(loads_c)
    facc[...] = jnp.zeros_like(facc)

    def ahead(j, carry):
        bias = jnp.concatenate([ub[j, 6:7, :], ub[j, 7:8, :]], axis=1).astype(f32)
        u = nn(y1, wup[j]) + bias
        cdf = 0.5 * (1.0 + lax.erf(u * INV_ROOT_TWO))
        hj = (u * cdf).astype(bf16)
        hid[j] = hj
        slope[j] = cdf + u * jnp.exp(-0.5 * u * u) * INV_ROOT_TAU
        facc[...] += nn(hj, wdn[j])
        return carry

    lax.fori_loop(0, 4, ahead, 0)
    h2 = y1.astype(f32) + (facc[...] + db)
    mu2 = jnp.mean(h2, axis=1, keepdims=True)
    r2 = lax.rsqrt(jnp.mean(h2 * h2, axis=1, keepdims=True) - mu2 * mu2 + EPS)
    n2 = (h2 - mu2) * r2
    res_ref[...] = (n2 * g2 + s2).astype(bf16)
    own, other = dya_ref[...], dyb_ref[...]
    left = jnp.where(c == 0, own, other)
    right = jnp.where(c == 0, other, own)
    dy = jnp.concatenate([left, right], axis=1).astype(f32)
    e2 = dy * g2
    dh2 = r2 * (e2 - jnp.mean(e2, axis=1, keepdims=True) - n2 * jnp.mean(e2 * n2, axis=1, keepdims=True))
    g2g = jnp.sum(dy * n2, axis=0, keepdims=True)
    s2g = jnp.sum(dy, axis=0, keepdims=True)
    df = dh2.astype(bf16)
    dbg = jnp.sum(df.astype(f32), axis=0, keepdims=True)
    yacc[...] = dh2
    y1t = y1.T

    def back(j, carry):
        du = (nt(df, wdn[j]) * slope[j]).astype(bf16)
        ubg = jnp.sum(du.astype(f32), axis=0, keepdims=True)
        gd = tn(hid[j], df).astype(bf16)
        gu = nn(y1t, du).astype(bf16)
        for cc in range(2):
            cs = slice(cc * wide, (cc + 1) * wide)
            for h in range(2):
                gbuf[j, cc, h * wide : (h + 1) * wide, :] = gu[cs, h * wide : (h + 1) * wide]
            gbuf[j, cc, DOWN:OUT, :] = gd[:, cs]
        ub[j, 6:7, :] = ubg[:, :wide].astype(bf16)
        ub[j, 7:8, :] = ubg[:, wide:].astype(bf16)
        yacc[...] += nt(du, wup[j])
        return carry

    lax.fori_loop(0, 4, back, 0)
    dy1 = yacc[...]
    e1 = dy1 * g1
    dh1 = r1 * (e1 - jnp.mean(e1, axis=1, keepdims=True) - n1 * jnp.mean(e1 * n1, axis=1, keepdims=True))
    dh1_ref[...] = dh1
    g1g = jnp.sum(dy1 * n1, axis=0, keepdims=True)
    s1g = jnp.sum(dy1, axis=0, keepdims=True)
    da = dh1.astype(bf16)
    obg = jnp.sum(da.astype(f32), axis=0, keepdims=True)
    dot_ref[...] = nt(da, wo[...]).T.astype(bf16).reshape(dot_ref.shape)
    go = nn(ot_ref[...].reshape(width, tok), da).astype(bf16)
    pad = g_ref.shape[2] - VEC
    row = lax.broadcasted_iota(jnp.int32, (pad, wide), 0)
    for j in range(4):
        for cc in range(2):
            cs = slice(cc * wide, (cc + 1) * wide)
            gbuf[j, cc, OUT:VEC, :] = go[j * 192 : (j + 1) * 192, cs]
            tail = jnp.zeros((pad, wide), f32)
            for i, v in enumerate((obg, g1g, s1g, dbg, g2g, s2g)):
                tail = jnp.where(row == i, v[:, cs], tail)
            tail = jnp.where(row == 6, ub[j, 6:7, :].astype(f32), tail)
            tail = jnp.where(row == 7, ub[j, 7:8, :].astype(f32), tail)
            gbuf[j, cc, VEC:, :] = tail.astype(bf16)
    out = pltpu.make_async_copy(gbuf, g_ref, gsem)
    out.start()
    out.wait()


def middle_call(ot, xf, dya, dyb, w, g_rows):
    tok, wide = dya.shape
    width = 2 * wide
    return pl.pallas_call(
        middle_kernel,
        out_shape=(
            sds((tok, width), bf16),
            sds((tok, width), f32),
            sds((4, width // 4, tok), bf16),
            sds((4, 2, g_rows, wide), bf16),
        ),
        in_specs=[VM] * 4 + [ANY],
        out_specs=(VM, VM, VM, ANY),
        scratch_shapes=[
            pltpu.VMEM((4, width, width), bf16),
            pltpu.VMEM((4, width, width), bf16),
            pltpu.VMEM((width, width), bf16),
            pltpu.VMEM((16, width), bf16),
            pltpu.VMEM((4, 16, wide), bf16),
            pltpu.VMEM((4, tok, width), bf16),
            pltpu.VMEM((4, tok, width), f32),
            pltpu.VMEM((4, 2, g_rows, wide), bf16),
            pltpu.VMEM((tok, width), f32),
            pltpu.VMEM((tok, width), f32),
            DMA((3,)),
            DMA,
        ],
        compiler_params=pltpu.CompilerParams(vmem_limit_bytes=VMEM_LIMIT),
        cost_estimate=pl.CostEstimate(flops=16 * 10**9, bytes_accessed=30 * 10**6, transcendentals=4 * 10**6),
        name="middle",
    )(ot, xf, dya, dyb, w)


def return_kernel(
    n_dp, dqkv_ref, dqkvt_ref, wq_ref, xf_ref, dh1_ref, res_ref, deal_ref,
    out_ref, ig_ref, gq_ref,
    back_a, back_b, fin, tocore, fromcore, toz, fromz, s_a, r_a, s_b, r_b, s_c, r_c, s_z, r_z,
):
    d, r, c = me()
    half = lax.rem(r, 2)
    tok = dh1_ref.shape[0]
    wide = wq_ref.shape[2] if False else xf_ref.shape[3]
    width = 2 * wide
    tokens = 2 * tok
    piece = tokens // n_dp
    n_half = n_dp // 2
    core = (d, r, 1 - c)
    zdev = (d, flip(r), c)
    peers = [(lax.rem(d + k, n_dp), r, cc) for k in range(1, n_dp) for cc in (0, 1)]
    greet(peers + [core, zdev])

    def grp(g):
        return pl.ds(pl.multiple_of(g * piece, piece), piece)

    def send_back(src, back, ss, rs):
        for i in range(n_half):
            s = c * n_half + i
            for cc in range(2):
                ref = src.at[cc, i * piece : (i + 1) * piece, :]
                cp = remote(ref, back.at[grp(d), :], ss.at[i, cc], rs.at[d], (s, r, cc))
                local = (s == d) & (c == cc)

                @pl.when(jnp.logical_not(local))
                def _():
                    cp.start()

                @pl.when(local)
                def _():
                    back[grp(d), :] = src[cc, i * piece : (i + 1) * piece, :]

    def sent_back(src, back, ss, rs):
        for i in range(n_half):
            s = c * n_half + i
            for cc in range(2):
                ref = src.at[cc, i * piece : (i + 1) * piece, :]

                @pl.when(jnp.logical_not((s == d) & (c == cc)))
                def _():
                    remote(ref, back.at[grp(d), :], ss.at[i, cc], rs.at[d], (s, r, cc)).wait_send()

    def got_back(src, back, ss, rs):
        holder = lax.div(d, n_half)
        for g in range(n_dp):

            @pl.when(jnp.logical_not((d == g) & (holder == c)))
            def _():
                remote(
                    src.at[0, 0:piece, :], back.at[grp(g), :], ss.at[0, 0], rs.at[g], (d, r, 1 - c)
                ).wait_recv()

    fin[0, 0] = res_ref[:, :wide]
    fin[0, 1] = res_ref[:, wide:]
    send_back(fin.at[0], back_a, s_a, r_a)

    w0 = wq_ref[0, :wide, :]
    w1 = wq_ref[1, :wide, :]

    def part(h, cc):
        q = h * 2 + cc
        rows = dqkv_ref[pl.ds(pl.multiple_of(q * tok, tok), tok), :]
        return jnp.concatenate([nt(rows, w0), nt(rows, w1)], axis=1)

    tocore[0] = part(1 - half, 1 - c).astype(bf16)
    cp_far = remote(tocore.at[0], fromcore.at[0], s_c.at[0], r_c.at[0], core)
    cp_far.start()
    tocore[1] = part(half, 1 - c).astype(bf16)
    cp_near = remote(tocore.at[1], fromcore.at[1], s_c.at[1], r_c.at[1], core)
    cp_near.start()
    far = part(1 - half, c)
    cp_far.wait_recv()
    toz[...] = (far + fromcore[0].astype(f32)).astype(bf16)
    cp_z = remote(toz, fromz, s_z, r_z, zdev)
    cp_z.start()
    total = part(half, c) + dh1_ref[...]
    n_cols = dqkvt_ref.shape[0]
    length = dqkvt_ref.shape[1]
    for f in range(2):
        g = nn(dqkvt_ref[:, : length // 2], xf_ref[0, f]) + nn(dqkvt_ref[:, length // 2 :], xf_ref[1, f])
        gq_ref[f, :n_cols, :] = g.astype(bf16)
    third = n_cols // 3
    sums = jnp.sum(dqkv_ref[...].astype(f32), axis=0, keepdims=True)
    bias = jnp.concatenate([sums[:, :third], sums[:, 2 * third :]], axis=1)
    pad = gq_ref.shape[1] - n_cols
    row = lax.broadcasted_iota(jnp.int32, (pad, wide), 0)
    tail = jnp.where(row == 0, bias, 0.0).astype(bf16)
    for f in range(2):
        gq_ref[f, n_cols:, :] = tail
    place = (lax.broadcasted_iota(jnp.int32, (tokens, tokens), 0) == deal_ref[...]).astype(bf16)
    got_back(fin.at[0], back_a, s_a, r_a)
    out_ref[...] = nn(place, back_a[...]).astype(bf16)
    cp_near.wait_recv()
    total = total + fromcore[1].astype(f32)
    cp_z.wait_recv()
    total = (total + fromz[...].astype(f32)).astype(bf16)
    fin[1, 0] = total[:, :wide]
    fin[1, 1] = total[:, wide:]
    send_back(fin.at[1], back_b, s_b, r_b)
    got_back(fin.at[1], back_b, s_b, r_b)
    ig_ref[...] = nn(place, back_b[...]).astype(bf16)
    sent_back(fin.at[0], back_a, s_a, r_a)
    sent_back(fin.at[1], back_b, s_b, r_b)
    cp_far.wait_send()
    cp_near.wait_send()
    cp_z.wait_send()


def return_call(n_dp, dqkv, dqkvt, wq, xf, dh1, res, deal_row, gq_rows):
    tok, width = dh1.shape
    wide = width // 2
    tokens = 2 * tok
    n_half = n_dp // 2
    return pl.pallas_call(
        functools.partial(return_kernel, n_dp),
        out_shape=(
            sds((tokens, wide), bf16),
            sds((tokens, wide), bf16),
            sds((2, gq_rows, wide), bf16),
        ),
        in_specs=[VM] * 7,
        out_specs=(VM,) * 3,
        scratch_shapes=[
            pltpu.VMEM((tokens, wide), bf16),
            pltpu.VMEM((tokens, wide), bf16),
            pltpu.VMEM((2, 2, tok, wide), bf16),
            pltpu.VMEM((2, tok, width), bf16),
            pltpu.VMEM((2, tok, width), bf16),
            pltpu.VMEM((tok, width), bf16),
            pltpu.VMEM((tok, width), bf16),
            DMA((n_half, 2)), DMA((n_dp,)),
            DMA((n_half, 2)), DMA((n_dp,)),
            DMA((2,)), DMA((2,)), DMA, DMA,
        ],
        compiler_params=pltpu.CompilerParams(
            collective_id=4, has_side_effects=True, vmem_limit_bytes=VMEM_LIMIT
        ),
        name="return",
    )(dqkv, dqkvt, wq, xf, dh1, res, deal_row)


def round_up(v, m):
    return (v + m - 1) // m * m


def on_device(
    n_dp, inputs, out_grad, deal, seq_lengths, key_trim, query_weight, query_bias, key_weight,
    value_weight, value_bias, out_weight, out_bias, first_gain, first_shift, up_weight, up_bias,
    down_weight, down_bias, second_gain, second_shift,
):
    d, r, c = me()
    wide = inputs.shape[1]
    n_seq = seq_lengths.shape[1]
    unit = 16 * n_dp // math.gcd(16, n_dp)
    step = 16 * n_dp

    blob = jnp.concatenate(
        [up_weight[:, :wide], up_weight[:, wide:], down_weight, out_weight]
        + [v[None, :] for v in (out_bias, first_gain, first_shift, down_bias, second_gain, second_shift)]
        + [up_bias.reshape(2, wide)],
        axis=0,
    )
    rows_w = round_up(BLOCK_ROWS, unit)
    blob = jnp.pad(blob, ((0, rows_w - blob.shape[0]), (0, 0)))
    share = lax.dynamic_slice_in_dim(blob, d * (rows_w // n_dp), rows_w // n_dp, 0)
    gathered = lax.all_gather(share, ("row", "col", "dp"), axis=0, tiled=True)
    gathered = gathered.reshape(4, 2, rows_w, wide)

    third = query_weight.shape[1]
    bias_row = jnp.concatenate([query_bias, jnp.zeros((third,), bf16), value_bias])[None, :]
    wqkv = jnp.concatenate([query_weight, key_weight, value_weight], axis=1)
    wqkv = jnp.concatenate([wqkv, jnp.pad(bias_row, ((0, 15), (0, 0)))], axis=0)
    seq = jnp.pad(jnp.concatenate([seq_lengths, key_trim], axis=0), ((0, 6), (0, 128 - n_seq)))

    xf, dya, dyb, qkv, qkvt, wq, seq = deal_call(n_dp, inputs, out_grad, deal.reshape(-1, 1), wqkv, seq)
    ot, lse = attend_call(n_seq, seq, qkv, qkvt)
    ot_mid = spread_call(ot)
    g_rows = round_up(VEC + 16, step)
    res, dh1, dot_mid, grads = middle_call(ot_mid, xf, dya, dyb, gathered, g_rows)
    dot = gather_call(dot_mid)
    dqkv, dqkvt = attend_back_call(n_seq, seq, qkv, qkvt, dot, ot, lse)
    gq_rows = round_up(3 * third + 16, step)
    output, input_grad, gq = return_call(n_dp, dqkv, dqkvt, wq, xf, dh1, res, deal, gq_rows)

    mine = lax.psum_scatter(grads.reshape(-1, wide), ("row", "col", "dp"), scatter_dimension=0, tiled=True)
    mine = lax.all_gather(mine, "dp", axis=0, tiled=True)
    placed = jnp.where((jnp.arange(4) == shard_of(r, c))[:, None, None, None], gq[None], 0).astype(bf16)
    mine_q = lax.psum_scatter(placed.reshape(-1, wide), ("row", "col", "dp"), scatter_dimension=0, tiled=True)
    mine_q = lax.all_gather(mine_q, "dp", axis=0, tiled=True)

    g = mine.astype(f32)
    up_grad = jnp.concatenate([g[:wide], g[wide : 2 * wide]], axis=1)
    down_grad = g[DOWN:OUT]
    out_grad_w = g[OUT:VEC]
    vec = g[VEC : VEC + 8]
    gqf = mine_q.astype(f32)
    query_grad = gqf[:third].T
    key_grad = gqf[third : 2 * third].T
    value_grad = gqf[2 * third : 3 * third].T
    brow = gqf[3 * third]
    return (
        output, input_grad, query_grad, brow[:third], key_grad, value_grad, brow[third:], out_grad_w,
        vec[0], vec[1], vec[2], up_grad, vec[6:8].reshape(-1), down_grad, vec[3], vec[4], vec[5],
    )


def solution(mesh):
    n_dp = mesh.shape["dp"]
    tok = P(("dp", "row"), "col")
    one = P("col")
    row = P("row")
    a = P("col", "row")
    b = P("row", "col")
    seqs = P(("dp", "col"), None)
    in_specs = (
        tok, tok, P(("dp", "row"), None), seqs, seqs, a, row, a, a, row, b, one, one, one, a, row, b, one, one, one,
    )
    out_specs = (tok, tok, a, row, a, a, row, b, one, one, one, a, row, b, one, one, one)
    return jax.shard_map(
        functools.partial(on_device, n_dp), mesh=mesh, in_specs=in_specs, out_specs=out_specs, check_vma=False
    )
```

time: 1110 us -> 499 us (0.45); the launches traced: 1090 us -> 496 us
  waiting for transfers between devices: 583 us -> 176 us
  Pallas kernels: 0 us -> 254 us
  matrix products: 157 us -> 0 us
  blocking collectives: 103 us -> 10.6 us
  other arithmetic: 88.1 us -> 7.79 us
  local copies, waits for them, and re-layouts: 84.2 us -> 33.2 us
  loops' own time: 48.1 us -> 0 us
  starting transfers between devices: 14.8 us -> 0.38 us
    all_gather x8 -> x2, waiting for transfers between devices: 311 us -> 18.8 us  [the longest x1 18.8 us: on_device(): mine = lax.all_gather(mine, 'dp', axis=0, tiled=True)]
    pallas_call x0 -> x7, Pallas kernels: none -> 254 us  [the longest x1 67.4 us: return_call(): pl.pallas_call(functools.partial(return_kernel, n_dp), out_shape=(sds((to...]
    dot_general x96 -> x0, matrix products: 157 us -> none  [the longest x40 75.3 us: contract_cols(): lax.dot_general(left, right, (((1,), (1,)), ((), ())), preferred_element_...]
    reduce_scatter x8 -> x2, waiting for transfers between devices: 262 us -> 157 us  [the longest x1 109 us: on_device(): lax.psum_scatter(placed.reshape(-1, wide), ('row', 'col', 'dp'), scatter_...]
    psum x6 -> x0, blocking collectives: 89.6 us -> none  [the longest x1 72.2 us: on_device(): lax.psum((out_bias_part, first_gain_part, first_shift_part, down_bias_par...]
    another operation x8 -> x0, loops' own time: 48.1 us -> none  [the longest x3 23.9 us: one_head(): lax.scan(one_block, (zero_acc, zero_acc), offsets)]
    convert_element_type x36 -> x2, other arithmetic: 48.6 us -> 1.69 us  [the longest x1 1.62 us: on_device(): g = mine.astype(f32)]
    reduce_sum x23 -> x0, other arithmetic: 35 us -> none  [the longest x12 8.53 us: one_block(): row_sum = jnp.sum(exp_scores, axis=1, keepdims=True)]
  transfers between devices with their start and end apart: 20 -> 4, of which waited for: 17 -> 3; matrix products, arithmetic and copies ran while one was open for 5% -> 2% of each run, Pallas kernels for 0% -> 44%
where the time goes in v1:
time: 499 us; the launch traced here: 496 us
  Pallas kernels  254 us (51%)
  waiting for transfers between devices  176 us (35%)
  local copies, waits for them, and re-layouts  33.2 us (7%)
  between operations  14 us (3%)
  blocking collectives  10.6 us (2%)
  other arithmetic  7.79 us (2%)
    reduce_scatter x1, waiting for transfers between devices, on_device(): lax.psum_scatter(placed.reshape(-1, wide), ('row', 'col', 'dp'), scatter_...  109 us
    pallas_call x1, Pallas kernels, return_call(): pl.pallas_call(functools.partial(return_kernel, n_dp), out_shape=(sds((to...  67.4 us
    pallas_call x1, Pallas kernels, deal_call(): pl.pallas_call(functools.partial(deal_kernel, n_dp), out_shape=(sds((2, 2...  50 us
    reduce_scatter x1, waiting for transfers between devices, on_device(): lax.psum_scatter(grads.reshape(-1, wide), ('row', 'col', 'dp'), scatter_d...  48.1 us
    pallas_call x1, Pallas kernels, middle_call(): pl.pallas_call(middle_kernel, out_shape=(sds((tok, width), bf16), sds((to...  33.8 us
    pallas_call x1, Pallas kernels, attend_back_call(): pl.pallas_call(functools.partial(attend_back_kernel, n_seq, block), out_s...  33.5 us
    pallas_call x1, Pallas kernels, attend_call(): pl.pallas_call(functools.partial(attend_kernel, n_seq, block), out_shape=...  28.2 us
    pallas_call x1, Pallas kernels, spread_call(): pl.pallas_call(spread_kernel, out_shape=sds((4, rows, n), bf16), in_specs...  27.1 us
  transfers between devices with their start and end apart: 4, of which 3 were waited for; matrix products, arithmetic and copies ran while one was open for 2% of the time, Pallas kernels for 44%

profile of v1, /device:TPU:30, one launch (start us, length us, event | category | flops | bytes accessed | tf_op | source)
XLA Modules:
  0.0 496.4 jit_solution(4829629400836016658)
XLA Ops:
  7.2 0.0 all-gather.6.cloned.1.call-start
  7.2 1.1 fusion.4
  8.4 0.7 broadcast_in_dim.54
  9.1 0.7 broadcast_in_dim.55
  9.8 0.7 broadcast_in_dim.56
  10.5 0.7 broadcast_in_dim.57
  11.1 0.7 broadcast_in_dim.58
  11.8 0.7 broadcast_in_dim.59
  12.5 0.7 reshape.60
  13.2 4.1 concatenate.22
  17.3 0.8 fusion.2
  18.2 0.0 reduce-scatter.5.cloned.1.call-start
  18.2 0.1 copy.44
  18.4 0.1 copy.45
  18.6 0.1 copy.46
  18.7 0.1 pad_maximum_fusion.1
  18.8 1.0 copy.47.deal_ref
  19.9 0.6 pad.13.seq_ref
  20.5 0.9 fusion.1.w_ref
  21.4 50.0 %deal.1 = (bf16[2,2,1024,384]{3,2,1,0:T(8,128)(2,1)}, bf16[512,384]{1,0:T(8,128)(2,1)}, bf16[512,384]{1,0:T(8,128)(2,1)}, bf16[2048,576]{1,0:T(8,128)(2,1)}, bf1...) custom-call(bf16[1024,384]{1,0:T(8,128)(2,1)} %x_ref.1, bf16[1024,384]{1,0:T(8,128)(2,1)} %dy_ref.1, ...), custom_call_target="tpu_custom_call" | custom-call | tf_op jit(solution)/shard_map/deal/pallas_call | solution.py:189
  71.4 28.2 %attend.1 = (bf16[192,2048]{1,0:T(8,128)(2,1)}, f32[8,2048]{1,0:T(8,128)}) custom-call(s32[8,128]{1,0:T(8,128)} %get-tuple-element.35.seq_ref, bf16[2048,576]{1,0:T(8,128)(2,1)} %get-tuple-element.36.qkv_ref, bf16[576,2048]{1,0:T(8,128)(2,1)} %get-tuple-element.37.qkvt_ref), custom_call_target="tpu_custom_call" | custom-call | flops 4000000000 | bytes 6000000 | tf_op jit(solution)/shard_map/attend/pallas_call | solution.py:320
  99.6 27.1 %spread.1.ot_ref = bf16[4,192,512]{2,1,0:T(8,128)(2,1)} custom-call(bf16[192,2048]{1,0:T(8,128)(2,1)} %get-tuple-element.38.src_ref.ot_ref), custom_call_target="tpu_custom_call" | custom-call | tf_op jit(solution)/shard_map/spread/pallas_call | solution.py:459
  126.8 0.0 all-gather.6.cloned.1.call-done
  126.8 13.7 %reshape.61.w_ref = bf16[4,2,1744,384]{3,2,1,0:T(8,128)(2,1)} reshape(bf16[32,436,384]{2,1,0:T(8,128)(2,1)} %all-gather.6.cloned.1.call-done) | data formatting | bytes 21430272 | tf_op jit(solution)/shard_map/reshape | solution.py:828
  140.5 33.8 %middle.1 = (bf16[512,768]{1,0:T(8,128)(2,1)}, f32[512,768]{1,0:T(8,128)}, bf16[4,192,512]{2,1,0:T(8,128)(2,1)}, bf16[4,2,1792,384]{3,2,1,0:T(8,128)(2,1)}) custom-call(bf16[4,192,512]{2,1,0:T(8,128)(2,1)} %spread.1.ot_ref, bf16[2,2,1024,384]{3,2,1,0:T(8,128)(2,1)} %get-tuple-element.39.xf_ref, bf16[512,384]{1,0:T(8,128)(2,1)} %get-tuple-element.40.dya_ref, ...), custom_call_target="tpu_custom_call" | custom-call | flops 16000000000 | bytes 30000000 | tf_op jit(solution)/shard_map/middle/pallas_call | solution.py:627
  174.3 0.3 reduce-scatter.3.cloned.1.call-start
  174.6 0.1 broadcast_in_dim.60
  174.7 14.2 %gather.1.dot_ref = bf16[192,2048]{1,0:T(8,128)(2,1)} custom-call(bf16[4,192,512]{2,1,0:T(8,128)(2,1)} %get-tuple-element.42.src_ref), custom_call_target="tpu_custom_call" | custom-call | tf_op jit(solution)/shard_map/gather/pallas_call | solution.py:492
  188.9 33.5 %attend_back.1 = (bf16[2048,576]{1,0:T(8,128)(2,1)}, bf16[576,2048]{1,0:T(8,128)(2,1)}) custom-call(s32[8,128]{1,0:T(8,128)} %get-tuple-element.35.seq_ref, bf16[2048,576]{1,0:T(8,128)(2,1)} %get-tuple-element.36.qkv_ref, bf16[576,2048]{1,0:T(8,128)(2,1)} %get-tuple-element.37.qkvt_ref, bf16[192,2048]{1,0:T(8,128)(2,1)} %gather.1.dot_ref, ...), custom_call_target="tpu_custom_call" | custom-call | flops 10000000000 | bytes 12000000 | tf_op jit(solution)/shard_map/attend_back/pallas_call | solution.py:412
  222.4 67.4 %return.1 = (bf16[1024,384]{1,0:T(8,128)(2,1)}, bf16[1024,384]{1,0:T(8,128)(2,1)}, bf16[2,640,384]{2,1,0:T(8,128)(2,1)}) custom-call(bf16[2048,576]{1,0:T(8,128)(2,1)} %get-tuple-element.44.dqkv_ref, bf16[576,2048]{1,0:T(8,128)(2,1)} %get-tuple-element.45.dqkvt_ref, bf16[2,400,576]{2,1,0:T(8,128)(2,1)} %get-tuple-element.46.wq_ref, ...), custom_call_target="tpu_custom_call" | custom-call | tf_op jit(solution)/shard_map/return/pallas_call | solution.py:775
  289.8 4.0 bitcast_select_fusion
  293.8 0.0 all-gather.4.cloned.1.call-start
  293.9 48.1 %reduce-scatter.5.cloned.1.call-done = bf16[448,384]{1,0:T(8,128)(2,1)} async-done(((bf16[14336,384]{1,0:T(8,128)(2,1)}), bf16[448,384]{1,0:T(8,128)(2,1)}) %reduce-scatter.5.cloned.1.call-update) | async-done | bytes 344080 | tf_op jit(solution)/shard_map/reduce_scatter | solution.py:846
  342.0 109.2 %reduce-scatter.3.cloned.1.call-done = bf16[160,384]{1,0:T(8,128)(2,1)} async-done(((bf16[5120,384]{1,0:T(8,128)(2,1)}), bf16[160,384]{1,0:T(8,128)(2,1)}) %reduce-scatter.3.cloned.1.call-update) | async-done | bytes 122896 | tf_op jit(solution)/shard_map/reduce_scatter | solution.py:849
  451.2 10.6 %all_gather.10 = bf16[640,384]{1,0:T(8,128)(2,1)S(1)} all-gather(bf16[160,384]{1,0:T(8,128)(2,1)} %reduce-scatter.3.cloned.1.call-done), channel_id=1, replica_groups=mesh['dp'=4,'row'=4,'col'=2] {'dp'}, dimensions={0}, use_global_device_ids=true | all-gather | bytes 614400 | tf_op jit(solution)/shard_map/all_gather | solution.py:850
  461.8 0.1 convert_element_type.12
  461.9 0.6 fusion.5
  462.5 0.9 slice_bitcast_fusion
  463.5 18.8 %all-gather.4.cloned.1.call-done = bf16[1792,384]{1,0:T(8,128)(2,1)} async-done(((bf16[448,384]{1,0:T(8,128)(2,1)}), bf16[1792,384]{1,0:T(8,128)(2,1)}) %all-gather.4.cloned.1.call-update) | async-done | bytes 1376272 | tf_op jit(solution)/shard_map/all_gather | solution.py:847
  482.3 1.6 convert_element_type.13
  483.9 0.6 slice_reduce_fusion
  484.5 0.6 reshape.63
  485.1 0.1 fusion.3
  485.2 1.1 pad_maximum_fusion
  486.3 1.1 slice.103
  487.4 0.7 slice.96
  488.1 0.9 copy.50
  489.0 0.9 copy.51
  (32 shorter events, 0.2 us)
Async XLA Ops:
  7.2 119.6 %all-gather.6.cloned.1.call-start = ((), (), s32[]{:S(2)}) async-start(), calls=%async_computation.5 | async-start | bytes 11151360 | tf_op jit(solution)/shard_map/all_gather | solution.py:827
  8.4 9.9 %copy-start.3 = (bf16[384,192]{0,1:T(8,128)(2,1)S(1)}, bf16[384,192]{0,1:T(8,128)(2,1)}, u32[]{:S(2)}) copy-start(bf16[384,192]{0,1:T(8,128)(2,1)} %param.25) | copy-start | bytes 442372
  13.2 5.2 %copy-start.4 = (bf16[384,192]{0,1:T(8,128)(2,1)S(1)}, bf16[384,192]{0,1:T(8,128)(2,1)}, u32[]{:S(2)}) copy-start(bf16[384,192]{0,1:T(8,128)(2,1)} %param.27) | copy-start | bytes 442372
  13.2 5.4 %copy-start.5 = (bf16[384,192]{0,1:T(8,128)(2,1)S(1)}, bf16[384,192]{0,1:T(8,128)(2,1)}, u32[]{:S(2)}) copy-start(bf16[384,192]{0,1:T(8,128)(2,1)} %param.28) | copy-start | bytes 442372
  13.2 5.5 %copy-start.7 = (bf16[192]{0:T(256)(128)(2,1)S(1)}, bf16[192]{0:T(256)(128)(2,1)}, u32[]{:S(2)}) copy-start(bf16[192]{0:T(256)(128)(2,1)} %param.29) | copy-start | bytes 1156
  13.2 5.5 %copy-start.8 = (bf16[192]{0:T(256)(128)(2,1)S(1)}, bf16[192]{0:T(256)(128)(2,1)}, u32[]{:S(2)}) copy-start(bf16[192]{0:T(256)(128)(2,1)} %param.26) | copy-start | bytes 1156
  13.2 5.6 %copy-start.6 = (s32[1,1024]{1,0:T(1,128)S(1)}, s32[1,1024]{1,0:T(1,128)}, u32[]{:S(2)}) copy-start(s32[1,1024]{1,0:T(1,128)} %deal_ref.1) | copy-start | bytes 12292
  17.3 2.5 copy-start.9
  17.3 2.5 copy-start.10
  18.2 323.8 %reduce-scatter.5.cloned.1.call-start = ((), (), s32[]{:S(2)}) async-start(), calls=%async_computation.3 | async-start | bytes 11354112 | tf_op jit(solution)/shard_map/reduce_scatter | solution.py:846
  174.3 276.9 %reduce-scatter.3.cloned.1.call-start = ((), (), s32[]{:S(2)}) async-start(), calls=%async_computation.2 | async-start | bytes 4055040 | tf_op jit(solution)/shard_map/reduce_scatter | solution.py:849
  293.8 188.4 %all-gather.4.cloned.1.call-start = ((), (), s32[]{:S(2)}) async-start(), calls=%async_computation.4 | async-start | bytes 1720320 | tf_op jit(solution)/shard_map/all_gather | solution.py:847
  482.3 2.3 copy-start
  485.2 2.9 copy-start.2
  486.3 2.7 copy-start.1
Sparse Core Ops, SparseCore 0:
  18.3 107.9 all-gather.5
  174.5 167.4 reduce-scatter.4
  347.3 103.7 reduce-scatter.2
  452.9 29.3 all-gather.3

commit v2 on v1

--- a/solution.py
+++ b/solution.py
@@ -1,5 +1,4 @@
 import functools
-import math
 
 import jax
 import jax.numpy as jnp
@@ -18,6 +17,7 @@
 INV_ROOT_TWO = 0.7071067811865476
 INV_ROOT_TAU = 0.3989422804014327
 VMEM_LIMIT = 62 * 1024 * 1024
+DOWN, OUT, VEC = 768, 1536, 1728
 
 VM = pl.BlockSpec(memory_space=pltpu.VMEM)
 SM = pl.BlockSpec(memory_space=pltpu.SMEM)
@@ -63,56 +63,92 @@
 
 
 def deal_kernel(
-    n_dp, x_ref, dy_ref, deal_ref, w_ref, seq_ref,
-    xf_ref, dya_ref, dyb_ref, qkv_ref, qkvt_ref, wq_ref, seqo_ref,
-    xs, dys, dyin, seqrx, sx, rx, sc, rc, sz, rz, sc2, rc2, sd, rd, sw, rw, sm, rm,
+    n_dp, rows_w, x_ref, dy_ref, deal_ref, qw_ref, kw_ref, vw_ref, qb_ref, vb_ref, up_ref, dn_ref, ow_ref,
+    ob_ref, g1_ref, s1_ref, db_ref, g2_ref, s2_ref, ub_ref, len_ref, trim_ref,
+    xf_ref, dys_ref, qkv_ref, qkvt_ref, wq_ref, seqo_ref, wg_ref,
+    xs, seq, seqrx, w, bias, biases, blob, col,
+    sx, rx, sc, rc, sz, rz, sc2, rc2, sw, rw, sb, rb, sm, rm, ss, rs, sf, rf, sl,
 ):
     d, r, c = me()
     half = lax.rem(r, 2)
-    tokens = x_ref.shape[0]
+    tokens, wide = x_ref.shape
     piece = tokens // n_dp
+    third = qw_ref.shape[0]
     core = (d, r, 1 - c)
     zdev = (d, flip(r), c)
     far_row = lax.rem(r + 2, 4)
     ring = [(lax.rem(d + k, n_dp), r, c) for k in range(1, n_dp)]
-    greet(ring + [core, zdev, (d, far_row, 0), (d, far_row, 1)])
-
-    w_far = remote(w_ref, wq_ref.at[c], sw.at[0], rw.at[c], (d, far_row, 1))
-    w_far.start()
-    w_near = remote(w_ref, wq_ref.at[1], sw.at[1], rw.at[1], (d, r, 0))
-
-    @pl.when(c == 0)
-    def _():
-        wq_ref[0] = w_ref[...]
-
-    @pl.when(c == 1)
-    def _():
-        w_near.start()
-
-    seq_cp = remote(seq_ref, seqrx, sm.at[0], rm.at[0], core)
-    seq_cp.start()
+    rows_dev = [(d, lax.rem(r + k, 4), c) for k in (1, 2, 3)]
+    greet(ring + rows_dev + [core, (d, far_row, 1 - c)])
+
+    blob[0:wide, :] = up_ref[:, :wide]
+    blob[wide : 2 * wide, :] = up_ref[:, wide:]
+    blob[DOWN:OUT, :] = dn_ref[...]
+    blob[OUT:VEC, :] = ow_ref[...]
+    vecs = [v[...].reshape(1, wide) for v in (ob_ref, g1_ref, s1_ref, db_ref, g2_ref, s2_ref)]
+    vecs += [ub_ref[0:wide].reshape(1, wide), ub_ref[wide : 2 * wide].reshape(1, wide)]
+    row = lax.broadcasted_iota(jnp.int32, (16, wide), 0)
+    tail = jnp.zeros((16, wide), f32)
+    for i, v in enumerate(vecs):
+        tail = jnp.where(row == i, v.astype(f32), tail)
+    blob[VEC : VEC + 16, :] = tail.astype(bf16)
+    blob[VEC + 16 :, :] = jnp.zeros((rows_w - VEC - 16, wide), bf16)
+    share = rows_w // n_dp
+    my_share = pl.ds(pl.multiple_of(d * share, share), share)
+    share_cp = [
+        remote(blob.at[my_share, :], wg_ref.at[r, my_share, :], ss.at[k], rs.at[k], dev)
+        for k, dev in enumerate(rows_dev)
+    ]
+    for cp in share_cp:
+        cp.start()
+    local_w = pltpu.make_async_copy(blob, wg_ref.at[r], sl)
+    local_w.start()
 
     def rows(s):
         return pl.ds(pl.multiple_of(s * piece, piece), piece)
 
+    col[...] = jnp.broadcast_to(deal_ref[...], (8, tokens)).T
     lane = lax.broadcasted_iota(jnp.int32, (piece, tokens), 1)
     sends = []
-    dsends = []
     for k in list(range(1, n_dp)) + [0]:
         dest = lax.rem(d + k, n_dp)
-        pick = (deal_ref[rows(dest), :] == lane).astype(bf16)
+        pick = (col[rows(dest), 0:1] == lane).astype(bf16)
         px = nn(pick, x_ref[...]).astype(bf16)
-        pd = nn(pick, dy_ref[...]).astype(bf16)
         if k:
             xs[k] = px
             cp = remote(xs.at[k], xf_ref.at[half, c, rows(d), :], sx.at[k], rx.at[k], (dest, r, c))
             cp.start()
             sends.append(cp)
-            dys[k] = pd
-            dsends.append(remote(dys.at[k], dyin.at[rows(d), :], sd.at[k], rd.at[k], (dest, r, c)))
         else:
             xf_ref[half, c, rows(d), :] = px
-            dyin[rows(d), :] = pd
+
+    w[:third, :] = qw_ref[...]
+    w[third : 2 * third, :] = kw_ref[...]
+    w[2 * third :, :] = vw_ref[...]
+    w_far = remote(w, wq_ref.at[c], sw.at[0], rw.at[c], (d, far_row, 1))
+    w_far.start()
+    w_near = remote(w, wq_ref.at[1], sw.at[1], rw.at[1], (d, r, 0))
+    flat = jnp.concatenate(
+        [qb_ref[...].reshape(1, third), jnp.zeros((1, third), bf16), vb_ref[...].reshape(1, third)], axis=1
+    )
+    bias[...] = jnp.broadcast_to(flat.astype(f32), (8, 3 * third))
+    b_far = remote(bias, biases.at[1], sb.at[0], rb.at[0], (d, far_row, 1))
+
+    @pl.when(c == 0)
+    def _():
+        wq_ref[0] = w[...]
+        b_far.start()
+
+    @pl.when(c == 1)
+    def _():
+        w_near.start()
+
+    biases[0] = bias[...]
+    seq[...] = jnp.zeros_like(seq)
+    seq[0:1, 0 : len_ref.shape[1]] = len_ref[...]
+    seq[1:2, 0 : len_ref.shape[1]] = trim_ref[...]
+    seq_cp = remote(seq, seqrx, sm.at[0], rm.at[0], core)
+    seq_cp.start()
 
     core_cp, z_cp, core2_cp = [], [], []
     for k in range(n_dp):
@@ -126,9 +162,20 @@
         b.start()
         z_cp.append(a)
         core_cp.append(b)
+
+    pass_cp = []
+    for k in range(3):
+        share_cp[k].wait_recv()
+        ref = wg_ref.at[lax.rem(r - k + 3, 4), my_share, :]
+        for i, dev in enumerate(ring):
+            cp = remote(ref, ref, sf.at[k, i], rf.at[k, i], dev)
+            cp.start()
+            pass_cp.append(cp)
         if k == 0:
-            for cp in dsends:
-                cp.start()
+            for dest in range(n_dp):
+                pick = (col[dest * piece : (dest + 1) * piece, 0:1] == lane).astype(bf16)
+                dys_ref[dest] = nn(pick, dy_ref[...]).astype(bf16)
+
     for k in range(n_dp):
         s = lax.rem(d - k + n_dp, n_dp)
         z_cp[k].wait_recv()
@@ -136,40 +183,29 @@
         b = remote(ref, ref, sc2.at[k], rc2.at[k], core)
         b.start()
         core2_cp.append(b)
-    for cp in dsends:
-        cp.wait_recv()
-    own = tokens // 2
-    theirs = pl.ds(pl.multiple_of((1 - c) * own, own), own)
-    mine = pl.ds(pl.multiple_of(c * own, own), own)
-    dy_cp = remote(dyin.at[theirs, :], dyb_ref, sm.at[1], rm.at[1], core)
-    dy_cp.start()
-    dya_ref[...] = dyin[mine, :]
-    seq_cp.wait()
-    is_mine = lax.div(r, 2) == c
-    seqo_ref[...] = jnp.where(is_mine, seq_ref[...], seqrx[...])
 
     @pl.when(c == 0)
     def _():
         w_near.wait_recv()
+        b_far.wait_send()
 
     @pl.when(c == 1)
     def _():
         w_near.wait_send()
-        remote(w_ref, wq_ref.at[0], sw.at[0], rw.at[0], (d, far_row, 1)).wait_recv()
-        remote(w_ref, wq_ref.at[1], sw.at[0], rw.at[1], (d, far_row, 1)).wait_recv()
+        b_far.wait_recv()
+        remote(w, wq_ref.at[0], sw.at[0], rw.at[0], (d, far_row, 1)).wait_recv()
+        remote(w, wq_ref.at[1], sw.at[0], rw.at[1], (d, far_row, 1)).wait_recv()
 
     w_far.wait_send()
     for k in range(n_dp):
         core_cp[k].wait_recv()
         core2_cp[k].wait_recv()
-    width = w_ref.shape[0] - 16
-    bias = wq_ref[0, width : width + 1, :].astype(f32)
+    brow = jnp.where(c == 0, biases[0], biases[1])[0:1, :]
 
     def project(i, carry):
         h = lax.div(i, 2)
         base = pl.ds(pl.multiple_of(lax.rem(i, 2) * 512, 512), 512)
-        y = nn(xf_ref[h, 0, base, :], wq_ref[0, :width, :])
-        y = y + nn(xf_ref[h, 1, base, :], wq_ref[1, :width, :]) + bias
+        y = nt(xf_ref[h, 0, base, :], wq_ref[0]) + nt(xf_ref[h, 1, base, :], wq_ref[1]) + brow
         y = y.astype(bf16)
         out = pl.ds(pl.multiple_of(i * 512, 512), 512)
         qkv_ref[out, :] = y
@@ -177,41 +213,54 @@
         return carry
 
     lax.fori_loop(0, 4, project, 0)
-    for cp in sends + dsends + core_cp + z_cp + core2_cp:
+    seq_cp.wait()
+    is_mine = lax.div(r, 2) == c
+    seqo_ref[...] = jnp.where(is_mine, seq[...], seqrx[...])
+    for cp in pass_cp:
+        cp.wait()
+    for cp in sends + core_cp + z_cp + core2_cp + share_cp:
         cp.wait_send()
-    dy_cp.wait()
-
-
-def deal_call(n_dp, x, dy, deal_col, w, seq):
+    local_w.wait()
+
+
+def deal_call(n_dp, rows_w, args):
+    x, qw = args[0], args[3]
     tokens, wide = x.shape
     piece = tokens // n_dp
-    cols = w.shape[1]
+    cols = 3 * qw.shape[0]
     return pl.pallas_call(
-        functools.partial(deal_kernel, n_dp),
+        functools.partial(deal_kernel, n_dp, rows_w),
         out_shape=(
             sds((2, 2, tokens, wide), bf16),
-            sds((tokens // 2, wide), bf16),
-            sds((tokens // 2, wide), bf16),
+            sds((n_dp, piece, wide), bf16),
             sds((2 * tokens, cols), bf16),
             sds((cols, 2 * tokens), bf16),
-            sds((2,) + w.shape, bf16),
-            sds(seq.shape, jnp.int32),
+            sds((2, cols, wide), bf16),
+            sds((8, 128), jnp.int32),
+            sds((4, rows_w, wide), bf16),
         ),
-        in_specs=[VM] * 5,
-        out_specs=(VM,) * 7,
+        in_specs=[VM] * len(args),
+        out_specs=(VM,) * 6 + (ANY,),
         scratch_shapes=[
             pltpu.VMEM((n_dp, piece, wide), bf16),
-            pltpu.VMEM((n_dp, piece, wide), bf16),
-            pltpu.VMEM((tokens, wide), bf16),
-            pltpu.VMEM(seq.shape, jnp.int32),
+            pltpu.VMEM((8, 128), jnp.int32),
+            pltpu.VMEM((8, 128), jnp.int32),
+            pltpu.VMEM((cols, wide), bf16),
+            pltpu.VMEM((8, cols), f32),
+            pltpu.VMEM((2, 8, cols), f32),
+            pltpu.VMEM((rows_w, wide), bf16),
+            pltpu.VMEM((tokens, 8), jnp.int32),
         ]
-        + [DMA((n_dp,))] * 10
-        + [DMA((2,))] * 4,
+        + [DMA((n_dp,))] * 8
+        + [DMA((2,))] * 6
+        + [DMA((3,))] * 2
+        + [DMA((3, n_dp - 1))] * 2
+        + [DMA],
         compiler_params=pltpu.CompilerParams(
             collective_id=1, has_side_effects=True, vmem_limit_bytes=VMEM_LIMIT
         ),
         name="deal",
-    )(x, dy, deal_col, w, seq)
+    )(*args)
 
 
 def seq_bounds(seq_ref, n_seq):
@@ -432,112 +481,85 @@
     return lax.rem(r + 2 * c, 4)
 
 
-def spread_kernel(src_ref, dst_ref, ss, rs):
+def middle_kernel(
+    n_dp, oin_ref, xf_ref, dys_ref, w_ref, res_ref, dh1_ref, dout_ref, *rest
+):
+    g_refs, rest = rest[:n_dp], rest[n_dp:]
+    middle_body(n_dp, oin_ref, xf_ref, dys_ref, w_ref, res_ref, dh1_ref, dout_ref, g_refs, *rest)
+
+
+def middle_body(
+    n_dp, oin_ref, xf_ref, dys_ref, w_ref, res_ref, dh1_ref, dout_ref, g_refs,
+    dyin, dyb, ot_ref, dot_ref, wup, wdn, wo, vec, ub, hid, slope, gbuf, gin, facc, yacc,
+    so, ro, sg, rg, lsem, wss, wrs, sgb, rgb, sgt, rgt, gsem, sd, rd, sm, rm,
+):
     d, r, c = me()
-    half = lax.rem(r, 2)
-    base = r - half
-    n = dst_ref.shape[2]
-    peers = [(d, flip(r), c), (d, flip(r), 1 - c), (d, r, 1 - c)]
-    greet(peers)
-    shard = shard_of(r, c)
-    cps = []
-    for i, dev in enumerate(peers):
-        q = (dev[1] - base) * 2 + dev[2]
-        src = src_ref.at[:, pl.ds(pl.multiple_of(q * n, n), n)]
-        cp = remote(src, dst_ref.at[shard], ss.at[i], rs.at[i], dev)
-        cp.start()
-        cps.append(cp)
-    q = half * 2 + c
-    dst_ref[shard] = src_ref[:, pl.ds(pl.multiple_of(q * n, n), n)]
-    for cp in cps:
-        cp.wait()
-
-
-def spread_call(src):
-    rows, length = src.shape
-    n = length // 4
-    return pl.pallas_call(
-        spread_kernel,
-        out_shape=sds((4, rows, n), bf16),
-        in_specs=[VM],
-        out_specs=VM,
-        scratch_shapes=[DMA((3,)), DMA((3,))],
-        compiler_params=pltpu.CompilerParams(
-            collective_id=2, has_side_effects=True, vmem_limit_bytes=VMEM_LIMIT
-        ),
-        name="spread",
-    )(src)
-
-
-def gather_kernel(src_ref, dst_ref, ss, rs):
-    d, r, c = me()
-    half = lax.rem(r, 2)
-    n = src_ref.shape[2]
-    peers = [(d, flip(r), c), (d, flip(r), 1 - c), (d, r, 1 - c)]
-    greet(peers)
-    q = half * 2 + c
-    mine = pl.ds(pl.multiple_of(q * n, n), n)
-    cps = []
-    for i, dev in enumerate(peers):
-        cp = remote(src_ref.at[shard_of(dev[1], dev[2])], dst_ref.at[:, mine], ss.at[i], rs.at[i], dev)
-        cp.start()
-        cps.append(cp)
-    dst_ref[:, mine] = src_ref[shard_of(r, c)]
-    for cp in cps:
-        cp.wait()
-
-
-def gather_call(src):
-    _, rows, n = src.shape
-    return pl.pallas_call(
-        gather_kernel,
-        out_shape=sds((rows, 4 * n), bf16),
-        in_specs=[VM],
-        out_specs=VM,
-        scratch_shapes=[DMA((3,)), DMA((3,))],
-        compiler_params=pltpu.CompilerParams(
-            collective_id=3, has_side_effects=True, vmem_limit_bytes=VMEM_LIMIT
-        ),
-        name="gather",
-    )(src)
-
-
-UP, DOWN, OUT, VEC = 0, 768, 1536, 1728
-BLOCK_ROWS = 1744
-
-
-def middle_kernel(
-    ot_ref, xf_ref, dya_ref, dyb_ref, w_ref, res_ref, dh1_ref, dot_ref, g_ref,
-    wup, wdn, wo, vec, ub, hid, slope, gbuf, facc, yacc, wsem, gsem,
-):
-    r, c = lax.axis_index("row"), lax.axis_index("col")
     half = lax.rem(r, 2)
     wide = xf_ref.shape[3]
     width = 2 * wide
-    tok = dya_ref.shape[0]
-    loads_a, loads_b, loads_c = [], [], []
+    tok = dyb.shape[0]
+    hrows = oin_ref.shape[0]
+    core = (d, r, 1 - c)
+    peers = [(d, flip(r), c), (d, flip(r), 1 - c), core]
+    ring = [(lax.rem(d + k, n_dp), r, c) for k in range(1, n_dp)]
+    greet(peers + ring)
+    base = r - half
+    shard = shard_of(r, c)
+    o_cp = []
+    for i, dev in enumerate(peers):
+        q = (dev[1] - base) * 2 + dev[2]
+        src = oin_ref.at[:, pl.ds(pl.multiple_of(q * tok, tok), tok)]
+        cp = remote(src, ot_ref.at[shard], so.at[i], ro.at[i], dev)
+        cp.start()
+        o_cp.append(cp)
+    myq = pl.ds(pl.multiple_of((half * 2 + c) * tok, tok), tok)
+    ot_ref[shard] = oin_ref[:, myq]
+
+    piece = dys_ref.shape[1]
+    here = pl.ds(pl.multiple_of(d * piece, piece), piece)
+    d_cp = []
+    for k, dev in enumerate(ring):
+        cp = remote(dys_ref.at[dev[0]], dyin.at[here, :], sd.at[k], rd.at[k], dev)
+        cp.start()
+        d_cp.append(cp)
+    dyin[here, :] = dys_ref[d]
+
+    loads = [[], [], []]
+    mycols = pl.ds(pl.multiple_of(c * wide, 128), wide)
     for j in range(4):
-        for cc in range(2):
-            cs = slice(cc * wide, (cc + 1) * wide)
-            loads_a.append((w_ref.at[j, cc, OUT:VEC], wo.at[j * 192 : (j + 1) * 192, cs], wsem.at[0]))
-            for h in range(2):
-                hs = slice(h * wide, (h + 1) * wide)
-                loads_b.append((w_ref.at[j, cc, hs], wup.at[j, cs, hs], wsem.at[1]))
-            loads_c.append((w_ref.at[j, cc, DOWN:OUT], wdn.at[j, :, cs], wsem.at[2]))
-        loads_a.append((w_ref.at[j, 0, VEC:BLOCK_ROWS], ub.at[j], wsem.at[0]))
-    for cc in range(2):
-        loads_a.append((w_ref.at[0, cc, VEC:BLOCK_ROWS], vec.at[:, cc * wide : (cc + 1) * wide], wsem.at[0]))
-    for group in (loads_a, loads_b, loads_c):
-        for src, dst, sem in group:
-            pltpu.make_async_copy(src, dst, sem).start()
-
-    def settle(group):
-        for src, dst, sem in group:
-            pltpu.make_async_copy(src, dst, sem).wait()
-
+        js = slice(j * hrows, (j + 1) * hrows)
+        loads[0].append((w_ref.at[j, OUT:VEC], wo.at[js, mycols]))
+        loads[0].append((w_ref.at[j, VEC : VEC + 16], ub.at[j, c]))
+        for h in range(2):
+            hs = slice(h * wide, (h + 1) * wide)
+            loads[1].append((w_ref.at[j, hs], wup.at[j, mycols, hs]))
+        loads[2].append((w_ref.at[j, DOWN:OUT], wdn.at[j, :, mycols]))
+    w_cps = []
+    for i, group in enumerate(loads):
+        cps = []
+        for k, (src, dst) in enumerate(group):
+            a = pltpu.make_async_copy(src, dst, lsem.at[i, k])
+            a.start()
+            b = remote(src, dst, wss.at[i, k], wrs.at[i, k], core)
+            b.start()
+            cps += [a, b]
+        w_cps.append(cps)
+
+    def settle(i):
+        for cp in w_cps[i]:
+            cp.wait()
+
+    for cp in o_cp:
+        cp.wait_recv()
+    for cp in d_cp:
+        cp.wait_recv()
+    theirs = pl.ds(pl.multiple_of((1 - c) * tok, tok), tok)
+    dy_cp = remote(dyin.at[theirs, :], dyb, sm, rm, core)
+    dy_cp.start()
     mine = pl.ds(pl.multiple_of(c * tok, tok), tok)
     x = jnp.concatenate([xf_ref[half, 0, mine, :], xf_ref[half, 1, mine, :]], axis=1).astype(f32)
-    settle(loads_a)
+    settle(0)
+    vec[...] = jnp.concatenate([ub[0, 0], ub[0, 1]], axis=1)
     ob, g1, s1, db, g2, s2 = [vec[i : i + 1, :].astype(f32) for i in range(6)]
     o = ot_ref[...].reshape(width, tok).T
     h1 = x + (nn(o, wo[...]) + ob)
@@ -545,12 +567,12 @@
     r1 = lax.rsqrt(jnp.mean(h1 * h1, axis=1, keepdims=True) - mu * mu + EPS)
     n1 = (h1 - mu) * r1
     y1 = (n1 * g1 + s1).astype(bf16)
-    settle(loads_b)
-    settle(loads_c)
+    settle(1)
+    settle(2)
     facc[...] = jnp.zeros_like(facc)
 
     def ahead(j, carry):
-        bias = jnp.concatenate([ub[j, 6:7, :], ub[j, 7:8, :]], axis=1).astype(f32)
+        bias = jnp.concatenate([ub[j, 0, 6:7, :], ub[j, 0, 7:8, :]], axis=1).astype(f32)
         u = nn(y1, wup[j]) + bias
         cdf = 0.5 * (1.0 + lax.erf(u * INV_ROOT_TWO))
         hj = (u * cdf).astype(bf16)
@@ -565,7 +587,8 @@
     r2 = lax.rsqrt(jnp.mean(h2 * h2, axis=1, keepdims=True) - mu2 * mu2 + EPS)
     n2 = (h2 - mu2) * r2
     res_ref[...] = (n2 * g2 + s2).astype(bf16)
-    own, other = dya_ref[...], dyb_ref[...]
+    dy_cp.wait_recv()
+    own, other = dyin[mine, :], dyb[...]
     left = jnp.where(c == 0, own, other)
     right = jnp.where(c == 0, other, own)
     dy = jnp.concatenate([left, right], axis=1).astype(f32)
@@ -578,6 +601,9 @@
     yacc[...] = dh2
     y1t = y1.T
 
+    def big_cp(j):
+        return remote(gbuf.at[j, 1 - c, 0:OUT], gin.at[j, 0:OUT], sgb.at[j], rgb.at[j], core)
+
     def back(j, carry):
         du = (nt(df, wdn[j]) * slope[j]).astype(bf16)
         ubg = jnp.sum(du.astype(f32), axis=0, keepdims=True)
@@ -588,8 +614,11 @@
             for h in range(2):
                 gbuf[j, cc, h * wide : (h + 1) * wide, :] = gu[cs, h * wide : (h + 1) * wide]
             gbuf[j, cc, DOWN:OUT, :] = gd[:, cs]
-        ub[j, 6:7, :] = ubg[:, :wide].astype(bf16)
-        ub[j, 7:8, :] = ubg[:, wide:].astype(bf16)
+        for cc in range(2):
+            gbuf[j, cc, VEC : VEC + 16, :] = jnp.concatenate(
+                [jnp.broadcast_to(ubg[:, :wide], (8, wide)), jnp.broadcast_to(ubg[:, wide:], (8, wide))], axis=0
+            ).astype(bf16)
+        big_cp(j).start()
         yacc[...] += nt(du, wup[j])
         return carry
 
@@ -603,66 +632,108 @@
     da = dh1.astype(bf16)
     obg = jnp.sum(da.astype(f32), axis=0, keepdims=True)
     dot_ref[...] = nt(da, wo[...]).T.astype(bf16).reshape(dot_ref.shape)
+    g_cp = []
+    for i, dev in enumerate(peers):
+        cp = remote(dot_ref.at[shard_of(dev[1], dev[2])], dout_ref.at[:, myq], sg.at[i], rg.at[i], dev)
+        cp.start()
+        g_cp.append(cp)
+    dout_ref[:, myq] = dot_ref[shard]
     go = nn(ot_ref[...].reshape(width, tok), da).astype(bf16)
-    pad = g_ref.shape[2] - VEC
+    pad = gbuf.shape[2] - VEC
     row = lax.broadcasted_iota(jnp.int32, (pad, wide), 0)
+    t_cp = []
     for j in range(4):
         for cc in range(2):
             cs = slice(cc * wide, (cc + 1) * wide)
-            gbuf[j, cc, OUT:VEC, :] = go[j * 192 : (j + 1) * 192, cs]
+            gbuf[j, cc, OUT:VEC, :] = go[j * hrows : (j + 1) * hrows, cs]
             tail = jnp.zeros((pad, wide), f32)
             for i, v in enumerate((obg, g1g, s1g, dbg, g2g, s2g)):
                 tail = jnp.where(row == i, v[:, cs], tail)
-            tail = jnp.where(row == 6, ub[j, 6:7, :].astype(f32), tail)
-            tail = jnp.where(row == 7, ub[j, 7:8, :].astype(f32), tail)
+            tail = jnp.where(row == 6, gbuf[j, cc, VEC : VEC + 16, :][0:1].astype(f32), tail)
+            tail = jnp.where(row == 7, gbuf[j, cc, VEC : VEC + 16, :][8:9].astype(f32), tail)
             gbuf[j, cc, VEC:, :] = tail.astype(bf16)
-    out = pltpu.make_async_copy(gbuf, g_ref, gsem)
-    out.start()
-    out.wait()
-
-
-def middle_call(ot, xf, dya, dyb, w, g_rows):
-    tok, wide = dya.shape
+        cp = remote(gbuf.at[j, 1 - c, OUT:], gin.at[j, OUT:], sgt.at[j], rgt.at[j], core)
+        cp.start()
+        t_cp.append(cp)
+    rows_q = gbuf.shape[2] // n_dp
+    outs = []
+    for j in range(4):
+        big_cp(j).wait()
+        t_cp[j].wait()
+        gin[j] = (gin[j].astype(f32) + gbuf[j, c].astype(f32)).astype(bf16)
+        for k in range(n_dp):
+            dest = lax.rem(d + k, n_dp)
+            span = pl.ds(pl.multiple_of(dest * rows_q, rows_q), rows_q)
+            cp = pltpu.make_async_copy(gin.at[j, span], g_refs[k].at[j], gsem.at[j, k])
+            cp.start()
+            outs.append(cp)
+    for cp in o_cp + d_cp + [dy_cp]:
+        cp.wait_send()
+    for cp in g_cp + outs:
+        cp.wait()
+
+
+def middle_call(n_dp, oin, xf, dys, w, g_rows):
+    tok, wide = xf.shape[2] // 2, xf.shape[3]
     width = 2 * wide
+    hrows = oin.shape[0]
     return pl.pallas_call(
-        middle_kernel,
+        functools.partial(middle_kernel, n_dp),
         out_shape=(
             sds((tok, width), bf16),
             sds((tok, width), f32),
-            sds((4, width // 4, tok), bf16),
-            sds((4, 2, g_rows, wide), bf16),
-        ),
-        in_specs=[VM] * 4 + [ANY],
-        out_specs=(VM, VM, VM, ANY),
+            sds((hrows, 4 * tok), bf16),
+        )
+        + (sds((4, g_rows // n_dp, wide), bf16),) * n_dp,
+        in_specs=[VM] * 3 + [ANY],
+        out_specs=(VM, VM, VM) + (ANY,) * n_dp,
         scratch_shapes=[
+            pltpu.VMEM((2 * tok, wide), bf16),
+            pltpu.VMEM((tok, wide), bf16),
+            pltpu.VMEM((4, hrows, tok), bf16),
+            pltpu.VMEM((4, hrows, tok), bf16),
             pltpu.VMEM((4, width, width), bf16),
             pltpu.VMEM((4, width, width), bf16),
             pltpu.VMEM((width, width), bf16),
             pltpu.VMEM((16, width), bf16),
-            pltpu.VMEM((4, 16, wide), bf16),
+            pltpu.VMEM((4, 2, 16, wide), bf16),
             pltpu.VMEM((4, tok, width), bf16),
             pltpu.VMEM((4, tok, width), f32),
             pltpu.VMEM((4, 2, g_rows, wide), bf16),
+            pltpu.VMEM((4, g_rows, wide), bf16),
             pltpu.VMEM((tok, width), f32),
             pltpu.VMEM((tok, width), f32),
-            DMA((3,)),
-            DMA,
+            DMA((3,)), DMA((3,)), DMA((3,)), DMA((3,)),
+            DMA((3, 8)), DMA((3, 8)), DMA((3, 8)),
+            DMA((4,)), DMA((4,)), DMA((4,)), DMA((4,)),
+            DMA((4, n_dp)), DMA((n_dp,)), DMA((n_dp,)), DMA, DMA,
         ],
-        compiler_params=pltpu.CompilerParams(vmem_limit_bytes=VMEM_LIMIT),
+        compiler_params=pltpu.CompilerParams(
+            collective_id=2, has_side_effects=True, vmem_limit_bytes=VMEM_LIMIT
+        ),
         cost_estimate=pl.CostEstimate(flops=16 * 10**9, bytes_accessed=30 * 10**6, transcendentals=4 * 10**6),
         name="middle",
-    )(ot, xf, dya, dyb, w)
+    )(oin, xf, dys, w)
 
 
 def return_kernel(
-    n_dp, dqkv_ref, dqkvt_ref, wq_ref, xf_ref, dh1_ref, res_ref, deal_ref,
-    out_ref, ig_ref, gq_ref,
-    back_a, back_b, fin, tocore, fromcore, toz, fromz, s_a, r_a, s_b, r_b, s_c, r_c, s_z, r_z,
+    n_dp, dqkv_ref, dqkvt_ref, wq_ref, xf_ref, dh1_ref, res_ref, deal_ref, *rest
+):
+    parts, rest = rest[:n_dp], rest[n_dp:]
+    return_body(n_dp, dqkv_ref, dqkvt_ref, wq_ref, xf_ref, dh1_ref, res_ref, deal_ref, parts, *rest)
+
+
+def return_body(
+    n_dp, dqkv_ref, dqkvt_ref, wq_ref, xf_ref, dh1_ref, res_ref, deal_ref, parts,
+    out_ref, ig_ref, gout_ref, gall_ref,
+    rsum, zin, rfin, s_r, r_r, s_t, r_t,
+    back_a, back_b, fin, tocore, fromcore, toz, fromz, gq_ref, gqin, gsum, xq, gfin,
+    s_a, r_a, s_b, r_b, s_c, r_c, s_z, r_z, s_q, r_q, s_x, r_x, s_g, r_g,
 ):
     d, r, c = me()
     half = lax.rem(r, 2)
     tok = dh1_ref.shape[0]
-    wide = wq_ref.shape[2] if False else xf_ref.shape[3]
+    wide = xf_ref.shape[3]
     width = 2 * wide
     tokens = 2 * tok
     piece = tokens // n_dp
@@ -670,7 +741,19 @@
     core = (d, r, 1 - c)
     zdev = (d, flip(r), c)
     peers = [(lax.rem(d + k, n_dp), r, cc) for k in range(1, n_dp) for cc in (0, 1)]
-    greet(peers + [core, zdev])
+    far_row = lax.rem(r + 2, 4)
+    rows_dev = [(d, lax.rem(r + k, 4), c) for k in (1, 2, 3)]
+    greet(peers + rows_dev + [core, (d, far_row, 1 - c)])
+
+    total = parts[0][...].astype(f32)
+    for k in range(1, n_dp):
+        total = total + parts[k][...].astype(f32)
+    rsum[...] = total.astype(bf16)
+    row_cp = []
+    for k, dev in enumerate(rows_dev):
+        cp = remote(rsum.at[dev[1]], zin.at[k], s_r.at[k], r_r.at[k], dev)
+        cp.start()
+        row_cp.append(cp)
 
     def grp(g):
         return pl.ds(pl.multiple_of(g * piece, piece), piece)
@@ -715,13 +798,13 @@
     fin[0, 1] = res_ref[:, wide:]
     send_back(fin.at[0], back_a, s_a, r_a)
 
-    w0 = wq_ref[0, :wide, :]
-    w1 = wq_ref[1, :wide, :]
+    w0 = wq_ref[0]
+    w1 = wq_ref[1]
 
     def part(h, cc):
         q = h * 2 + cc
         rows = dqkv_ref[pl.ds(pl.multiple_of(q * tok, tok), tok), :]
-        return jnp.concatenate([nt(rows, w0), nt(rows, w1)], axis=1)
+        return jnp.concatenate([nn(rows, w0), nn(rows, w1)], axis=1)
 
     tocore[0] = part(1 - half, 1 - c).astype(bf16)
     cp_far = remote(tocore.at[0], fromcore.at[0], s_c.at[0], r_c.at[0], core)
@@ -748,9 +831,53 @@
     tail = jnp.where(row == 0, bias, 0.0).astype(bf16)
     for f in range(2):
         gq_ref[f, n_cols:, :] = tail
+    rq = gq_ref.shape[1] // n_dp
+
+    def quarter(s):
+        return pl.ds(pl.multiple_of(s * rq, rq), rq)
+
+    q_cp = []
+    for k in range(1, n_dp):
+        dest = lax.rem(d + k, n_dp)
+        cp = remote(gq_ref.at[:, quarter(dest), :], gqin.at[k], s_q.at[k], r_q.at[k], (dest, r, c))
+        cp.start()
+        q_cp.append(cp)
     place = (lax.broadcasted_iota(jnp.int32, (tokens, tokens), 0) == deal_ref[...]).astype(bf16)
     got_back(fin.at[0], back_a, s_a, r_a)
     out_ref[...] = nn(place, back_a[...]).astype(bf16)
+    acc = gq_ref[:, quarter(d), :].astype(f32)
+    for k in range(1, n_dp):
+        q_cp[k - 1].wait_recv()
+        acc = acc + gqin[k].astype(f32)
+    gsum[...] = acc.astype(bf16)
+    to_one = remote(gsum.at[1], xq.at[1], s_x.at[1], r_x.at[1], (d, r, 1))
+    far_0 = remote(gsum.at[0], xq.at[0], s_x.at[0], r_x.at[0], (d, far_row, 0))
+    far_1 = remote(gsum.at[1], xq.at[0], s_x.at[1], r_x.at[0], (d, far_row, 1))
+
+    @pl.when(c == 0)
+    def _():
+        to_one.start()
+
+    @pl.when(c == 1)
+    def _():
+        far_0.start()
+        far_1.start()
+
+    held = rsum[r].astype(f32)
+    for k in range(3):
+        row_cp[k].wait_recv()
+        held = held + zin[k].astype(f32)
+    rfin[...] = held.astype(bf16)
+    n_keep = rfin.shape[0]
+    keep = pl.ds(pl.multiple_of(d * n_keep, n_keep), n_keep)
+    gall_ref[keep, :] = rfin[...]
+    t_cp = []
+    for k in range(1, n_dp):
+        dest = lax.rem(d + k, n_dp)
+        cp = remote(rfin, gall_ref.at[keep, :], s_t.at[k], r_t.at[k], (dest, r, c))
+        cp.start()
+        t_cp.append(cp)
+
     cp_near.wait_recv()
     total = total + fromcore[1].astype(f32)
     cp_z.wait_recv()
@@ -758,6 +885,24 @@
     fin[1, 0] = total[:, :wide]
     fin[1, 1] = total[:, wide:]
     send_back(fin.at[1], back_b, s_b, r_b)
+    far_0.wait_recv()
+
+    @pl.when(c == 0)
+    def _():
+        gfin[...] = (gsum[0].astype(f32) + xq[0].astype(f32)).astype(bf16)
+
+    @pl.when(c == 1)
+    def _():
+        to_one.wait_recv()
+        gfin[...] = (xq[0].astype(f32) + xq[1].astype(f32)).astype(bf16)
+
+    g_cp = []
+    for k in range(1, n_dp):
+        dest = lax.rem(d + k, n_dp)
+        cp = remote(gfin, gout_ref.at[quarter(d), :], s_g.at[k], r_g.at[k], (dest, r, c))
+        cp.start()
+        g_cp.append(cp)
+    gout_ref[quarter(d), :] = gfin[...]
     got_back(fin.at[1], back_b, s_b, r_b)
     ig_ref[...] = nn(place, back_b[...]).astype(bf16)
     sent_back(fin.at[0], back_a, s_a, r_a)
@@ -765,9 +910,25 @@
     cp_far.wait_send()
     cp_near.wait_send()
     cp_z.wait_send()
-
-
-def return_call(n_dp, dqkv, dqkvt, wq, xf, dh1, res, deal_row, gq_rows):
+    for cp in q_cp:
+        cp.wait_send()
+    for cp in row_cp:
+        cp.wait_send()
+    for cp in g_cp + t_cp:
+        cp.wait()
+
+    @pl.when(c == 0)
+    def _():
+        to_one.wait_send()
+
+    @pl.when(c == 1)
+    def _():
+        far_0.wait_send()
+        far_1.wait_send()
+
+
+def return_call(n_dp, dqkv, dqkvt, wq, xf, dh1, res, deal_row, parts, gq_rows):
+    share = parts[0].shape[1]
     tok, width = dh1.shape
     wide = width // 2
     tokens = 2 * tok
@@ -777,11 +938,16 @@
         out_shape=(
             sds((tokens, wide), bf16),
             sds((tokens, wide), bf16),
-            sds((2, gq_rows, wide), bf16),
+            sds((gq_rows, wide), bf16),
+            sds((n_dp * share, wide), bf16),
         ),
-        in_specs=[VM] * 7,
-        out_specs=(VM,) * 3,
+        in_specs=[VM] * (7 + n_dp),
+        out_specs=(VM,) * 4,
         scratch_shapes=[
+            pltpu.VMEM((4, share, wide), bf16),
+            pltpu.VMEM((3, share, wide), bf16),
+            pltpu.VMEM((share, wide), bf16),
+            DMA((3,)), DMA((3,)), DMA((n_dp,)), DMA((n_dp,)),
             pltpu.VMEM((tokens, wide), bf16),
             pltpu.VMEM((tokens, wide), bf16),
             pltpu.VMEM((2, 2, tok, wide), bf16),
@@ -789,15 +955,21 @@
             pltpu.VMEM((2, tok, width), bf16),
             pltpu.VMEM((tok, width), bf16),
             pltpu.VMEM((tok, width), bf16),
+            pltpu.VMEM((2, gq_rows, wide), bf16),
+            pltpu.VMEM((n_dp, 2, gq_rows // n_dp, wide), bf16),
+            pltpu.VMEM((2, gq_rows // n_dp, wide), bf16),
+            pltpu.VMEM((2, gq_rows // n_dp, wide), bf16),
+            pltpu.VMEM((gq_rows // n_dp, wide), bf16),
             DMA((n_half, 2)), DMA((n_dp,)),
             DMA((n_half, 2)), DMA((n_dp,)),
             DMA((2,)), DMA((2,)), DMA, DMA,
+            DMA((n_dp,)), DMA((n_dp,)), DMA((2,)), DMA((2,)), DMA((n_dp,)), DMA((n_dp,)),
         ],
         compiler_params=pltpu.CompilerParams(
             collective_id=4, has_side_effects=True, vmem_limit_bytes=VMEM_LIMIT
         ),
         name="return",
-    )(dqkv, dqkvt, wq, xf, dh1, res, deal_row)
+    )(dqkv, dqkvt, wq, xf, dh1, res, deal_row, *parts)
 
 
 def round_up(v, m):
@@ -809,45 +981,29 @@
     value_weight, value_bias, out_weight, out_bias, first_gain, first_shift, up_weight, up_bias,
     down_weight, down_bias, second_gain, second_shift,
 ):
-    d, r, c = me()
     wide = inputs.shape[1]
     n_seq = seq_lengths.shape[1]
-    unit = 16 * n_dp // math.gcd(16, n_dp)
     step = 16 * n_dp
-
-    blob = jnp.concatenate(
-        [up_weight[:, :wide], up_weight[:, wide:], down_weight, out_weight]
-        + [v[None, :] for v in (out_bias, first_gain, first_shift, down_bias, second_gain, second_shift)]
-        + [up_bias.reshape(2, wide)],
-        axis=0,
+    third = query_weight.shape[1]
+    rows_w = round_up(VEC + 16, step)
+    xf, dys, qkv, qkvt, wq, seq, wg = deal_call(
+        n_dp, rows_w,
+        (
+            inputs, out_grad, deal, query_weight.T, key_weight.T, value_weight.T, query_bias, value_bias, up_weight,
+            down_weight, out_weight, out_bias, first_gain, first_shift, down_bias, second_gain, second_shift, up_bias,
+            seq_lengths, key_trim,
+        ),
     )
-    rows_w = round_up(BLOCK_ROWS, unit)
-    blob = jnp.pad(blob, ((0, rows_w - blob.shape[0]), (0, 0)))
-    share = lax.dynamic_slice_in_dim(blob, d * (rows_w // n_dp), rows_w // n_dp, 0)
-    gathered = lax.all_gather(share, ("row", "col", "dp"), axis=0, tiled=True)
-    gathered = gathered.reshape(4, 2, rows_w, wide)
-
-    third = query_weight.shape[1]
-    bias_row = jnp.concatenate([query_bias, jnp.zeros((third,), bf16), value_bias])[None, :]
-    wqkv = jnp.concatenate([query_weight, key_weight, value_weight], axis=1)
-    wqkv = jnp.concatenate([wqkv, jnp.pad(bias_row, ((0, 15), (0, 0)))], axis=0)
-    seq = jnp.pad(jnp.concatenate([seq_lengths, key_trim], axis=0), ((0, 6), (0, 128 - n_seq)))
-
-    xf, dya, dyb, qkv, qkvt, wq, seq = deal_call(n_dp, inputs, out_grad, deal.reshape(-1, 1), wqkv, seq)
     ot, lse = attend_call(n_seq, seq, qkv, qkvt)
-    ot_mid = spread_call(ot)
-    g_rows = round_up(VEC + 16, step)
-    res, dh1, dot_mid, grads = middle_call(ot_mid, xf, dya, dyb, gathered, g_rows)
-    dot = gather_call(dot_mid)
+    res, dh1, dot, *grads = middle_call(n_dp, ot, xf, dys, wg, rows_w)
+    parts = [grads[0]]
+    for k in range(1, n_dp):
+        parts.append(lax.ppermute(grads[k], "dp", [(i, (i + k) % n_dp) for i in range(n_dp)]))
     dqkv, dqkvt = attend_back_call(n_seq, seq, qkv, qkvt, dot, ot, lse)
     gq_rows = round_up(3 * third + 16, step)
-    output, input_grad, gq = return_call(n_dp, dqkv, dqkvt, wq, xf, dh1, res, deal, gq_rows)
-
-    mine = lax.psum_scatter(grads.reshape(-1, wide), ("row", "col", "dp"), scatter_dimension=0, tiled=True)
-    mine = lax.all_gather(mine, "dp", axis=0, tiled=True)
-    placed = jnp.where((jnp.arange(4) == shard_of(r, c))[:, None, None, None], gq[None], 0).astype(bf16)
-    mine_q = lax.psum_scatter(placed.reshape(-1, wide), ("row", "col", "dp"), scatter_dimension=0, tiled=True)
-    mine_q = lax.all_gather(mine_q, "dp", axis=0, tiled=True)
+    output, input_grad, mine_q, mine = return_call(
+        n_dp, dqkv, dqkvt, wq, xf, dh1, res, deal, parts, gq_rows
+    )
 
     g = mine.astype(f32)
     up_grad = jnp.concatenate([g[:wide], g[wide : 2 * wide]], axis=1)

time: 499 us -> 322 us (0.65)
  waiting for transfers between devices: 176 us -> 25.7 us
  local copies, waits for them, and re-layouts: 33.2 us -> 10.5 us
  Pallas kernels: 254 us -> 275 us
  between operations: 14 us -> 0.73 us
  blocking collectives: 10.6 us -> 0 us
    reduce_scatter x2 -> x0, waiting for transfers between devices: 157 us -> none  [the longest x1 109 us: on_device(): lax.psum_scatter(placed.reshape(-1, wide), ('row', 'col', 'dp'), scatter_...]
    ppermute x0 -> x3, waiting for transfers between devices: none -> 25.7 us  [on_device(): lax.ppermute(grads[k], 'dp', [(i, (i + k) % n_dp) for i in range(n_dp)])]
    all_gather x2 -> x0, waiting for transfers between devices: 18.8 us -> none  [the longest x1 18.8 us: on_device(): mine = lax.all_gather(mine, 'dp', axis=0, tiled=True)]
    reshape x3 -> x0, local copies, waits for them, and re-layouts: 15.4 us -> none  [the longest x1 13.7 us: on_device(): gathered = gathered.reshape(4, 2, rows_w, wide)]
    pallas_call x4 -> x2, Pallas kernels: 125 us -> 138 us  [the longest x1 80.5 us: deal_call(): pl.pallas_call(functools.partial(deal_kernel, n_dp, rows_w), out_shape=(s...]
    all_gather x1 -> x0, blocking collectives: 10.6 us -> none  [on_device(): mine_q = lax.all_gather(mine_q, 'dp', axis=0, tiled=True)]
  transfers between devices with their start and end apart: 4 -> 3, of which waited for: 3 -> 1; matrix products, arithmetic and copies ran while one was open for 2% -> 0% of each run, Pallas kernels for 44% -> 11%
where the time goes in v2:
time: 322 us; the launch traced here: 320 us
  Pallas kernels  275 us (85%)
  waiting for transfers between devices  25.7 us (8%)
  local copies, waits for them, and re-layouts  10.5 us (3%)
  other arithmetic  3.93 us (1%)
  starting transfers between devices  3.76 us (1%)
    pallas_call x1, Pallas kernels, deal_call(): pl.pallas_call(functools.partial(deal_kernel, n_dp, rows_w), out_shape=(s...  80.5 us
    pallas_call x1, Pallas kernels, return_call(): pl.pallas_call(functools.partial(return_kernel, n_dp), out_shape=(sds((to...  72.1 us
    pallas_call x1, Pallas kernels, middle_call(): pl.pallas_call(functools.partial(middle_kernel, n_dp), out_shape=(sds((to...  57.9 us
    pallas_call x1, Pallas kernels, attend_back_call(): pl.pallas_call(functools.partial(attend_back_kernel, n_seq, block), out_s...  34.7 us
    pallas_call x1, Pallas kernels, attend_call(): pl.pallas_call(functools.partial(attend_kernel, n_seq, block), out_shape=...  30 us
    ppermute x3, waiting for transfers between devices, on_device(): lax.ppermute(grads[k], 'dp', [(i, (i + k) % n_dp) for i in range(n_dp)])  25.7 us
  transfers between devices with their start and end apart: 3, of which 1 were waited for; matrix products, arithmetic and copies ran while one was open for 0% of the time, Pallas kernels for 11%

profile of v2, /device:TPU:30, one launch (start us, length us, event | category | flops | bytes accessed | tf_op | source)
XLA Modules:
  0.0 319.8 jit_solution(6679677950347540971)
XLA Ops:
  0.7 80.5 %deal.1 = (bf16[2,2,1024,384]{3,2,1,0:T(8,128)(2,1)}, bf16[4,256,384]{2,1,0:T(8,128)(2,1)}, bf16[2048,576]{1,0:T(8,128)(2,1)}, bf16[576,2048]{1,0:T(8,128)(2,1)}...) custom-call(bf16[1024,384]{1,0:T(8,128)(2,1)} %x_ref.1, bf16[1024,384]{1,0:T(8,128)(2,1)} %dy_ref.1, ...), custom_call_target="tpu_custom_call" | custom-call | tf_op jit(solution)/shard_map/deal/pallas_call | solution.py:231
  81.2 30.0 %attend.1 = (bf16[192,2048]{1,0:T(8,128)(2,1)}, f32[8,2048]{1,0:T(8,128)}) custom-call(s32[8,128]{1,0:T(8,128)} %get-tuple-element.39.seq_ref, bf16[2048,576]{1,0:T(8,128)(2,1)} %get-tuple-element.40.qkv_ref, bf16[576,2048]{1,0:T(8,128)(2,1)} %get-tuple-element.41.qkvt_ref), custom_call_target="tpu_custom_call" | custom-call | flops 4000000000 | bytes 6000000 | tf_op jit(solution)/shard_map/attend/pallas_call | solution.py:369
  111.2 57.9 %middle.1 = (bf16[512,768]{1,0:T(8,128)(2,1)}, f32[512,768]{1,0:T(8,128)}, bf16[192,2048]{1,0:T(8,128)(2,1)}, bf16[4,448,384]{2,1,0:T(8,128)(2,1)}, bf16[4,448,3...) custom-call(bf16[192,2048]{1,0:T(8,128)(2,1)} %get-tuple-element.42.oin_ref.ot_ref, ...), custom_call_target="tpu_custom_call" | custom-call | flops 16000000000 | bytes 30000000 | tf_op jit(solution)/shard_map/middle/pallas_call | solution.py:680
  169.1 1.5 collective-permute-start
  170.6 0.6 collective-permute-start.1
  171.2 1.7 collective-permute-start.2
  172.8 34.7 %attend_back.1 = (bf16[2048,576]{1,0:T(8,128)(2,1)}, bf16[576,2048]{1,0:T(8,128)(2,1)}) custom-call(s32[8,128]{1,0:T(8,128)} %get-tuple-element.39.seq_ref, bf16[2048,576]{1,0:T(8,128)(2,1)} %get-tuple-element.40.qkv_ref, bf16[576,2048]{1,0:T(8,128)(2,1)} %get-tuple-element.41.qkvt_ref, bf16[192,2048]{1,0:T(8,128)(2,1)} %get-tuple-element.46.dot_ref, ...), custom_call_target="tpu_custom_call" | custom-call | flops 10000000000 | bytes 12000000 | tf_op jit(solution)/shard_map/attend_back/pallas_call | solution.py:461
  207.5 0.0 collective-permute-done.rest_1_
  207.6 0.0 copy-start.1
  207.6 25.6 %collective-permute-done.1.rest_2_ = bf16[4,448,384]{2,1,0:T(8,128)(2,1)} collective-permute-done((bf16[4,448,384]{2,1,0:T(8,128)(2,1)}, bf16[4,448,384]{2,1,0:T(8,128)(2,1)}, u32[]{:S(2)}, u32[]{:S(2)}) %collective-permute-start.1) | collective-permute-done | bytes 1376288 | tf_op jit(solution)/shard_map/ppermute | solution.py:1001
  233.2 0.0 collective-permute-done.2.rest_3_
  233.2 0.0 copy-done.1
  233.2 72.1 %return.1 = (bf16[1024,384]{1,0:T(8,128)(2,1)}, bf16[1024,384]{1,0:T(8,128)(2,1)}, bf16[640,384]{1,0:T(8,128)(2,1)}, bf16[1792,384]{1,0:T(8,128)(2,1)}) custom-call(bf16[2048,576]{1,0:T(8,128)(2,1)} %get-tuple-element.48.dqkv_ref, bf16[576,2048]{1,0:T(8,128)(2,1)} %get-tuple-element.49.dqkvt_ref, bf16[2,576,384]{2,1,0:T(8,128)(2,1)} %get-tuple-element.50.wq_ref, ...), custom_call_target="tpu_custom_call" | custom-call | tf_op jit(solution)/shard_map/return/pallas_call | solution.py:936
  305.3 0.0 copy-start
  305.3 0.8 slice.94
  306.1 1.6 slice.88
  307.8 1.4 fusion.1
  309.2 1.1 convert_element_type.6
  310.3 0.0 copy-done
  310.3 1.1 slice.95
  311.4 0.1 fusion
  311.5 1.7 convert_element_type.7
  313.2 0.6 reshape.39
  313.8 0.9 slice_bitcast_fusion
  314.7 0.0 copy-start.3
  314.7 1.7 slice_reduce_fusion
  316.4 1.1 pad_maximum_fusion
  317.5 0.0 copy-start.2
  317.5 0.0 copy-done.3
  317.5 0.9 copy.39
  318.4 0.5 copy-done.2
  318.9 0.9 copy.40
Async XLA Ops:
  169.1 38.5 %collective-permute-start = (bf16[4,448,384]{2,1,0:T(8,128)(2,1)}, bf16[4,448,384]{2,1,0:T(8,128)(2,1)S(1)}, u32[]{:S(2)}, u32[]{:S(2)}) collective-permute-start(bf16[4,448,384]{2,1,0:T(8,128)(2,1)} %get-tuple-element.54), channel_id=1, source_target_pairs={{0,8},{8,16},{16,24},{24,0},{1,9},{9,17},{17,25},{25,1},{2,10},{10... | collective-permute-start | bytes 4128776 | tf_op jit(solution)/shard_map/ppermute | solution.py:1001
  170.6 62.6 %collective-permute-start.1 = (bf16[4,448,384]{2,1,0:T(8,128)(2,1)}, bf16[4,448,384]{2,1,0:T(8,128)(2,1)}, u32[]{:S(2)}, u32[]{:S(2)}) collective-permute-start(bf16[4,448,384]{2,1,0:T(8,128)(2,1)} %get-tuple-element.55), channel_id=1, source_target_pairs={{0,16},{8,24},{16,0},{24,8},{1,17},{9,25},{17,1},{25,9},{2,18},{10... | collective-permute-start | bytes 4128776 | tf_op jit(solution)/shard_map/ppermute | solution.py:1001
  171.2 62.0 %collective-permute-start.2 = (bf16[4,448,384]{2,1,0:T(8,128)(2,1)}, bf16[4,448,384]{2,1,0:T(8,128)(2,1)}, u32[]{:S(2)}, u32[]{:S(2)}) collective-permute-start(bf16[4,448,384]{2,1,0:T(8,128)(2,1)} %get-tuple-element.56), channel_id=1, source_target_pairs={{0,24},{8,0},{16,8},{24,16},{1,25},{9,1},{17,9},{25,17},{2,26},{10... | collective-permute-start | bytes 4128776 | tf_op jit(solution)/shard_map/ppermute | solution.py:1001
  207.6 25.7 %copy-start.1 = (bf16[4,448,384]{2,1,0:T(8,128)(2,1)}, bf16[4,448,384]{2,1,0:T(8,128)(2,1)S(1)}, u32[]{:S(2)}) copy-start(bf16[4,448,384]{2,1,0:T(8,128)(2,1)S(1)} %collective-permute-done.rest_1_) | copy-start | bytes 4128772
  305.3 4.9 %copy-start = (bf16[1792,384]{1,0:T(8,128)(2,1)S(1)}, bf16[1792,384]{1,0:T(8,128)(2,1)}, u32[]{:S(2)}) copy-start(bf16[1792,384]{1,0:T(8,128)(2,1)} %get-tuple-element.60) | copy-start | bytes 4128772
  314.7 2.8 copy-start.3
  317.5 1.4 copy-start.2

commit v3 on v2

--- a/solution.py
+++ b/solution.py
@@ -62,10 +62,59 @@
     pl.semaphore_wait(barrier, len(devs))
 
 
+def send_back(n_dp, src, back, ss, rs):
+    d, r, c = me()
+    n_half = n_dp // 2
+    piece = back.shape[0] // n_dp
+    here = pl.ds(pl.multiple_of(d * piece, piece), piece)
+    for i in range(n_half):
+        s = c * n_half + i
+        for cc in range(2):
+            ref = src.at[cc, i * piece : (i + 1) * piece, :]
+            cp = remote(ref, back.at[here, :], ss.at[i, cc], rs.at[d], (s, r, cc))
+            local = (s == d) & (c == cc)
+
+            @pl.when(jnp.logical_not(local))
+            def _():
+                cp.start()
+
+            @pl.when(local)
+            def _():
+                back[here, :] = src[cc, i * piece : (i + 1) * piece, :]
+
+
+def sent_back(n_dp, src, back, ss, rs):
+    d, r, c = me()
+    n_half = n_dp // 2
+    piece = back.shape[0] // n_dp
+    for i in range(n_half):
+        s = c * n_half + i
+        for cc in range(2):
+            ref = src.at[cc, i * piece : (i + 1) * piece, :]
+
+            @pl.when(jnp.logical_not((s == d) & (c == cc)))
+            def _():
+                remote(ref, back.at[0:piece, :], ss.at[i, cc], rs.at[0], (s, r, cc)).wait_send()
+
+
+def got_back(n_dp, src, back, ss, rs):
+    d, r, c = me()
+    holder = lax.div(d, n_dp // 2)
+    piece = back.shape[0] // n_dp
+    for g in range(n_dp):
+
+        @pl.when(jnp.logical_not((d == g) & (holder == c)))
+        def _():
+            remote(
+                src.at[0, 0:piece, :], back.at[g * piece : (g + 1) * piece, :], ss.at[0, 0], rs.at[g], (d, r, 1 - c)
+            ).wait_recv()
+
+
 def deal_kernel(
     n_dp, rows_w, x_ref, dy_ref, deal_ref, qw_ref, kw_ref, vw_ref, qb_ref, vb_ref, up_ref, dn_ref, ow_ref,
     ob_ref, g1_ref, s1_ref, db_ref, g2_ref, s2_ref, ub_ref, len_ref, trim_ref,
-    xf_ref, dys_ref, qkv_ref, qkvt_ref, wq_ref, seqo_ref, wg_ref,
+    xf_out, dys_out, qkv_out, qkvt_out, wq_out, seqo_ref, wg_ref,
+    xf_ref, dys_ref, qkv_ref, qkvt_ref, wq_ref, so,
     xs, seq, seqrx, w, bias, biases, blob, col,
     sx, rx, sc, rc, sz, rz, sc2, rc2, sw, rw, sb, rb, sm, rm, ss, rs, sf, rf, sl,
 ):
@@ -200,6 +249,13 @@
     for k in range(n_dp):
         core_cp[k].wait_recv()
         core2_cp[k].wait_recv()
+    stores = [
+        pltpu.make_async_copy(xf_ref, xf_out, so.at[0]),
+        pltpu.make_async_copy(wq_ref, wq_out, so.at[1]),
+        pltpu.make_async_copy(dys_ref, dys_out, so.at[2]),
+    ]
+    for cp in stores:
+        cp.start()
     brow = jnp.where(c == 0, biases[0], biases[1])[0:1, :]
 
     def project(i, carry):
@@ -213,6 +269,9 @@
         return carry
 
     lax.fori_loop(0, 4, project, 0)
+    stores += [pltpu.make_async_copy(qkv_ref, qkv_out, so.at[3]), pltpu.make_async_copy(qkvt_ref, qkvt_out, so.at[4])]
+    stores[3].start()
+    stores[4].start()
     seq_cp.wait()
     is_mine = lax.div(r, 2) == c
     seqo_ref[...] = jnp.where(is_mine, seq[...], seqrx[...])
@@ -220,6 +279,8 @@
         cp.wait()
     for cp in sends + core_cp + z_cp + core2_cp + share_cp:
         cp.wait_send()
+    for cp in stores:
+        cp.wait()
     local_w.wait()
 
 
@@ -240,8 +301,14 @@
             sds((4, rows_w, wide), bf16),
         ),
         in_specs=[VM] * len(args),
-        out_specs=(VM,) * 6 + (ANY,),
+        out_specs=(ANY,) * 5 + (VM, ANY),
         scratch_shapes=[
+            pltpu.VMEM((2, 2, tokens, wide), bf16),
+            pltpu.VMEM((n_dp, piece, wide), bf16),
+            pltpu.VMEM((2 * tokens, cols), bf16),
+            pltpu.VMEM((cols, 2 * tokens), bf16),
+            pltpu.VMEM((2, cols, wide), bf16),
+            DMA((5,)),
             pltpu.VMEM((n_dp, piece, wide), bf16),
             pltpu.VMEM((8, 128), jnp.int32),
             pltpu.VMEM((8, 128), jnp.int32),
@@ -320,43 +387,62 @@
     length = qkv_ref.shape[0]
     heads = qkv_ref.shape[1] // (3 * HEAD)
     width = heads * HEAD
+    span = 2 * block
     starts, ends, lives = seq_bounds(seq_ref, n_seq)
-    kcols = key_columns(starts, ends, lives, length, 0)
-    qrows = query_rows(starts, ends, length).astype(bf16)
+    kcols = key_columns(starts, ends, lives, length, 3)
+    qrows = query_rows(starts, ends, length)
     ones = (lax.broadcasted_iota(jnp.int32, (16, length), 0) == 0).astype(f32).astype(bf16)
+    lane = lax.broadcasted_iota(jnp.int32, (block, 2 * HEAD), 1)
+    dead = jnp.where((lane >= HEAD) & (lane < HEAD + n_seq), FAR, 0.0).astype(bf16)
     for h in range(heads):
-        kaug[h, :, :HEAD] = qkv_ref[:, width + h * HEAD : width + (h + 1) * HEAD]
-        kaug[h, :, HEAD:] = kcols
+        kaug[h, :length, :HEAD] = qkv_ref[:, width + h * HEAD : width + (h + 1) * HEAD]
+        kaug[h, :length, HEAD:] = kcols
+        kaug[h, length:, :] = dead
         qaug[h, :HEAD, :] = qkvt_ref[h * HEAD : (h + 1) * HEAD, :] * 0.125
-        qaug[h, HEAD : HEAD + 16, :] = qrows
+        qaug[h, HEAD : HEAD + 16, :] = qrows.astype(bf16)
         qaug[h, HEAD + 16 :, :] = jnp.zeros((HEAD - 16, length), bf16)
-        vaug[h, :HEAD, :] = qkvt_ref[2 * width + h * HEAD : 2 * width + (h + 1) * HEAD, :]
-        vaug[h, HEAD:, :] = ones
+        vaug[h, :HEAD, :length] = qkvt_ref[2 * width + h * HEAD : 2 * width + (h + 1) * HEAD, :]
+        vaug[h, HEAD:, :length] = ones
+        vaug[h, :, length:] = jnp.zeros((HEAD + 16, block), bf16)
     lse_ref[...] = jnp.zeros_like(lse_ref)
 
     def q_step(qb, carry):
         qs = pl.ds(pl.multiple_of(qb * block, block), block)
         lo, hi = block_range(qb * block, qb * block + block - 1, starts, ends, block)
+        count = lax.div(hi - lo + 1, 2)
         for h in range(heads):
             acc[h] = jnp.zeros((HEAD + 16, block), f32)
             mx[h] = jnp.full((8, block), 2 * FAR, f32)
 
-        def k_step(kb, inner):
-            ks = pl.ds(pl.multiple_of(kb * block, block), block)
+        def max_step(i, inner):
+            ks = pl.ds(pl.multiple_of((lo + 2 * i) * block, block), span)
             for h in range(heads):
                 s = nn(kaug[h, ks, :], qaug[h, :, qs])
-                old = mx[h, 0:1, :]
-                new = jnp.maximum(old, jnp.max(s, axis=0, keepdims=True))
-                p = jnp.exp(s - new).astype(bf16)
-                acc[h] = acc[h] * jnp.exp(old - new) + nn(vaug[h, :, ks], p)
-                mx[h] = jnp.broadcast_to(new, (8, block))
+                mx[h] = jnp.maximum(mx[h], jnp.max(s.reshape(span // 8, 8, block), axis=0))
             return inner
 
-        lax.fori_loop(lo, hi, k_step, 0)
+        lax.fori_loop(0, count, max_step, 0)
+        tops = []
+        for h in range(heads):
+            top = jnp.max(mx[h], axis=0, keepdims=True)
+            rows = put_rows(
+                qaug[h, HEAD : HEAD + 16, qs].astype(f32), [jnp.broadcast_to(v, (16, block)) for v in split_three(top)], n_seq
+            )
+            qaug[h, HEAD : HEAD + 16, qs] = rows.astype(bf16)
+            tops.append(top)
+
+        def sum_step(i, inner):
+            ks = pl.ds(pl.multiple_of((lo + 2 * i) * block, block), span)
+            for h in range(heads):
+                p = jnp.exp(nn(kaug[h, ks, :], qaug[h, :, qs])).astype(bf16)
+                acc[h] = acc[h] + nn(vaug[h, :, ks], p)
+            return inner
+
+        lax.fori_loop(0, count, sum_step, 0)
         for h in range(heads):
             total = acc[h, HEAD : HEAD + 1, :]
             ot_ref[h * HEAD : (h + 1) * HEAD, qs] = (acc[h, :HEAD, :] / total).astype(bf16)
-            lse_ref[h : h + 1, qs] = mx[h, 0:1, :] + jnp.log(total)
+            lse_ref[h : h + 1, qs] = tops[h] + jnp.log(total)
         return carry
 
     lax.fori_loop(0, length // block, q_step, 0)
@@ -372,9 +458,9 @@
         in_specs=[SM, VM, VM],
         out_specs=(VM, VM),
         scratch_shapes=[
-            pltpu.VMEM((heads, length, 2 * HEAD), bf16),
+            pltpu.VMEM((heads, length + block, 2 * HEAD), bf16),
             pltpu.VMEM((heads, 2 * HEAD, length), bf16),
-            pltpu.VMEM((heads, HEAD + 16, length), bf16),
+            pltpu.VMEM((heads, HEAD + 16, length + block), bf16),
             pltpu.VMEM((heads, HEAD + 16, block), f32),
             pltpu.VMEM((heads, 8, block), f32),
         ],
@@ -397,25 +483,32 @@
     vcols = jnp.where(lane < 3, -1.0, 0.0).astype(bf16)
     qrows = query_rows(starts, ends, length)
     zero = jnp.zeros((HEAD - 16, length), bf16)
+    pad = jnp.zeros((2 * HEAD, block), bf16)
+    flat = jnp.zeros((block, HEAD), bf16)
+    span = 2 * block
     for h in range(heads):
         hs = slice(h * HEAD, (h + 1) * HEAD)
         kaug[h, :, :HEAD] = qkv_ref[:, width + h * HEAD : width + (h + 1) * HEAD]
         kaug[h, :, HEAD:] = kcols
         vaug[h, :, :HEAD] = qkv_ref[:, 2 * width + h * HEAD : 2 * width + (h + 1) * HEAD]
         vaug[h, :, HEAD:] = vcols
-        qaug[h, :HEAD, :] = qkvt_ref[hs, :] * 0.125
-        qaug[h, HEAD : HEAD + 16, :] = put_rows(qrows, split_three(lse_ref[h : h + 1, :]), n_seq).astype(bf16)
-        qaug[h, HEAD + 16 :, :] = zero
+        qaug[h, :HEAD, :length] = qkvt_ref[hs, :] * 0.125
+        qaug[h, HEAD : HEAD + 16, :length] = put_rows(qrows, split_three(lse_ref[h : h + 1, :]), n_seq).astype(bf16)
+        qaug[h, HEAD + 16 :, :length] = zero
+        qaug[h, :, length:] = pad
+        doaug[h, :, length:] = pad
+        don[h, length:, :] = flat
+        qn[h, length:, :] = flat
         do = dot_ref[hs, :]
         delta = jnp.sum(do.astype(f32) * ot_ref[hs, :].astype(f32), axis=0, keepdims=True)
-        doaug[h, :HEAD, :] = do
-        doaug[h, HEAD : HEAD + 16, :] = put_rows(
+        doaug[h, :HEAD, :length] = do
+        doaug[h, HEAD : HEAD + 16, :length] = put_rows(
             jnp.zeros((16, length), f32), split_three(delta), 0
         ).astype(bf16)
-        doaug[h, HEAD + 16 :, :] = zero
-        qn[h] = qkv_ref[:, hs] * 0.125
-        don[h] = do.T
-        dqt[h] = jnp.zeros((HEAD, length), f32)
+        doaug[h, HEAD + 16 :, :length] = zero
+        qn[h, :length, :] = qkv_ref[:, hs] * 0.125
+        don[h, :length, :] = do.T
+        dqt[h] = jnp.zeros((HEAD, length + block), f32)
 
     def k_step(kb, carry):
         ks = pl.ds(pl.multiple_of(kb * block, block), block)
@@ -423,8 +516,8 @@
         dk[...] = jnp.zeros_like(dk)
         dv[...] = jnp.zeros_like(dv)
 
-        def q_step(qb, inner):
-            qs = pl.ds(pl.multiple_of(qb * block, block), block)
+        def q_step(i, inner):
+            qs = pl.ds(pl.multiple_of((lo + 2 * i) * block, block), span)
             for h in range(heads):
                 p = jnp.exp(nn(kaug[h, ks, :], qaug[h, :, qs]))
                 ds = (p * nn(vaug[h, ks, :], doaug[h, :, qs])).astype(bf16)
@@ -434,7 +527,7 @@
                 dqt[h, :, qs] = dqt[h, :, qs] + nn(kt, ds)
             return inner
 
-        lax.fori_loop(lo, hi, q_step, 0)
+        lax.fori_loop(0, lax.div(hi - lo + 1, 2), q_step, 0)
         for h in range(heads):
             vk = dk[h].astype(bf16)
             vv = dv[h].astype(bf16)
@@ -447,7 +540,7 @@
 
     lax.fori_loop(0, length // block, k_step, 0)
     for h in range(heads):
-        v = (dqt[h] * 0.125).astype(bf16)
+        v = (dqt[h, :, :length] * 0.125).astype(bf16)
         dqkvt_ref[h * HEAD : (h + 1) * HEAD, :] = v
         dqkv_ref[:, h * HEAD : (h + 1) * HEAD] = v.T
 
@@ -457,7 +550,7 @@
     heads = cols // (3 * HEAD)
     block = 256
     nat = pltpu.VMEM((heads, length, 2 * HEAD), bf16)
-    tra = pltpu.VMEM((heads, 2 * HEAD, length), bf16)
+    tra = pltpu.VMEM((heads, 2 * HEAD, length + block), bf16)
     return pl.pallas_call(
         functools.partial(attend_back_kernel, n_seq, block),
         out_shape=(sds((length, cols), bf16), sds((cols, length), bf16)),
@@ -465,9 +558,9 @@
         out_specs=(VM, VM),
         scratch_shapes=[
             nat, tra, nat, tra,
-            pltpu.VMEM((heads, length, HEAD), bf16),
-            pltpu.VMEM((heads, length, HEAD), bf16),
-            pltpu.VMEM((heads, HEAD, length), f32),
+            pltpu.VMEM((heads, length + block, HEAD), bf16),
+            pltpu.VMEM((heads, length + block, HEAD), bf16),
+            pltpu.VMEM((heads, HEAD, length + block), f32),
             pltpu.VMEM((heads, block, HEAD), f32),
             pltpu.VMEM((heads, block, HEAD), f32),
         ],
@@ -477,32 +570,41 @@
     )(seq, qkv, qkvt, dot, ot, lse)
 
 
+def levels(n_dp):
+    n_in = 2 if n_dp < 16 else 4
+    return n_in, n_dp // n_in
+
+
 def shard_of(r, c):
     return lax.rem(r + 2 * c, 4)
 
 
 def middle_kernel(
-    n_dp, oin_ref, xf_ref, dys_ref, w_ref, res_ref, dh1_ref, dout_ref, *rest
+    n_dp, oin_ref, xf_any, dys_ref, w_ref, back_ref, dh1_ref, dout_ref, *rest
 ):
-    g_refs, rest = rest[:n_dp], rest[n_dp:]
-    middle_body(n_dp, oin_ref, xf_ref, dys_ref, w_ref, res_ref, dh1_ref, dout_ref, g_refs, *rest)
+    n_in, n_out = levels(n_dp)
+    a_refs, b_refs, rest = rest[:n_in], rest[n_in : n_in + n_out], rest[n_in + n_out :]
+    middle_body(n_dp, oin_ref, xf_any, dys_ref, w_ref, back_ref, dh1_ref, dout_ref, a_refs, b_refs, *rest)
 
 
 def middle_body(
-    n_dp, oin_ref, xf_ref, dys_ref, w_ref, res_ref, dh1_ref, dout_ref, g_refs,
-    dyin, dyb, ot_ref, dot_ref, wup, wdn, wo, vec, ub, hid, slope, gbuf, gin, facc, yacc,
+    n_dp, oin_ref, xf_any, dys_ref, w_ref, back_ref, dh1_ref, dout_ref, a_refs, b_refs,
+    xv, xsem, fin, s_a, r_a, dyin, dyb, ot_ref, dot_ref, wup, wdn, wo, vec, ub, hid, slope, gbuf, gin, facc, yacc,
     so, ro, sg, rg, lsem, wss, wrs, sgb, rgb, sgt, rgt, gsem, sd, rd, sm, rm,
 ):
     d, r, c = me()
     half = lax.rem(r, 2)
-    wide = xf_ref.shape[3]
+    wide = xf_any.shape[3]
     width = 2 * wide
     tok = dyb.shape[0]
+    mine = pl.ds(pl.multiple_of(c * tok, tok), tok)
+    x_cp = pltpu.make_async_copy(xf_any.at[half, :, mine, :], xv, xsem)
+    x_cp.start()
     hrows = oin_ref.shape[0]
     core = (d, r, 1 - c)
     peers = [(d, flip(r), c), (d, flip(r), 1 - c), core]
     ring = [(lax.rem(d + k, n_dp), r, c) for k in range(1, n_dp)]
-    greet(peers + ring)
+    greet(peers + ring + [(dev[0], r, 1 - c) for dev in ring])
     base = r - half
     shard = shard_of(r, c)
     o_cp = []
@@ -556,8 +658,8 @@
     theirs = pl.ds(pl.multiple_of((1 - c) * tok, tok), tok)
     dy_cp = remote(dyin.at[theirs, :], dyb, sm, rm, core)
     dy_cp.start()
-    mine = pl.ds(pl.multiple_of(c * tok, tok), tok)
-    x = jnp.concatenate([xf_ref[half, 0, mine, :], xf_ref[half, 1, mine, :]], axis=1).astype(f32)
+    x_cp.wait()
+    x = jnp.concatenate([xv[0], xv[1]], axis=1).astype(f32)
     settle(0)
     vec[...] = jnp.concatenate([ub[0, 0], ub[0, 1]], axis=1)
     ob, g1, s1, db, g2, s2 = [vec[i : i + 1, :].astype(f32) for i in range(6)]
@@ -586,7 +688,10 @@
     mu2 = jnp.mean(h2, axis=1, keepdims=True)
     r2 = lax.rsqrt(jnp.mean(h2 * h2, axis=1, keepdims=True) - mu2 * mu2 + EPS)
     n2 = (h2 - mu2) * r2
-    res_ref[...] = (n2 * g2 + s2).astype(bf16)
+    res = (n2 * g2 + s2).astype(bf16)
+    fin[0] = res[:, :wide]
+    fin[1] = res[:, wide:]
+    send_back(n_dp, fin, back_ref, s_a, r_a)
     dy_cp.wait_recv()
     own, other = dyin[mine, :], dyb[...]
     left = jnp.where(c == 0, own, other)
@@ -656,17 +761,25 @@
         cp.start()
         t_cp.append(cp)
     rows_q = gbuf.shape[2] // n_dp
+    n_in, n_out = levels(n_dp)
     outs = []
     for j in range(4):
         big_cp(j).wait()
         t_cp[j].wait()
         gin[j] = (gin[j].astype(f32) + gbuf[j, c].astype(f32)).astype(bf16)
-        for k in range(n_dp):
-            dest = lax.rem(d + k, n_dp)
-            span = pl.ds(pl.multiple_of(dest * rows_q, rows_q), rows_q)
-            cp = pltpu.make_async_copy(gin.at[j, span], g_refs[k].at[j], gsem.at[j, k])
-            cp.start()
-            outs.append(cp)
+        n_first, n_second, refs = (n_in, n_out, a_refs) if j < 2 else (n_out, n_in, b_refs)
+        for k in range(n_first):
+            for m in range(n_second):
+                if j < 2:
+                    s = m * n_in + lax.rem(lax.rem(d, n_in) + k, n_in)
+                else:
+                    s = lax.rem(lax.div(d, n_in) + k, n_out) * n_in + m
+                span = pl.ds(pl.multiple_of(s * rows_q, rows_q), rows_q)
+                cp = pltpu.make_async_copy(gin.at[j, span], refs[k].at[m, j % 2], gsem.at[j, k * n_second + m])
+                cp.start()
+                outs.append(cp)
+    got_back(n_dp, fin, back_ref, s_a, r_a)
+    sent_back(n_dp, fin, back_ref, s_a, r_a)
     for cp in o_cp + d_cp + [dy_cp]:
         cp.wait_send()
     for cp in g_cp + outs:
@@ -677,17 +790,23 @@
     tok, wide = xf.shape[2] // 2, xf.shape[3]
     width = 2 * wide
     hrows = oin.shape[0]
+    n_in, n_out = levels(n_dp)
     return pl.pallas_call(
         functools.partial(middle_kernel, n_dp),
         out_shape=(
-            sds((tok, width), bf16),
+            sds((2 * tok, wide), bf16),
             sds((tok, width), f32),
             sds((hrows, 4 * tok), bf16),
         )
-        + (sds((4, g_rows // n_dp, wide), bf16),) * n_dp,
-        in_specs=[VM] * 3 + [ANY],
-        out_specs=(VM, VM, VM) + (ANY,) * n_dp,
+        + (sds((n_out, 2, g_rows // n_dp, wide), bf16),) * n_in
+        + (sds((n_in, 2, g_rows // n_dp, wide), bf16),) * n_out,
+        in_specs=[VM, ANY, VM, ANY],
+        out_specs=(VM, VM, VM) + (ANY,) * (n_in + n_out),
         scratch_shapes=[
+            pltpu.VMEM((2, tok, wide), bf16),
+            DMA,
+            pltpu.VMEM((2, tok, wide), bf16),
+            DMA((n_dp // 2, 2)), DMA((n_dp,)),
             pltpu.VMEM((2 * tok, wide), bf16),
             pltpu.VMEM((tok, wide), bf16),
             pltpu.VMEM((4, hrows, tok), bf16),
@@ -716,112 +835,83 @@
     )(oin, xf, dys, w)
 
 
-def return_kernel(
-    n_dp, dqkv_ref, dqkvt_ref, wq_ref, xf_ref, dh1_ref, res_ref, deal_ref, *rest
-):
-    parts, rest = rest[:n_dp], rest[n_dp:]
-    return_body(n_dp, dqkv_ref, dqkvt_ref, wq_ref, xf_ref, dh1_ref, res_ref, deal_ref, parts, *rest)
+def return_kernel(n_dp, dqkv_ref, dqkvt_ref, wq_any, xf_any, dh1_any, *rest):
+    n_in, n_out = levels(n_dp)
+    a_parts, b_parts, rest = rest[:n_in], rest[n_in : n_in + n_out], rest[n_in + n_out :]
+    return_body(n_dp, dqkv_ref, dqkvt_ref, wq_any, xf_any, dh1_any, a_parts, b_parts, *rest)
 
 
 def return_body(
-    n_dp, dqkv_ref, dqkvt_ref, wq_ref, xf_ref, dh1_ref, res_ref, deal_ref, parts,
-    out_ref, ig_ref, gout_ref, gall_ref,
-    rsum, zin, rfin, s_r, r_r, s_t, r_t,
-    back_a, back_b, fin, tocore, fromcore, toz, fromz, gq_ref, gqin, gsum, xq, gfin,
-    s_a, r_a, s_b, r_b, s_c, r_c, s_z, r_z, s_q, r_q, s_x, r_x, s_g, r_g,
+    n_dp, dqkv_ref, dqkvt_ref, wq_any, xf_any, dh1_any, a_parts, b_parts,
+    back_ref, gout_ref, gall_ref,
+    wq, xf, dh1, apart, bpart, lsem,
+    asum, bsum, ain, bin_, rsum, zin, rfin, fin, tocore, fromcore, toz, fromz, gq_ref, gqin, gsum, xq, gfin,
+    s_1, r_1, s_2, r_2, s_r, r_r, s_t, r_t, s_b, r_b, s_c, r_c, s_z, r_z, s_q, r_q, s_x, r_x, s_g, r_g,
 ):
     d, r, c = me()
+    n_in, n_out = levels(n_dp)
+    o, i = lax.div(d, n_in), lax.rem(d, n_in)
     half = lax.rem(r, 2)
-    tok = dh1_ref.shape[0]
-    wide = xf_ref.shape[3]
-    width = 2 * wide
-    tokens = 2 * tok
-    piece = tokens // n_dp
-    n_half = n_dp // 2
+    tok, width = dh1_any.shape
+    wide = width // 2
     core = (d, r, 1 - c)
     zdev = (d, flip(r), c)
-    peers = [(lax.rem(d + k, n_dp), r, cc) for k in range(1, n_dp) for cc in (0, 1)]
     far_row = lax.rem(r + 2, 4)
     rows_dev = [(d, lax.rem(r + k, 4), c) for k in (1, 2, 3)]
+    loads = [pltpu.make_async_copy(wq_any, wq, lsem.at[0])]
+    for k in range(n_in):
+        loads.append(pltpu.make_async_copy(a_parts[k], apart.at[k], lsem.at[3 + k]))
+    for k in range(n_out):
+        loads.append(pltpu.make_async_copy(b_parts[k], bpart.at[k], lsem.at[3 + n_in + k]))
+    loads.append(pltpu.make_async_copy(dh1_any, dh1, lsem.at[1]))
+    loads.append(pltpu.make_async_copy(xf_any, xf, lsem.at[2]))
+    for cp in loads:
+        cp.start()
+    peers = [(lax.rem(d + k, n_dp), r, cc) for k in range(1, n_dp) for cc in (0, 1)]
     greet(peers + rows_dev + [core, (d, far_row, 1 - c)])
-
-    total = parts[0][...].astype(f32)
-    for k in range(1, n_dp):
-        total = total + parts[k][...].astype(f32)
-    rsum[...] = total.astype(bf16)
-    row_cp = []
-    for k, dev in enumerate(rows_dev):
-        cp = remote(rsum.at[dev[1]], zin.at[k], s_r.at[k], r_r.at[k], dev)
-        cp.start()
-        row_cp.append(cp)
-
-    def grp(g):
-        return pl.ds(pl.multiple_of(g * piece, piece), piece)
-
-    def send_back(src, back, ss, rs):
-        for i in range(n_half):
-            s = c * n_half + i
-            for cc in range(2):
-                ref = src.at[cc, i * piece : (i + 1) * piece, :]
-                cp = remote(ref, back.at[grp(d), :], ss.at[i, cc], rs.at[d], (s, r, cc))
-                local = (s == d) & (c == cc)
-
-                @pl.when(jnp.logical_not(local))
-                def _():
-                    cp.start()
-
-                @pl.when(local)
-                def _():
-                    back[grp(d), :] = src[cc, i * piece : (i + 1) * piece, :]
-
-    def sent_back(src, back, ss, rs):
-        for i in range(n_half):
-            s = c * n_half + i
-            for cc in range(2):
-                ref = src.at[cc, i * piece : (i + 1) * piece, :]
-
-                @pl.when(jnp.logical_not((s == d) & (c == cc)))
-                def _():
-                    remote(ref, back.at[grp(d), :], ss.at[i, cc], rs.at[d], (s, r, cc)).wait_send()
-
-    def got_back(src, back, ss, rs):
-        holder = lax.div(d, n_half)
-        for g in range(n_dp):
-
-            @pl.when(jnp.logical_not((d == g) & (holder == c)))
-            def _():
-                remote(
-                    src.at[0, 0:piece, :], back.at[grp(g), :], ss.at[0, 0], rs.at[g], (d, r, 1 - c)
-                ).wait_recv()
-
-    fin[0, 0] = res_ref[:, :wide]
-    fin[0, 1] = res_ref[:, wide:]
-    send_back(fin.at[0], back_a, s_a, r_a)
-
-    w0 = wq_ref[0]
-    w1 = wq_ref[1]
 
     def part(h, cc):
         q = h * 2 + cc
         rows = dqkv_ref[pl.ds(pl.multiple_of(q * tok, tok), tok), :]
-        return jnp.concatenate([nn(rows, w0), nn(rows, w1)], axis=1)
-
+        return jnp.concatenate([nn(rows, wq[0]), nn(rows, wq[1])], axis=1)
+
+    loads[0].wait()
     tocore[0] = part(1 - half, 1 - c).astype(bf16)
     cp_far = remote(tocore.at[0], fromcore.at[0], s_c.at[0], r_c.at[0], core)
     cp_far.start()
-    tocore[1] = part(half, 1 - c).astype(bf16)
-    cp_near = remote(tocore.at[1], fromcore.at[1], s_c.at[1], r_c.at[1], core)
-    cp_near.start()
+
+    for cp in loads[1:-2]:
+        cp.wait()
+    total = apart[0].astype(f32)
+    for k in range(1, n_in):
+        total = total + apart[k].astype(f32)
+    asum[...] = total.astype(bf16)
+    total = bpart[0].astype(f32)
+    for k in range(1, n_out):
+        total = total + bpart[k].astype(f32)
+    bsum[...] = total.astype(bf16)
+    a_cp, b_cp = [], []
+    for k in range(1, n_out):
+        dest = lax.rem(o + k, n_out)
+        cp = remote(asum.at[dest], ain.at[k], s_1.at[k], r_1.at[k], (dest * n_in + i, r, c))
+        cp.start()
+        a_cp.append(cp)
+    for k in range(1, n_in):
+        dest = lax.rem(i + k, n_in)
+        cp = remote(bsum.at[dest], bin_.at[k], s_2.at[k], r_2.at[k], (o * n_in + dest, r, c))
+        cp.start()
+        b_cp.append(cp)
+
     far = part(1 - half, c)
     cp_far.wait_recv()
     toz[...] = (far + fromcore[0].astype(f32)).astype(bf16)
     cp_z = remote(toz, fromz, s_z, r_z, zdev)
     cp_z.start()
-    total = part(half, c) + dh1_ref[...]
-    n_cols = dqkvt_ref.shape[0]
-    length = dqkvt_ref.shape[1]
+
+    n_cols, length = dqkvt_ref.shape
+    loads[-1].wait()
     for f in range(2):
-        g = nn(dqkvt_ref[:, : length // 2], xf_ref[0, f]) + nn(dqkvt_ref[:, length // 2 :], xf_ref[1, f])
+        g = nn(dqkvt_ref[:, : length // 2], xf[0, f]) + nn(dqkvt_ref[:, length // 2 :], xf[1, f])
         gq_ref[f, :n_cols, :] = g.astype(bf16)
     third = n_cols // 3
     sums = jnp.sum(dqkv_ref[...].astype(f32), axis=0, keepdims=True)
@@ -842,9 +932,34 @@
         cp = remote(gq_ref.at[:, quarter(dest), :], gqin.at[k], s_q.at[k], r_q.at[k], (dest, r, c))
         cp.start()
         q_cp.append(cp)
-    place = (lax.broadcasted_iota(jnp.int32, (tokens, tokens), 0) == deal_ref[...]).astype(bf16)
-    got_back(fin.at[0], back_a, s_a, r_a)
-    out_ref[...] = nn(place, back_a[...]).astype(bf16)
+
+    tocore[1] = part(half, 1 - c).astype(bf16)
+    cp_near = remote(tocore.at[1], fromcore.at[1], s_c.at[1], r_c.at[1], core)
+    cp_near.start()
+
+    total = asum[o].astype(f32)
+    for cp in a_cp:
+        cp.wait_recv()
+    for k in range(1, n_out):
+        total = total + ain[k].astype(f32)
+    rsum[0:2] = total.astype(bf16)
+    total = bsum[i].astype(f32)
+    for cp in b_cp:
+        cp.wait_recv()
+    for k in range(1, n_in):
+        total = total + bin_[k].astype(f32)
+    rsum[2:4] = total.astype(bf16)
+    row_cp = []
+    for k, dev in enumerate(rows_dev):
+        cp = remote(rsum.at[dev[1]], zin.at[k], s_r.at[k], r_r.at[k], dev)
+        cp.start()
+        row_cp.append(cp)
+
+    loads[-2].wait()
+    total = part(half, c) + dh1[...]
+    cp_near.wait_recv()
+    total = total + fromcore[1].astype(f32)
+
     acc = gq_ref[:, quarter(d), :].astype(f32)
     for k in range(1, n_dp):
         q_cp[k - 1].wait_recv()
@@ -862,6 +977,12 @@
     def _():
         far_0.start()
         far_1.start()
+
+    cp_z.wait_recv()
+    total = (total + fromz[...].astype(f32)).astype(bf16)
+    fin[0] = total[:, :wide]
+    fin[1] = total[:, wide:]
+    send_back(n_dp, fin, back_ref, s_b, r_b)
 
     held = rsum[r].astype(f32)
     for k in range(3):
@@ -878,13 +999,6 @@
         cp.start()
         t_cp.append(cp)
 
-    cp_near.wait_recv()
-    total = total + fromcore[1].astype(f32)
-    cp_z.wait_recv()
-    total = (total + fromz[...].astype(f32)).astype(bf16)
-    fin[1, 0] = total[:, :wide]
-    fin[1, 1] = total[:, wide:]
-    send_back(fin.at[1], back_b, s_b, r_b)
     far_0.wait_recv()
 
     @pl.when(c == 0)
@@ -896,25 +1010,17 @@
         to_one.wait_recv()
         gfin[...] = (xq[0].astype(f32) + xq[1].astype(f32)).astype(bf16)
 
-    g_cp = []
     for k in range(1, n_dp):
         dest = lax.rem(d + k, n_dp)
         cp = remote(gfin, gout_ref.at[quarter(d), :], s_g.at[k], r_g.at[k], (dest, r, c))
         cp.start()
-        g_cp.append(cp)
+        t_cp.append(cp)
     gout_ref[quarter(d), :] = gfin[...]
-    got_back(fin.at[1], back_b, s_b, r_b)
-    ig_ref[...] = nn(place, back_b[...]).astype(bf16)
-    sent_back(fin.at[0], back_a, s_a, r_a)
-    sent_back(fin.at[1], back_b, s_b, r_b)
-    cp_far.wait_send()
-    cp_near.wait_send()
-    cp_z.wait_send()
-    for cp in q_cp:
+    got_back(n_dp, fin, back_ref, s_b, r_b)
+    sent_back(n_dp, fin, back_ref, s_b, r_b)
+    for cp in [cp_far, cp_near, cp_z] + q_cp + a_cp + b_cp + row_cp:
         cp.wait_send()
-    for cp in row_cp:
-        cp.wait_send()
-    for cp in g_cp + t_cp:
+    for cp in t_cp:
         cp.wait()
 
     @pl.when(c == 0)
@@ -927,41 +1033,32 @@
         far_1.wait_send()
 
 
-def return_call(n_dp, dqkv, dqkvt, wq, xf, dh1, res, deal_row, parts, gq_rows):
-    share = parts[0].shape[1]
+def return_call(n_dp, dqkv, dqkvt, wq, xf, dh1, a_parts, b_parts, gq_rows):
+    n_in, n_out = levels(n_dp)
     tok, width = dh1.shape
     wide = width // 2
+    share = a_parts[0].shape[2]
     tokens = 2 * tok
-    n_half = n_dp // 2
+
+    def vm(*shape):
+        return pltpu.VMEM(shape, bf16)
+
     return pl.pallas_call(
         functools.partial(return_kernel, n_dp),
-        out_shape=(
-            sds((tokens, wide), bf16),
-            sds((tokens, wide), bf16),
-            sds((gq_rows, wide), bf16),
-            sds((n_dp * share, wide), bf16),
-        ),
-        in_specs=[VM] * (7 + n_dp),
-        out_specs=(VM,) * 4,
+        out_shape=(sds((tokens, wide), bf16), sds((gq_rows, wide), bf16), sds((n_dp * share, wide), bf16)),
+        in_specs=[VM, VM] + [ANY] * (3 + n_in + n_out),
+        out_specs=(VM,) * 3,
         scratch_shapes=[
-            pltpu.VMEM((4, share, wide), bf16),
-            pltpu.VMEM((3, share, wide), bf16),
-            pltpu.VMEM((share, wide), bf16),
+            vm(*wq.shape), vm(*xf.shape), pltpu.VMEM(dh1.shape, f32),
+            vm(n_in, n_out, 2, share, wide), vm(n_out, n_in, 2, share, wide), DMA((3 + n_in + n_out,)),
+            vm(n_out, 2, share, wide), vm(n_in, 2, share, wide), vm(n_out, 2, share, wide), vm(n_in, 2, share, wide),
+            vm(4, share, wide), vm(3, share, wide), vm(share, wide),
+            vm(2, tok, wide), vm(2, tok, width), vm(2, tok, width), vm(tok, width), vm(tok, width),
+            vm(2, gq_rows, wide), vm(n_dp, 2, gq_rows // n_dp, wide), vm(2, gq_rows // n_dp, wide),
+            vm(2, gq_rows // n_dp, wide), vm(gq_rows // n_dp, wide),
+            DMA((n_out,)), DMA((n_out,)), DMA((n_in,)), DMA((n_in,)),
             DMA((3,)), DMA((3,)), DMA((n_dp,)), DMA((n_dp,)),
-            pltpu.VMEM((tokens, wide), bf16),
-            pltpu.VMEM((tokens, wide), bf16),
-            pltpu.VMEM((2, 2, tok, wide), bf16),
-            pltpu.VMEM((2, tok, width), bf16),
-            pltpu.VMEM((2, tok, width), bf16),
-            pltpu.VMEM((tok, width), bf16),
-            pltpu.VMEM((tok, width), bf16),
-            pltpu.VMEM((2, gq_rows, wide), bf16),
-            pltpu.VMEM((n_dp, 2, gq_rows // n_dp, wide), bf16),
-            pltpu.VMEM((2, gq_rows // n_dp, wide), bf16),
-            pltpu.VMEM((2, gq_rows // n_dp, wide), bf16),
-            pltpu.VMEM((gq_rows // n_dp, wide), bf16),
-            DMA((n_half, 2)), DMA((n_dp,)),
-            DMA((n_half, 2)), DMA((n_dp,)),
+            DMA((n_dp // 2, 2)), DMA((n_dp,)),
             DMA((2,)), DMA((2,)), DMA, DMA,
             DMA((n_dp,)), DMA((n_dp,)), DMA((2,)), DMA((2,)), DMA((n_dp,)), DMA((n_dp,)),
         ],
@@ -969,7 +1066,53 @@
             collective_id=4, has_side_effects=True, vmem_limit_bytes=VMEM_LIMIT
         ),
         name="return",
-    )(dqkv, dqkvt, wq, xf, dh1, res, deal_row, *parts)
+    )(dqkv, dqkvt, wq, xf, dh1, *a_parts, *b_parts)
+
+
+def finish_kernel(
+    a_ref, b_ref, deal_ref, g_ref, q_ref,
+    out_ref, ig_ref, qw_ref, qb_ref, kw_ref, vw_ref, vb_ref, ow_ref, ob_ref, g1_ref, s1_ref, up_ref, ub_ref, dn_ref,
+    db_ref, g2_ref, s2_ref,
+):
+    tokens, wide = a_ref.shape
+    third = qw_ref.shape[0]
+    place = (lax.broadcasted_iota(jnp.int32, (tokens, tokens), 0) == deal_ref[...]).astype(bf16)
+    out_ref[...] = nn(place, a_ref[...]).astype(bf16)
+    ig_ref[...] = nn(place, b_ref[...]).astype(bf16)
+    qw_ref[...] = q_ref[:third, :].astype(f32)
+    kw_ref[...] = q_ref[third : 2 * third, :].astype(f32)
+    vw_ref[...] = q_ref[2 * third : 3 * third, :].astype(f32)
+    bias = q_ref[3 * third : 3 * third + 16, :].astype(f32)[0:1]
+    qb_ref[...] = bias[0, :third]
+    vb_ref[...] = bias[0, third:]
+    up_ref[:, :wide] = g_ref[:wide, :].astype(f32)
+    up_ref[:, wide:] = g_ref[wide : 2 * wide, :].astype(f32)
+    dn_ref[...] = g_ref[DOWN:OUT, :].astype(f32)
+    ow_ref[...] = g_ref[OUT:VEC, :].astype(f32)
+    vec = g_ref[VEC : VEC + 16, :].astype(f32)
+    for i, ref in enumerate((ob_ref, g1_ref, s1_ref, db_ref, g2_ref, s2_ref)):
+        ref[...] = vec[i]
+    ub_ref[0:wide] = vec[6]
+    ub_ref[wide : 2 * wide] = vec[7]
+
+
+def finish_call(back_a, back_b, deal, gall, gq, third):
+    tokens, wide = back_a.shape
+    one = sds((wide,), f32)
+    row = sds((third,), f32)
+    head = sds((third, wide), f32)
+    tok = sds((tokens, wide), bf16)
+    return pl.pallas_call(
+        finish_kernel,
+        out_shape=(
+            tok, tok, head, row, head, head, row, head, one, one, one, sds((wide, 2 * wide), f32),
+            sds((2 * wide,), f32), sds((2 * wide, wide), f32), one, one, one,
+        ),
+        in_specs=[VM] * 5,
+        out_specs=(VM,) * 17,
+        compiler_params=pltpu.CompilerParams(vmem_limit_bytes=VMEM_LIMIT),
+        name="finish",
+    )(back_a, back_b, deal, gall, gq)
 
 
 def round_up(v, m):
@@ -995,30 +1138,24 @@
         ),
     )
     ot, lse = attend_call(n_seq, seq, qkv, qkvt)
-    res, dh1, dot, *grads = middle_call(n_dp, ot, xf, dys, wg, rows_w)
-    parts = [grads[0]]
-    for k in range(1, n_dp):
-        parts.append(lax.ppermute(grads[k], "dp", [(i, (i + k) % n_dp) for i in range(n_dp)]))
+    back_a, dh1, dot, *grads = middle_call(n_dp, ot, xf, dys, wg, rows_w)
+    n_in, n_out = levels(n_dp)
+    a_parts, b_parts = grads[:n_in], grads[n_in:]
+    for k in range(1, n_in):
+        a_parts[k] = lax.ppermute(
+            a_parts[k], "dp", [(o * n_in + i, o * n_in + (i + k) % n_in) for o in range(n_out) for i in range(n_in)]
+        )
+    for k in range(1, n_out):
+        b_parts[k] = lax.ppermute(
+            b_parts[k], "dp", [(o * n_in + i, (o + k) % n_out * n_in + i) for o in range(n_out) for i in range(n_in)]
+        )
     dqkv, dqkvt = attend_back_call(n_seq, seq, qkv, qkvt, dot, ot, lse)
     gq_rows = round_up(3 * third + 16, step)
-    output, input_grad, mine_q, mine = return_call(
-        n_dp, dqkv, dqkvt, wq, xf, dh1, res, deal, parts, gq_rows
-    )
-
-    g = mine.astype(f32)
-    up_grad = jnp.concatenate([g[:wide], g[wide : 2 * wide]], axis=1)
-    down_grad = g[DOWN:OUT]
-    out_grad_w = g[OUT:VEC]
-    vec = g[VEC : VEC + 8]
-    gqf = mine_q.astype(f32)
-    query_grad = gqf[:third].T
-    key_grad = gqf[third : 2 * third].T
-    value_grad = gqf[2 * third : 3 * third].T
-    brow = gqf[3 * third]
-    return (
-        output, input_grad, query_grad, brow[:third], key_grad, value_grad, brow[third:], out_grad_w,
-        vec[0], vec[1], vec[2], up_grad, vec[6:8].reshape(-1), down_grad, vec[3], vec[4], vec[5],
-    )
+    back_b, gq, gall = return_call(n_dp, dqkv, dqkvt, wq, xf, dh1, a_parts, b_parts, gq_rows)
+    outs = list(finish_call(back_a, back_b, deal, gall, gq, third))
+    for i in (2, 4, 5):
+        outs[i] = outs[i].T
+    return tuple(outs)
 
 
 def solution(mesh):

time: 322 us -> 292 us (0.907)
  waiting for transfers between devices: 25.7 us -> 0.01 us
  Pallas kernels: 275 us -> 285 us
  local copies, waits for them, and re-layouts: 10.5 us -> 1.06 us
  other arithmetic: 3.93 us -> 0 us
    ppermute x3 -> x2, waiting for transfers between devices: 25.7 us -> 0.01 us  [the longest x1 0.01 us: on_device(): lax.ppermute(a_parts[k], 'dp', [(o * n_in + i, o * n_in + (i + k) % n_in)...]
    pallas_call x1, Pallas kernels: 72.1 us -> 81.8 us  [return_call(): pl.pallas_call(functools.partial(return_kernel, n_dp), out_shape=(sds((to...]
    slice x6 -> x0, local copies, waits for them, and re-layouts: 6.66 us -> none  [the longest x1 1.65 us: on_device(): vec[5]]
    pallas_call x1, Pallas kernels: 30 us -> 33.5 us  [attend_call(): pl.pallas_call(functools.partial(attend_kernel, n_seq, block), out_shape=...]
    pallas_call x1 -> x2, Pallas kernels: 57.9 us -> 59.1 us  [the longest x1 52.5 us: middle_call(): pl.pallas_call(functools.partial(middle_kernel, n_dp), out_shape=(sds((2...]
  transfers between devices with their start and end apart: 3 -> 2, of which waited for: 1 -> 0; matrix products, arithmetic and copies ran while one was open for 0% -> 0% of each run, Pallas kernels for 11% -> 12%
where the time goes in v3:
time: 292 us; the launch traced here: 289 us
  Pallas kernels  285 us (98%)
    pallas_call x1, Pallas kernels, return_call(): pl.pallas_call(functools.partial(return_kernel, n_dp), out_shape=(sds((to...  81.8 us
    pallas_call x1, Pallas kernels, deal_call(): pl.pallas_call(functools.partial(deal_kernel, n_dp, rows_w), out_shape=(s...  77.4 us
    pallas_call x1, Pallas kernels, middle_call(): pl.pallas_call(functools.partial(middle_kernel, n_dp), out_shape=(sds((2...  52.5 us
    pallas_call x1, Pallas kernels, attend_call(): pl.pallas_call(functools.partial(attend_kernel, n_seq, block), out_shape=...  33.5 us
    pallas_call x1, Pallas kernels, attend_back_call(): pl.pallas_call(functools.partial(attend_back_kernel, n_seq, block), out_s...  33.5 us
    pallas_call x1, Pallas kernels, finish_call(): pl.pallas_call(finish_kernel, out_shape=(tok, tok, head, row, head, head,...  6.54 us
  transfers between devices with their start and end apart: 2, of which 0 were waited for; matrix products, arithmetic and copies ran while one was open for 0% of the time, Pallas kernels for 12%

profile of v3, /device:TPU:30, one launch (start us, length us, event | category | flops | bytes accessed | tf_op | source)
XLA Modules:
  0.0 289.1 jit_solution(2842466147361656410)
XLA Ops:
  0.7 77.4 %deal.1 = (bf16[2,2,1024,384]{3,2,1,0:T(8,128)(2,1)}, bf16[4,256,384]{2,1,0:T(8,128)(2,1)}, bf16[2048,576]{1,0:T(8,128)(2,1)}, bf16[576,2048]{1,0:T(8,128)(2,1)}...) custom-call(bf16[1024,384]{1,0:T(8,128)(2,1)} %x_ref.1, bf16[1024,384]{1,0:T(8,128)(2,1)} %dy_ref.1, ...), custom_call_target="tpu_custom_call" | custom-call | tf_op jit(solution)/shard_map/deal/pallas_call | solution.py:292
  78.1 33.5 %attend.1 = (bf16[192,2048]{1,0:T(8,128)(2,1)}, f32[8,2048]{1,0:T(8,128)}) custom-call(s32[8,128]{1,0:T(8,128)} %get-tuple-element.55.seq_ref, bf16[2048,576]{1,0:T(8,128)(2,1)} %get-tuple-element.56.qkv_ref, bf16[576,2048]{1,0:T(8,128)(2,1)} %get-tuple-element.57.qkvt_ref), custom_call_target="tpu_custom_call" | custom-call | flops 4000000000 | bytes 6000000 | tf_op jit(solution)/shard_map/attend/pallas_call | solution.py:455
  111.5 52.5 %middle.1 = (bf16[1024,384]{1,0:T(8,128)(2,1)}, f32[512,768]{1,0:T(8,128)}, bf16[192,2048]{1,0:T(8,128)(2,1)}, bf16[2,2,448,384]{3,2,1,0:T(8,128)(2,1)}, bf16[2,...) custom-call(bf16[192,2048]{1,0:T(8,128)(2,1)} %get-tuple-element.58.oin_ref.ot_ref, ...), custom_call_target="tpu_custom_call" | custom-call | flops 16000000000 | bytes 30000000 | tf_op jit(solution)/shard_map/middle/pallas_call | solution.py:794
  164.0 1.5 collective-permute-start
  165.5 0.5 collective-permute-start.1
  166.1 33.5 %attend_back.1 = (bf16[2048,576]{1,0:T(8,128)(2,1)}, bf16[576,2048]{1,0:T(8,128)(2,1)}) custom-call(s32[8,128]{1,0:T(8,128)} %get-tuple-element.55.seq_ref, bf16[2048,576]{1,0:T(8,128)(2,1)} %get-tuple-element.56.qkv_ref, bf16[576,2048]{1,0:T(8,128)(2,1)} %get-tuple-element.57.qkvt_ref, bf16[192,2048]{1,0:T(8,128)(2,1)} %get-tuple-element.63.dot_ref, ...), custom_call_target="tpu_custom_call" | custom-call | flops 10000000000 | bytes 12000000 | tf_op jit(solution)/shard_map/attend_back/pallas_call | solution.py:554
  199.5 0.0 collective-permute-done.rest_1_
  199.5 0.0 copy-start
  199.5 0.0 collective-permute-done.1.rest_3_
  199.5 1.1 copy-done
  200.6 81.8 %return.1 = (bf16[1024,384]{1,0:T(8,128)(2,1)}, bf16[640,384]{1,0:T(8,128)(2,1)}, bf16[1792,384]{1,0:T(8,128)(2,1)}) custom-call(bf16[2048,576]{1,0:T(8,128)(2,1)} %get-tuple-element.65.dqkv_ref, bf16[576,2048]{1,0:T(8,128)(2,1)} %get-tuple-element.66.dqkvt_ref, bf16[2,576,384]{2,1,0:T(8,128)(2,1)} %get-tuple-element.67.wq_any, ...), custom_call_target="tpu_custom_call" | custom-call | tf_op jit(solution)/shard_map/return/pallas_call | solution.py:1046
  282.4 6.5 %finish.1 = (bf16[1024,384]{1,0:T(8,128)(2,1)}, bf16[1024,384]{1,0:T(8,128)(2,1)}, f32[192,384]{1,0:T(8,128)}, f32[192]{0:T(256)}, f32[192,384]{1,0:T(8,128)}, /...) custom-call(bf16[1024,384]{1,0:T(8,128)(2,1)} %get-tuple-element.62., ...), custom_call_target="tpu_custom_call" | custom-call | tf_op jit(solution)/shard_map/finish/pallas_call | solution.py:1105
Async XLA Ops:
  164.0 35.5 %collective-permute-start = (bf16[2,2,448,384]{3,2,1,0:T(8,128)(2,1)}, bf16[2,2,448,384]{3,2,1,0:T(8,128)(2,1)S(1)}, u32[]{:S(2)}, u32[]{:S(2)}) collective-permute-start(bf16[2,2,448,384]{3,2,1,0:T(8,128)(2,1)} %get-tuple-element.70), channel_id=1, source_target_pairs={{0,8},{8,0},{16,24},{24,16},{1,9},{9,1},{17,25},{25,17},{2,10},{10... | collective-permute-start | bytes 4128776 | tf_op jit(solution)/shard_map/ppermute | solution.py:1145
  165.5 34.0 %collective-permute-start.1 = (bf16[2,2,448,384]{3,2,1,0:T(8,128)(2,1)}, bf16[2,2,448,384]{3,2,1,0:T(8,128)(2,1)}, u32[]{:S(2)}, u32[]{:S(2)}) collective-permute-start(bf16[2,2,448,384]{3,2,1,0:T(8,128)(2,1)} %get-tuple-element.72), channel_id=1, source_target_pairs={{0,16},{8,24},{16,0},{24,8},{1,17},{9,25},{17,1},{25,9},{2,18},{10... | collective-permute-start | bytes 4128776 | tf_op jit(solution)/shard_map/ppermute | solution.py:1149
  199.5 1.1 copy-start

commit v4 on v3

--- a/solution.py
+++ b/solution.py
@@ -383,62 +383,59 @@
     return base
 
 
-def attend_kernel(n_seq, block, seq_ref, qkv_ref, qkvt_ref, ot_ref, lse_ref, kaug, qaug, vaug, acc, mx):
+def attend_kernel(n_seq, block, seq_ref, qkv_ref, qkvt_ref, ot_ref, lse_ref, kaug, qaug, vaug, acc, mx, sbuf):
     length = qkv_ref.shape[0]
     heads = qkv_ref.shape[1] // (3 * HEAD)
     width = heads * HEAD
     span = 2 * block
     starts, ends, lives = seq_bounds(seq_ref, n_seq)
-    kcols = key_columns(starts, ends, lives, length, 3)
+    kcols = key_columns(starts, ends, lives, length, 0)
     qrows = query_rows(starts, ends, length)
     ones = (lax.broadcasted_iota(jnp.int32, (16, length), 0) == 0).astype(f32).astype(bf16)
-    lane = lax.broadcasted_iota(jnp.int32, (block, 2 * HEAD), 1)
-    dead = jnp.where((lane >= HEAD) & (lane < HEAD + n_seq), FAR, 0.0).astype(bf16)
     for h in range(heads):
-        kaug[h, :length, :HEAD] = qkv_ref[:, width + h * HEAD : width + (h + 1) * HEAD]
-        kaug[h, :length, HEAD:] = kcols
-        kaug[h, length:, :] = dead
+        kaug[h, :, :HEAD] = qkv_ref[:, width + h * HEAD : width + (h + 1) * HEAD]
+        kaug[h, :, HEAD:] = kcols
         qaug[h, :HEAD, :] = qkvt_ref[h * HEAD : (h + 1) * HEAD, :] * 0.125
         qaug[h, HEAD : HEAD + 16, :] = qrows.astype(bf16)
         qaug[h, HEAD + 16 :, :] = jnp.zeros((HEAD - 16, length), bf16)
-        vaug[h, :HEAD, :length] = qkvt_ref[2 * width + h * HEAD : 2 * width + (h + 1) * HEAD, :]
-        vaug[h, HEAD:, :length] = ones
-        vaug[h, :, length:] = jnp.zeros((HEAD + 16, block), bf16)
+        vaug[h, :HEAD, :] = qkvt_ref[2 * width + h * HEAD : 2 * width + (h + 1) * HEAD, :]
+        vaug[h, HEAD:, :] = ones
     lse_ref[...] = jnp.zeros_like(lse_ref)
 
     def q_step(qb, carry):
         qs = pl.ds(pl.multiple_of(qb * block, block), block)
         lo, hi = block_range(qb * block, qb * block + block - 1, starts, ends, block)
-        count = lax.div(hi - lo + 1, 2)
         for h in range(heads):
             acc[h] = jnp.zeros((HEAD + 16, block), f32)
             mx[h] = jnp.full((8, block), 2 * FAR, f32)
 
-        def max_step(i, inner):
-            ks = pl.ds(pl.multiple_of((lo + 2 * i) * block, block), span)
+        def max_step(size, i, inner):
+            ks = pl.ds(pl.multiple_of((lo + 2 * i) * block, block), size)
+            at = pl.ds(pl.multiple_of(i * span, span), size)
+            ss = [nn(kaug[h, ks, :], qaug[h, :, qs]) for h in range(heads)]
             for h in range(heads):
-                s = nn(kaug[h, ks, :], qaug[h, :, qs])
-                mx[h] = jnp.maximum(mx[h], jnp.max(s.reshape(span // 8, 8, block), axis=0))
+                sbuf[h, at, :] = ss[h]
+                mx[h] = jnp.maximum(mx[h], jnp.max(ss[h].reshape(size // 8, 8, block), axis=0))
             return inner
 
-        lax.fori_loop(0, count, max_step, 0)
+        pairs, odd = lax.div(hi - lo, 2), lax.rem(hi - lo, 2)
+        lax.fori_loop(0, pairs, functools.partial(max_step, span), 0)
+        lax.fori_loop(pairs, pairs + odd, functools.partial(max_step, block), 0)
         tops = []
         for h in range(heads):
             top = jnp.max(mx[h], axis=0, keepdims=True)
-            rows = put_rows(
-                qaug[h, HEAD : HEAD + 16, qs].astype(f32), [jnp.broadcast_to(v, (16, block)) for v in split_three(top)], n_seq
-            )
-            qaug[h, HEAD : HEAD + 16, qs] = rows.astype(bf16)
             tops.append(top)
 
-        def sum_step(i, inner):
-            ks = pl.ds(pl.multiple_of((lo + 2 * i) * block, block), span)
+        def sum_step(size, i, inner):
+            ks = pl.ds(pl.multiple_of((lo + 2 * i) * block, block), size)
+            at = pl.ds(pl.multiple_of(i * span, span), size)
+            ps = [jnp.exp(sbuf[h, at, :] - tops[h]).astype(bf16) for h in range(heads)]
             for h in range(heads):
-                p = jnp.exp(nn(kaug[h, ks, :], qaug[h, :, qs])).astype(bf16)
-                acc[h] = acc[h] + nn(vaug[h, :, ks], p)
+                acc[h] = acc[h] + nn(vaug[h, :, ks], ps[h])
             return inner
 
-        lax.fori_loop(0, count, sum_step, 0)
+        lax.fori_loop(0, pairs, functools.partial(sum_step, span), 0)
+        lax.fori_loop(pairs, pairs + odd, functools.partial(sum_step, block), 0)
         for h in range(heads):
             total = acc[h, HEAD : HEAD + 1, :]
             ot_ref[h * HEAD : (h + 1) * HEAD, qs] = (acc[h, :HEAD, :] / total).astype(bf16)
@@ -458,11 +455,12 @@
         in_specs=[SM, VM, VM],
         out_specs=(VM, VM),
         scratch_shapes=[
-            pltpu.VMEM((heads, length + block, 2 * HEAD), bf16),
+            pltpu.VMEM((heads, length, 2 * HEAD), bf16),
             pltpu.VMEM((heads, 2 * HEAD, length), bf16),
-            pltpu.VMEM((heads, HEAD + 16, length + block), bf16),
+            pltpu.VMEM((heads, HEAD + 16, length), bf16),
             pltpu.VMEM((heads, HEAD + 16, block), f32),
             pltpu.VMEM((heads, 8, block), f32),
+            pltpu.VMEM((heads, length, block), f32),
         ],
         compiler_params=pltpu.CompilerParams(vmem_limit_bytes=VMEM_LIMIT),
         cost_estimate=pl.CostEstimate(flops=4 * 10**9, bytes_accessed=6 * 10**6, transcendentals=10**7),
@@ -483,8 +481,6 @@
     vcols = jnp.where(lane < 3, -1.0, 0.0).astype(bf16)
     qrows = query_rows(starts, ends, length)
     zero = jnp.zeros((HEAD - 16, length), bf16)
-    pad = jnp.zeros((2 * HEAD, block), bf16)
-    flat = jnp.zeros((block, HEAD), bf16)
     span = 2 * block
     for h in range(heads):
         hs = slice(h * HEAD, (h + 1) * HEAD)
@@ -492,23 +488,19 @@
         kaug[h, :, HEAD:] = kcols
         vaug[h, :, :HEAD] = qkv_ref[:, 2 * width + h * HEAD : 2 * width + (h + 1) * HEAD]
         vaug[h, :, HEAD:] = vcols
-        qaug[h, :HEAD, :length] = qkvt_ref[hs, :] * 0.125
-        qaug[h, HEAD : HEAD + 16, :length] = put_rows(qrows, split_three(lse_ref[h : h + 1, :]), n_seq).astype(bf16)
-        qaug[h, HEAD + 16 :, :length] = zero
-        qaug[h, :, length:] = pad
-        doaug[h, :, length:] = pad
-        don[h, length:, :] = flat
-        qn[h, length:, :] = flat
+        qaug[h, :HEAD, :] = qkvt_ref[hs, :] * 0.125
+        qaug[h, HEAD : HEAD + 16, :] = put_rows(qrows, split_three(lse_ref[h : h + 1, :]), n_seq).astype(bf16)
+        qaug[h, HEAD + 16 :, :] = zero
         do = dot_ref[hs, :]
         delta = jnp.sum(do.astype(f32) * ot_ref[hs, :].astype(f32), axis=0, keepdims=True)
-        doaug[h, :HEAD, :length] = do
-        doaug[h, HEAD : HEAD + 16, :length] = put_rows(
+        doaug[h, :HEAD, :] = do
+        doaug[h, HEAD : HEAD + 16, :] = put_rows(
             jnp.zeros((16, length), f32), split_three(delta), 0
         ).astype(bf16)
-        doaug[h, HEAD + 16 :, :length] = zero
-        qn[h, :length, :] = qkv_ref[:, hs] * 0.125
-        don[h, :length, :] = do.T
-        dqt[h] = jnp.zeros((HEAD, length + block), f32)
+        doaug[h, HEAD + 16 :, :] = zero
+        qn[h] = qkv_ref[:, hs] * 0.125
+        don[h] = do.T
+        dqt[h] = jnp.zeros((HEAD, length), f32)
 
     def k_step(kb, carry):
         ks = pl.ds(pl.multiple_of(kb * block, block), block)
@@ -516,8 +508,8 @@
         dk[...] = jnp.zeros_like(dk)
         dv[...] = jnp.zeros_like(dv)
 
-        def q_step(i, inner):
-            qs = pl.ds(pl.multiple_of((lo + 2 * i) * block, block), span)
+        def q_step(size, i, inner):
+            qs = pl.ds(pl.multiple_of((lo + 2 * i) * block, block), size)
             for h in range(heads):
                 p = jnp.exp(nn(kaug[h, ks, :], qaug[h, :, qs]))
                 ds = (p * nn(vaug[h, ks, :], doaug[h, :, qs])).astype(bf16)
@@ -527,7 +519,9 @@
                 dqt[h, :, qs] = dqt[h, :, qs] + nn(kt, ds)
             return inner
 
-        lax.fori_loop(0, lax.div(hi - lo + 1, 2), q_step, 0)
+        pairs, odd = lax.div(hi - lo, 2), lax.rem(hi - lo, 2)
+        lax.fori_loop(0, pairs, functools.partial(q_step, span), 0)
+        lax.fori_loop(pairs, pairs + odd, functools.partial(q_step, block), 0)
         for h in range(heads):
             vk = dk[h].astype(bf16)
             vv = dv[h].astype(bf16)
@@ -540,7 +534,7 @@
 
     lax.fori_loop(0, length // block, k_step, 0)
     for h in range(heads):
-        v = (dqt[h, :, :length] * 0.125).astype(bf16)
+        v = (dqt[h] * 0.125).astype(bf16)
         dqkvt_ref[h * HEAD : (h + 1) * HEAD, :] = v
         dqkv_ref[:, h * HEAD : (h + 1) * HEAD] = v.T
 
@@ -550,7 +544,7 @@
     heads = cols // (3 * HEAD)
     block = 256
     nat = pltpu.VMEM((heads, length, 2 * HEAD), bf16)
-    tra = pltpu.VMEM((heads, 2 * HEAD, length + block), bf16)
+    tra = pltpu.VMEM((heads, 2 * HEAD, length), bf16)
     return pl.pallas_call(
         functools.partial(attend_back_kernel, n_seq, block),
         out_shape=(sds((length, cols), bf16), sds((cols, length), bf16)),
@@ -558,9 +552,9 @@
         out_specs=(VM, VM),
         scratch_shapes=[
             nat, tra, nat, tra,
-            pltpu.VMEM((heads, length + block, HEAD), bf16),
-            pltpu.VMEM((heads, length + block, HEAD), bf16),
-            pltpu.VMEM((heads, HEAD, length + block), f32),
+            pltpu.VMEM((heads, length, HEAD), bf16),
+            pltpu.VMEM((heads, length, HEAD), bf16),
+            pltpu.VMEM((heads, HEAD, length), f32),
             pltpu.VMEM((heads, block, HEAD), f32),
             pltpu.VMEM((heads, block, HEAD), f32),
         ],
@@ -589,7 +583,7 @@
 
 def middle_body(
     n_dp, oin_ref, xf_any, dys_ref, w_ref, back_ref, dh1_ref, dout_ref, a_refs, b_refs,
-    xv, xsem, fin, s_a, r_a, dyin, dyb, ot_ref, dot_ref, wup, wdn, wo, vec, ub, hid, slope, gbuf, gin, facc, yacc,
+    xv, xsem, fin, s_a, r_a, dyin, dyb, ot_ref, dot_ref, wup, wdn, wo, vec, ub, hid, slope, dub, sums, gbuf, gin, facc, yacc,
     so, ro, sg, rg, lsem, wss, wrs, sgb, rgb, sgt, rgt, gsem, sd, rd, sm, rm,
 ):
     d, r, c = me()
@@ -653,11 +647,6 @@
 
     for cp in o_cp:
         cp.wait_recv()
-    for cp in d_cp:
-        cp.wait_recv()
-    theirs = pl.ds(pl.multiple_of((1 - c) * tok, tok), tok)
-    dy_cp = remote(dyin.at[theirs, :], dyb, sm, rm, core)
-    dy_cp.start()
     x_cp.wait()
     x = jnp.concatenate([xv[0], xv[1]], axis=1).astype(f32)
     settle(0)
@@ -669,6 +658,11 @@
     r1 = lax.rsqrt(jnp.mean(h1 * h1, axis=1, keepdims=True) - mu * mu + EPS)
     n1 = (h1 - mu) * r1
     y1 = (n1 * g1 + s1).astype(bf16)
+    for cp in d_cp:
+        cp.wait_recv()
+    theirs = pl.ds(pl.multiple_of((1 - c) * tok, tok), tok)
+    dy_cp = remote(dyin.at[theirs, :], dyb, sm, rm, core)
+    dy_cp.start()
     settle(1)
     settle(2)
     facc[...] = jnp.zeros_like(facc)
@@ -704,26 +698,13 @@
     df = dh2.astype(bf16)
     dbg = jnp.sum(df.astype(f32), axis=0, keepdims=True)
     yacc[...] = dh2
-    y1t = y1.T
-
     def big_cp(j):
         return remote(gbuf.at[j, 1 - c, 0:OUT], gin.at[j, 0:OUT], sgb.at[j], rgb.at[j], core)
 
     def back(j, carry):
         du = (nt(df, wdn[j]) * slope[j]).astype(bf16)
-        ubg = jnp.sum(du.astype(f32), axis=0, keepdims=True)
-        gd = tn(hid[j], df).astype(bf16)
-        gu = nn(y1t, du).astype(bf16)
-        for cc in range(2):
-            cs = slice(cc * wide, (cc + 1) * wide)
-            for h in range(2):
-                gbuf[j, cc, h * wide : (h + 1) * wide, :] = gu[cs, h * wide : (h + 1) * wide]
-            gbuf[j, cc, DOWN:OUT, :] = gd[:, cs]
-        for cc in range(2):
-            gbuf[j, cc, VEC : VEC + 16, :] = jnp.concatenate(
-                [jnp.broadcast_to(ubg[:, :wide], (8, wide)), jnp.broadcast_to(ubg[:, wide:], (8, wide))], axis=0
-            ).astype(bf16)
-        big_cp(j).start()
+        dub[j] = du
+        sums[j] = jnp.broadcast_to(jnp.sum(du.astype(f32), axis=0, keepdims=True), (8, width))
         yacc[...] += nt(du, wup[j])
         return carry
 
@@ -743,6 +724,20 @@
         cp.start()
         g_cp.append(cp)
     dout_ref[:, myq] = dot_ref[shard]
+    y1t = y1.T
+
+    def grads(j, carry):
+        gd = tn(hid[j], df).astype(bf16)
+        gu = nn(y1t, dub[j]).astype(bf16)
+        for cc in range(2):
+            cs = slice(cc * wide, (cc + 1) * wide)
+            for h in range(2):
+                gbuf[j, cc, h * wide : (h + 1) * wide, :] = gu[cs, h * wide : (h + 1) * wide]
+            gbuf[j, cc, DOWN:OUT, :] = gd[:, cs]
+        big_cp(j).start()
+        return carry
+
+    lax.fori_loop(0, 4, grads, 0)
     go = nn(ot_ref[...].reshape(width, tok), da).astype(bf16)
     pad = gbuf.shape[2] - VEC
     row = lax.broadcasted_iota(jnp.int32, (pad, wide), 0)
@@ -754,8 +749,8 @@
             tail = jnp.zeros((pad, wide), f32)
             for i, v in enumerate((obg, g1g, s1g, dbg, g2g, s2g)):
                 tail = jnp.where(row == i, v[:, cs], tail)
-            tail = jnp.where(row == 6, gbuf[j, cc, VEC : VEC + 16, :][0:1].astype(f32), tail)
-            tail = jnp.where(row == 7, gbuf[j, cc, VEC : VEC + 16, :][8:9].astype(f32), tail)
+            tail = jnp.where(row == 6, sums[j, 0:1, :wide], tail)
+            tail = jnp.where(row == 7, sums[j, 0:1, wide:], tail)
             gbuf[j, cc, VEC:, :] = tail.astype(bf16)
         cp = remote(gbuf.at[j, 1 - c, OUT:], gin.at[j, OUT:], sgt.at[j], rgt.at[j], core)
         cp.start()
@@ -818,6 +813,8 @@
             pltpu.VMEM((4, 2, 16, wide), bf16),
             pltpu.VMEM((4, tok, width), bf16),
             pltpu.VMEM((4, tok, width), f32),
+            pltpu.VMEM((4, tok, width), bf16),
+            pltpu.VMEM((4, 8, width), f32),
             pltpu.VMEM((4, 2, g_rows, wide), bf16),
             pltpu.VMEM((4, g_rows, wide), bf16),
             pltpu.VMEM((tok, width), f32),
@@ -882,25 +879,33 @@
 
     for cp in loads[1:-2]:
         cp.wait()
-    total = apart[0].astype(f32)
-    for k in range(1, n_in):
-        total = total + apart[k].astype(f32)
-    asum[...] = total.astype(bf16)
-    total = bpart[0].astype(f32)
-    for k in range(1, n_out):
-        total = total + bpart[k].astype(f32)
-    bsum[...] = total.astype(bf16)
+    n_ch = s_r.shape[1]
+    chunk = rsum.shape[1] // n_ch
     a_cp, b_cp = [], []
-    for k in range(1, n_out):
-        dest = lax.rem(o + k, n_out)
-        cp = remote(asum.at[dest], ain.at[k], s_1.at[k], r_1.at[k], (dest * n_in + i, r, c))
-        cp.start()
-        a_cp.append(cp)
-    for k in range(1, n_in):
-        dest = lax.rem(i + k, n_in)
-        cp = remote(bsum.at[dest], bin_.at[k], s_2.at[k], r_2.at[k], (o * n_in + dest, r, c))
-        cp.start()
-        b_cp.append(cp)
+    for t in range(n_ch):
+        ts = slice(t * chunk, (t + 1) * chunk)
+        total = apart[0, :, :, ts].astype(f32)
+        for k in range(1, n_in):
+            total = total + apart[k, :, :, ts].astype(f32)
+        asum[:, :, ts] = total.astype(bf16)
+        total = bpart[0, :, :, ts].astype(f32)
+        for k in range(1, n_out):
+            total = total + bpart[k, :, :, ts].astype(f32)
+        bsum[:, :, ts] = total.astype(bf16)
+        for k in range(1, n_out):
+            dest = lax.rem(o + k, n_out)
+            cp = remote(
+                asum.at[dest, :, ts], ain.at[k, :, ts], s_1.at[k, t], r_1.at[k, t], (dest * n_in + i, r, c)
+            )
+            cp.start()
+            a_cp.append(cp)
+        for k in range(1, n_in):
+            dest = lax.rem(i + k, n_in)
+            cp = remote(
+                bsum.at[dest, :, ts], bin_.at[k, :, ts], s_2.at[k, t], r_2.at[k, t], (o * n_in + dest, r, c)
+            )
+            cp.start()
+            b_cp.append(cp)
 
     far = part(1 - half, c)
     cp_far.wait_recv()
@@ -908,11 +913,33 @@
     cp_z = remote(toz, fromz, s_z, r_z, zdev)
     cp_z.start()
 
+    row_cp = []
+
+    def to_rows(t):
+        ts = slice(t * chunk, (t + 1) * chunk)
+        total = asum[o, :, ts].astype(f32)
+        for k in range(1, n_out):
+            a_cp[t * (n_out - 1) + k - 1].wait_recv()
+            total = total + ain[k, :, ts].astype(f32)
+        rsum[0:2, ts] = total.astype(bf16)
+        total = bsum[i, :, ts].astype(f32)
+        for k in range(1, n_in):
+            b_cp[t * (n_in - 1) + k - 1].wait_recv()
+            total = total + bin_[k, :, ts].astype(f32)
+        rsum[2:4, ts] = total.astype(bf16)
+        for k, dev in enumerate(rows_dev):
+            cp = remote(rsum.at[dev[1], ts], zin.at[k, ts], s_r.at[k, t], r_r.at[k, t], dev)
+            cp.start()
+            row_cp.append(cp)
+
+    to_rows(0)
+
     n_cols, length = dqkvt_ref.shape
     loads[-1].wait()
     for f in range(2):
         g = nn(dqkvt_ref[:, : length // 2], xf[0, f]) + nn(dqkvt_ref[:, length // 2 :], xf[1, f])
         gq_ref[f, :n_cols, :] = g.astype(bf16)
+        to_rows(1 + f)
     third = n_cols // 3
     sums = jnp.sum(dqkv_ref[...].astype(f32), axis=0, keepdims=True)
     bias = jnp.concatenate([sums[:, :third], sums[:, 2 * third :]], axis=1)
@@ -937,23 +964,8 @@
     cp_near = remote(tocore.at[1], fromcore.at[1], s_c.at[1], r_c.at[1], core)
     cp_near.start()
 
-    total = asum[o].astype(f32)
-    for cp in a_cp:
-        cp.wait_recv()
-    for k in range(1, n_out):
-        total = total + ain[k].astype(f32)
-    rsum[0:2] = total.astype(bf16)
-    total = bsum[i].astype(f32)
-    for cp in b_cp:
-        cp.wait_recv()
-    for k in range(1, n_in):
-        total = total + bin_[k].astype(f32)
-    rsum[2:4] = total.astype(bf16)
-    row_cp = []
-    for k, dev in enumerate(rows_dev):
-        cp = remote(rsum.at[dev[1]], zin.at[k], s_r.at[k], r_r.at[k], dev)
-        cp.start()
-        row_cp.append(cp)
+    for t in range(3, n_ch):
+        to_rows(t)
 
     loads[-2].wait()
     total = part(half, c) + dh1[...]
@@ -984,20 +996,22 @@
     fin[1] = total[:, wide:]
     send_back(n_dp, fin, back_ref, s_b, r_b)
 
-    held = rsum[r].astype(f32)
-    for k in range(3):
-        row_cp[k].wait_recv()
-        held = held + zin[k].astype(f32)
-    rfin[...] = held.astype(bf16)
     n_keep = rfin.shape[0]
-    keep = pl.ds(pl.multiple_of(d * n_keep, n_keep), n_keep)
-    gall_ref[keep, :] = rfin[...]
     t_cp = []
-    for k in range(1, n_dp):
-        dest = lax.rem(d + k, n_dp)
-        cp = remote(rfin, gall_ref.at[keep, :], s_t.at[k], r_t.at[k], (dest, r, c))
-        cp.start()
-        t_cp.append(cp)
+    for t in range(n_ch):
+        ts = slice(t * chunk, (t + 1) * chunk)
+        held = rsum[r, ts].astype(f32)
+        for k in range(3):
+            row_cp[t * 3 + k].wait_recv()
+            held = held + zin[k, ts].astype(f32)
+        rfin[ts] = held.astype(bf16)
+        keep = pl.ds(pl.multiple_of(d * n_keep + t * chunk, chunk), chunk)
+        gall_ref[keep, :] = rfin[ts]
+        for k in range(1, n_dp):
+            dest = lax.rem(d + k, n_dp)
+            cp = remote(rfin.at[ts], gall_ref.at[keep, :], s_t.at[k, t], r_t.at[k, t], (dest, r, c))
+            cp.start()
+            t_cp.append(cp)
 
     far_0.wait_recv()
 
@@ -1056,8 +1070,8 @@
             vm(2, tok, wide), vm(2, tok, width), vm(2, tok, width), vm(tok, width), vm(tok, width),
             vm(2, gq_rows, wide), vm(n_dp, 2, gq_rows // n_dp, wide), vm(2, gq_rows // n_dp, wide),
             vm(2, gq_rows // n_dp, wide), vm(gq_rows // n_dp, wide),
-            DMA((n_out,)), DMA((n_out,)), DMA((n_in,)), DMA((n_in,)),
-            DMA((3,)), DMA((3,)), DMA((n_dp,)), DMA((n_dp,)),
+            DMA((n_out, 4)), DMA((n_out, 4)), DMA((n_in, 4)), DMA((n_in, 4)),
+            DMA((3, 4)), DMA((3, 4)), DMA((n_dp, 4)), DMA((n_dp, 4)),
             DMA((n_dp // 2, 2)), DMA((n_dp,)),
             DMA((2,)), DMA((2,)), DMA, DMA,
             DMA((n_dp,)), DMA((n_dp,)), DMA((2,)), DMA((2,)), DMA((n_dp,)), DMA((n_dp,)),

time: 292 us -> 263 us (0.901)
  Pallas kernels: 285 us -> 250 us
  waiting for transfers between devices: 0.01 us -> 3.89 us
    pallas_call x1, Pallas kernels: 33.5 us -> 16.1 us  [attend_call(): pl.pallas_call(functools.partial(attend_kernel, n_seq, block), out_shape=...]
    pallas_call x1, Pallas kernels: 81.8 us -> 74.6 us  [return_call(): pl.pallas_call(functools.partial(return_kernel, n_dp), out_shape=(sds((to...]
    pallas_call x1, Pallas kernels: 33.5 us -> 26.8 us  [attend_back_call(): pl.pallas_call(functools.partial(attend_back_kernel, n_seq, block), out_s...]
    ppermute x1, waiting for transfers between devices: 0.01 us -> 3.46 us  [on_device(): lax.ppermute(a_parts[k], 'dp', [(o * n_in + i, o * n_in + (i + k) % n_in)...]
    pallas_call x1, Pallas kernels: 52.5 us -> 49.1 us  [middle_call(): pl.pallas_call(functools.partial(middle_kernel, n_dp), out_shape=(sds((2...]
  transfers between devices with their start and end apart: 2 -> 2, of which waited for: 0 -> 2; matrix products, arithmetic and copies ran while one was open for 0% -> 0% of each run, Pallas kernels for 12% -> 10%
where the time goes in v4:
time: 263 us; the launch traced here: 258 us
  Pallas kernels  250 us (95%)
  waiting for transfers between devices  3.89 us (1%)
    pallas_call x1, Pallas kernels, deal_call(): pl.pallas_call(functools.partial(deal_kernel, n_dp, rows_w), out_shape=(s...  77.4 us
    pallas_call x1, Pallas kernels, return_call(): pl.pallas_call(functools.partial(return_kernel, n_dp), out_shape=(sds((to...  74.6 us
    pallas_call x1, Pallas kernels, middle_call(): pl.pallas_call(functools.partial(middle_kernel, n_dp), out_shape=(sds((2...  49.1 us
    pallas_call x1, Pallas kernels, attend_back_call(): pl.pallas_call(functools.partial(attend_back_kernel, n_seq, block), out_s...  26.8 us
    pallas_call x1, Pallas kernels, attend_call(): pl.pallas_call(functools.partial(attend_kernel, n_seq, block), out_shape=...  16.1 us
    pallas_call x1, Pallas kernels, finish_call(): pl.pallas_call(finish_kernel, out_shape=(tok, tok, head, row, head, head,...  6.54 us
  transfers between devices with their start and end apart: 2, of which 2 were waited for; matrix products, arithmetic and copies ran while one was open for 0% of the time, Pallas kernels for 10%

profile of v4, /device:TPU:30, one launch (start us, length us, event | category | flops | bytes accessed | tf_op | source)
XLA Modules:
  0.0 258.3 jit_solution(10834686523140305943)
XLA Ops:
  0.7 77.4 %deal.1 = (bf16[2,2,1024,384]{3,2,1,0:T(8,128)(2,1)}, bf16[4,256,384]{2,1,0:T(8,128)(2,1)}, bf16[2048,576]{1,0:T(8,128)(2,1)}, bf16[576,2048]{1,0:T(8,128)(2,1)}...) custom-call(bf16[1024,384]{1,0:T(8,128)(2,1)} %x_ref.1, bf16[1024,384]{1,0:T(8,128)(2,1)} %dy_ref.1, ...), custom_call_target="tpu_custom_call" | custom-call | tf_op jit(solution)/shard_map/deal/pallas_call | solution.py:292
  78.1 16.1 %attend.1 = (bf16[192,2048]{1,0:T(8,128)(2,1)}, f32[8,2048]{1,0:T(8,128)}) custom-call(s32[8,128]{1,0:T(8,128)} %get-tuple-element.55.seq_ref, bf16[2048,576]{1,0:T(8,128)(2,1)} %get-tuple-element.56.qkv_ref, bf16[576,2048]{1,0:T(8,128)(2,1)} %get-tuple-element.57.qkvt_ref), custom_call_target="tpu_custom_call" | custom-call | flops 4000000000 | bytes 6000000 | tf_op jit(solution)/shard_map/attend/pallas_call | solution.py:452
  94.1 49.1 %middle.1 = (bf16[1024,384]{1,0:T(8,128)(2,1)}, f32[512,768]{1,0:T(8,128)}, bf16[192,2048]{1,0:T(8,128)(2,1)}, bf16[2,2,448,384]{3,2,1,0:T(8,128)(2,1)}, bf16[2,...) custom-call(bf16[192,2048]{1,0:T(8,128)(2,1)} %get-tuple-element.58.oin_ref.ot_ref, ...), custom_call_target="tpu_custom_call" | custom-call | flops 16000000000 | bytes 30000000 | tf_op jit(solution)/shard_map/middle/pallas_call | solution.py:789
  143.2 0.7 collective-permute-start
  143.9 1.8 collective-permute-start.1
  145.7 26.8 %attend_back.1 = (bf16[2048,576]{1,0:T(8,128)(2,1)}, bf16[576,2048]{1,0:T(8,128)(2,1)}) custom-call(s32[8,128]{1,0:T(8,128)} %get-tuple-element.55.seq_ref, bf16[2048,576]{1,0:T(8,128)(2,1)} %get-tuple-element.56.qkv_ref, bf16[576,2048]{1,0:T(8,128)(2,1)} %get-tuple-element.57.qkvt_ref, bf16[192,2048]{1,0:T(8,128)(2,1)} %get-tuple-element.63.dot_ref, ...), custom_call_target="tpu_custom_call" | custom-call | flops 10000000000 | bytes 12000000 | tf_op jit(solution)/shard_map/attend_back/pallas_call | solution.py:548
  172.5 3.5 %collective-permute-done.rest_1_ = bf16[2,2,448,384]{3,2,1,0:T(8,128)(2,1)S(1)} collective-permute-done((bf16[2,2,448,384]{3,2,1,0:T(8,128)(2,1)}, bf16[2,2,448,384]{3,2,1,0:T(8,128)(2,1)S(1)}, u32[]{:S(2)}, u32[]{:S(2)}) %collective-permute-start) | collective-permute-done | bytes 1376288 | tf_op jit(solution)/shard_map/ppermute | solution.py:1159
  176.0 0.0 copy-start
  176.0 0.4 collective-permute-done.1.rest_3_
  176.4 0.6 copy-done
  177.1 74.6 %return.1 = (bf16[1024,384]{1,0:T(8,128)(2,1)}, bf16[640,384]{1,0:T(8,128)(2,1)}, bf16[1792,384]{1,0:T(8,128)(2,1)}) custom-call(bf16[2048,576]{1,0:T(8,128)(2,1)} %get-tuple-element.65.dqkv_ref, bf16[576,2048]{1,0:T(8,128)(2,1)} %get-tuple-element.66.dqkvt_ref, bf16[2,576,384]{2,1,0:T(8,128)(2,1)} %get-tuple-element.67.wq_any, ...), custom_call_target="tpu_custom_call" | custom-call | tf_op jit(solution)/shard_map/return/pallas_call | solution.py:1060
  251.6 6.5 %finish.1 = (bf16[1024,384]{1,0:T(8,128)(2,1)}, bf16[1024,384]{1,0:T(8,128)(2,1)}, f32[192,384]{1,0:T(8,128)}, f32[192]{0:T(256)}, f32[192,384]{1,0:T(8,128)}, /...) custom-call(bf16[1024,384]{1,0:T(8,128)(2,1)} %get-tuple-element.62., ...), custom_call_target="tpu_custom_call" | custom-call | tf_op jit(solution)/shard_map/finish/pallas_call | solution.py:1119
Async XLA Ops:
  143.2 32.7 %collective-permute-start = (bf16[2,2,448,384]{3,2,1,0:T(8,128)(2,1)}, bf16[2,2,448,384]{3,2,1,0:T(8,128)(2,1)S(1)}, u32[]{:S(2)}, u32[]{:S(2)}) collective-permute-start(bf16[2,2,448,384]{3,2,1,0:T(8,128)(2,1)} %get-tuple-element.70), channel_id=1, source_target_pairs={{0,8},{8,0},{16,24},{24,16},{1,9},{9,1},{17,25},{25,17},{2,10},{10... | collective-permute-start | bytes 4128776 | tf_op jit(solution)/shard_map/ppermute | solution.py:1159
  143.9 32.5 %collective-permute-start.1 = (bf16[2,2,448,384]{3,2,1,0:T(8,128)(2,1)}, bf16[2,2,448,384]{3,2,1,0:T(8,128)(2,1)}, u32[]{:S(2)}, u32[]{:S(2)}) collective-permute-start(bf16[2,2,448,384]{3,2,1,0:T(8,128)(2,1)} %get-tuple-element.72), channel_id=1, source_target_pairs={{0,16},{8,24},{16,0},{24,8},{1,17},{9,25},{17,1},{25,9},{2,18},{10... | collective-permute-start | bytes 4128776 | tf_op jit(solution)/shard_map/ppermute | solution.py:1163
  176.0 1.1 copy-start
